TPU v7x, 256 devices: a whole 4x4x8 slice. The times are simulated.
256 devices in a mesh: ens: 8 (over z), polar: 2 (over core), azimuth: 16 (over y, x).
Axes of the slice: x: 4, y: 4, z: 8, core: 2. Of those that a mesh axis runs over, the one named last changes fastest.
Arguments:
- fields: bfloat16 [8, 16, 1440, 256], P('ens', 'polar', 'azimuth'), may hold values from -6 to 6
- basis_spectra: bfloat16 [9, 8, 5, 720], P(None, 'polar'), may hold values from -3 to 3
- support: int32 [8, 2], P('polar'), may hold values from 0 to 4, as said below
- weights: bfloat16 [9, 256, 256], replicated, may hold values from -0.125 to 0.125
- out_grad: bfloat16 [8, 8, 720, 256], P('ens', 'polar', 'azimuth'), may hold values from -6 to 6
Outputs:
- conv_out: bfloat16 [8, 8, 720, 256], P('ens', 'polar', 'azimuth')
- field_grad: bfloat16 [8, 16, 1440, 256], P('ens', 'polar', 'azimuth')
- weight_grad: float32 [9, 256, 256], P(None, 'azimuth')
Inputs may be any that keep to these rules, and one draw needn't show every extreme that they name: Row o uses window rows support[o, 0] to support[o, 1]; support[o, 0] <= 2 <= support[o, 1]; rows o with o mod 4 equal to 0 or 3 use the whole window.
All inputs are finite; a program needn't handle non-finite values.
Results may differ from a plain program's by a relative error of at most 0.02.
Values may be sent and summed in bfloat16 or wider, within the bound.
No kernel may reach another device: no remote copies, remote signals or barrier semaphores. Data moves between devices by JAX's collectives and lax.ppermute only.
A program may use at most 64 MiB of HBM per device.

v0:
```python
import math

import jax
import jax.numpy as jnp
import numpy as np
from jax import lax
from jax.experimental import pallas as pl
from jax.experimental.pallas import tpu as pltpu
from jax.sharding import PartitionSpec as P

WIN, WOUT, MODES = 1440, 720, 360
K, C, SUPPORT = 9, 256, 5
HOUT, HIN = 8, 16
LANES, BANDS = 16, 2
SHARES = LANES * BANDS
M12, M16 = 12, 16
WPART, WROWS = 90, 96
VPART, VROWS = 45, 24
CHUNK_IN = WROWS + VROWS
CHUNK_MID = M16 + 2 * M12
F32, BF16 = jnp.float32, jnp.bfloat16
JOINT = ("polar", "azimuth")


def factor_tables():
    share = np.arange(SHARES)[:, None, None]
    col = np.arange(SHARES * 2 * M12).reshape(SHARES, 2, M12)
    mode = (12 * share + np.arange(M12)[None, None, :] + 0 * col).reshape(-1)
    imag = (np.arange(2)[None, :, None] + 0 * col).reshape(-1) == 1
    keep = mode < MODES
    alpha = 2 * math.pi * ((mode[None, :] * (WPART * np.arange(LANES)[:, None])) % WIN) / WIN
    beta = 2 * math.pi * ((mode[None, :] * np.arange(WROWS)[:, None]) % WIN) / WIN
    keep_w = keep[None, :] & (np.arange(WROWS)[:, None] < WPART)
    u1 = np.where(imag[None, :], -np.sin(alpha), np.cos(alpha))
    u2 = np.where(imag[None, :], -np.cos(alpha), -np.sin(alpha))
    f1 = np.where(keep_w, np.cos(beta), 0.0)
    f2 = np.where(keep_w, np.sin(beta), 0.0)
    wide = [a.astype(np.float32) for a in (u1, u2, f1, f2)]

    slot = np.arange(SHARES * M16)
    mode = 12 * (slot // M16) + slot % M16
    keep = (slot % M16 < M12) & (mode < MODES)
    scale = np.where(mode == 0, 1.0, 2.0) / WIN
    alpha = 2 * math.pi * ((mode[None, :] * (VPART * np.arange(LANES)[:, None])) % WOUT) / WOUT
    ca, sa = np.cos(alpha), np.sin(alpha)
    fs = []
    for part in range(2):
        v = VROWS * part + np.arange(VROWS)
        beta = 2 * math.pi * ((mode[None, :] * v[:, None]) % WOUT) / WOUT
        ok = keep[None, :] & (v[:, None] < VPART)
        fs.append(np.where(ok, scale * np.cos(beta), 0.0))
        fs.append(np.where(ok, scale * np.sin(beta), 0.0))
    narrow = [a.astype(np.float32) for a in (ca, sa, *fs)]
    return wide, narrow


def whole(shape):
    return pl.BlockSpec(shape, lambda *_: (0,) * len(shape))


def call(body, outs, name, flops=0, scratch=(), nbytes=1 << 20):
    def run(*args):
        return pl.pallas_call(
            body,
            out_shape=[jax.ShapeDtypeStruct(s, d) for s, d in outs],
            in_specs=[pl.BlockSpec(memory_space=pltpu.VMEM)] * len(args),
            out_specs=[pl.BlockSpec(memory_space=pltpu.VMEM)] * len(outs),
            scratch_shapes=list(scratch),
            name=name,
            cost_estimate=pl.CostEstimate(flops=flops, bytes_accessed=nbytes, transcendentals=0),
        )(*args)

    return run


def low_half(shape):
    return lax.broadcasted_iota(jnp.int32, shape, len(shape) - 1) < 64


def swap64(value):
    return pltpu.roll(value, 64, value.ndim - 1)


def dot(a, b):
    return jnp.dot(a, b, preferred_element_type=F32)


def pack_body(f_ref, g_ref, o_ref, pad_ref):
    for r in range(HIN // BANDS):
        for h in range(2):
            o_ref[2 * r + h, 0:WPART, :] = f_ref[r, :, 128 * h : 128 * h + 128]
            o_ref[2 * r + h, WPART:WROWS, :] = jnp.zeros((WROWS - WPART, 128), BF16)
    keep = low_half((VROWS, 128))
    for o in range(HOUT // BANDS):
        pad_ref[40:48, :] = jnp.zeros((8, C), F32)
        pad_ref[0:VPART, :] = g_ref[o].astype(F32)
        for i in range(2):
            top = pad_ref[0:24, 128 * i : 128 * i + 128]
            bottom = pad_ref[24:48, 128 * i : 128 * i + 128]
            even = jnp.where(keep, top, swap64(bottom))
            odd = jnp.where(keep, swap64(top), bottom)
            o_ref[4 * o + 2 * i, WROWS:CHUNK_IN, :] = even.astype(BF16)
            o_ref[4 * o + 2 * i + 1, WROWS:CHUNK_IN, :] = odd.astype(BF16)


def wide_table_body(u1, u2, f1, f2, tt_ref, t_ref):
    for b in range(LANES):
        block = u1[b : b + 1, :] * f1[...] + u2[b : b + 1, :] * f2[...]
        tt_ref[WROWS * b : WROWS * (b + 1), :] = block.astype(BF16)
    for i in range(12):
        for j in range(6):
            piece = tt_ref[128 * i : 128 * (i + 1), 128 * j : 128 * (j + 1)]
            t_ref[128 * j : 128 * (j + 1), 128 * i : 128 * (i + 1)] = piece.astype(F32).T.astype(BF16)


def narrow_table_body(ca, sa, f0c, f0s, f1c, f1s, v_ref, vt_ref):
    for part, (fc, fs) in enumerate(((f0c, f0s), (f1c, f1s))):
        for b in range(LANES):
            c, s = ca[b : b + 1, :], sa[b : b + 1, :]
            rows = slice(VROWS * b, VROWS * (b + 1))
            v_ref[2 * part, rows, :] = (c * fc[...] - s * fs[...]).astype(BF16)
            v_ref[2 * part + 1, rows, :] = (-(s * fc[...]) - c * fs[...]).astype(BF16)
    for n in range(4):
        for i in range(3):
            for j in range(4):
                piece = v_ref[n, 128 * i : 128 * (i + 1), 128 * j : 128 * (j + 1)]
                vt_ref[n, 128 * j : 128 * (j + 1), 128 * i : 128 * (i + 1)] = piece.astype(F32).T.astype(BF16)


def spectra_body(r_ref, t_ref, vt_ref, o_ref):
    x = r_ref[:, 0:WROWS, :].reshape(LANES * WROWS, 128)
    o_ref[:, M16:CHUNK_MID, :] = dot(t_ref[...], x).astype(BF16).reshape(SHARES, 2 * M12, 128)
    g = r_ref[:, WROWS:CHUNK_IN, :].reshape(LANES * VROWS, 128)
    re = dot(vt_ref[0], g) + swap64(dot(vt_ref[2], g))
    im = swap64(dot(vt_ref[1], g)) + dot(vt_ref[3], g)
    both = jnp.where(low_half(re.shape), re, im)
    o_ref[:, 0:M16, :] = both.astype(BF16).reshape(SHARES, M16, 128)


def mixing_body(b_ref, a_ref, at_ref, p_ref):
    rows, width = K * 16, HIN * 2 * M12
    row = lax.broadcasted_iota(jnp.int32, (120, width), 0)
    lane = lax.broadcasted_iota(jnp.int32, (120, width), 1)
    owner = (lax.broadcasted_iota(jnp.int32, (rows, width), 0) // 2) % HOUT
    total = jnp.zeros((rows, width), F32)
    for o in range(HOUT):
        shift = jnp.where(lane - row == 48 * (o - 1), 1.0, 0.0).astype(BF16)
        total = jnp.where(owner == o, dot(b_ref[...], shift), total)
    p_ref[...] = total
    mode = lax.broadcasted_iota(jnp.int32, (M16, width), 1) % M12
    same = lax.broadcasted_iota(jnp.int32, (M16, width), 0) == mode
    for i in range(rows):
        block = jnp.where(same, jnp.broadcast_to(p_ref[i : i + 1, :], (M16, width)), 0.0)
        a_ref[i // 16, M16 * (i % 16) : M16 * (i % 16 + 1), :] = block.astype(BF16)
    spot = lax.broadcasted_iota(jnp.int32, (16, 256), 1) // M16
    spread = jnp.where(lax.broadcasted_iota(jnp.int32, (16, 256), 0) == spot, 1.0, 0.0).astype(BF16)
    left = lax.broadcasted_iota(jnp.int32, (width, 256), 0) % M12
    right = lax.broadcasted_iota(jnp.int32, (width, 256), 1) % M16
    for k in range(K):
        part = p_ref[16 * k : 16 * (k + 1), :].astype(BF16)
        grown = lax.dot_general(part, spread, (((0,), (0,)), ((), ())), preferred_element_type=F32)
        at_ref[k] = jnp.where(left == right, grown, 0.0).astype(BF16)


def middle_body(band_ref, r_ref, a_ref, at_ref, w_ref, mine_ref, other_ref, o_ref, gs_ref, out_ref, sg_ref):
    keep = low_half((M16, 128))
    for o in range(HOUT):
        for i in range(2):
            first = r_ref[2 * o + i, 0, 0:M16, :].astype(F32)
            second = r_ref[2 * o + i, 1, 0:M16, :].astype(F32)
            cols = slice(128 * i, 128 * (i + 1))
            gs_ref[32 * o : 32 * o + 16, cols] = jnp.where(keep, first, swap64(second)).astype(BF16)
            gs_ref[32 * o + 16 : 32 * o + 32, cols] = jnp.where(keep, swap64(first), second).astype(BF16)
    rows = HIN * 2 * M12
    x = jnp.concatenate(
        [r_ref[:, h, M16:CHUNK_MID, :].reshape(rows, 128) for h in range(2)], axis=1
    )
    gs = gs_ref[...]
    low = band_ref[0, 0] == 0
    for k in range(K):
        mixed = dot(a_ref[k], x).astype(BF16)
        out_now = dot(mixed, w_ref[k])
        grad = lax.dot_general(mixed, gs, (((0,), (0,)), ((), ())), preferred_element_type=F32)
        left, right = grad[:, :128], grad[:, 128:]
        mine_ref[:, k] = jnp.where(low, left, right).astype(BF16).reshape(LANES, 16, 128)
        other_ref[:, k] = jnp.where(low, right, left).astype(BF16).reshape(LANES, 16, 128)
        back = lax.dot_general(gs, w_ref[k], (((1,), (1,)), ((), ())), preferred_element_type=F32)
        sg_now = dot(at_ref[k], back.astype(BF16))
        if k == 0:
            out_ref[...] = out_now
            sg_ref[...] = sg_now
        else:
            out_ref[...] += out_now
            sg_ref[...] += sg_now
    for o in range(HOUT):
        for i in range(2):
            cols = slice(128 * i, 128 * (i + 1))
            re = out_ref[32 * o : 32 * o + 16, cols]
            im = out_ref[32 * o + 16 : 32 * o + 32, cols]
            o_ref[4 * o + 2 * i, 0:M16, :] = jnp.where(keep, re, swap64(im)).astype(BF16)
            o_ref[4 * o + 2 * i + 1, 0:M16, :] = jnp.where(keep, swap64(re), im).astype(BF16)
    for r in range(HIN):
        for h in range(2):
            piece = sg_ref[24 * r : 24 * (r + 1), 128 * h : 128 * (h + 1)]
            o_ref[2 * r + h, M16:CHUNK_MID, :] = piece.astype(BF16)


def fields_body(r_ref, tt_ref, v_ref, o_ref):
    sg = r_ref[:, M16:CHUNK_MID, :].reshape(SHARES * 2 * M12, 128)
    o_ref[:, 0:WROWS, :] = dot(tt_ref[...], sg).astype(BF16).reshape(LANES, WROWS, 128)
    c = r_ref[:, 0:M16, :].reshape(SHARES * M16, 128)
    first = dot(v_ref[0], c) + swap64(dot(v_ref[1], c))
    second = swap64(dot(v_ref[2], c)) + dot(v_ref[3], c)
    both = jnp.where(low_half(first.shape), first, second)
    o_ref[:, WROWS:CHUNK_IN, :] = both.astype(BF16).reshape(LANES, VROWS, 128)


def unpack_body(r_ref, f_ref, c_ref):
    for r in range(HIN // BANDS):
        for h in range(2):
            f_ref[r, :, 128 * h : 128 * h + 128] = r_ref[2 * r + h, 0:WPART, :]
    keep = low_half((VROWS, 128))
    for o in range(HOUT // BANDS):
        for i in range(2):
            even = r_ref[4 * o + 2 * i, WROWS:CHUNK_IN, :].astype(F32)
            odd = r_ref[4 * o + 2 * i + 1, WROWS:CHUNK_IN, :].astype(F32)
            cols = slice(128 * i, 128 * (i + 1))
            c_ref[o, 0:VROWS, cols] = jnp.where(keep, even, swap64(odd)).astype(BF16)
            bottom = jnp.where(keep, swap64(even), odd).astype(BF16)
            c_ref[o, VROWS:VPART, cols] = bottom[0 : VPART - VROWS]


def mask_filters(filters, support):
    window = jnp.arange(filters.shape[2], dtype=jnp.int32)
    inside = (window[None, :] >= support[:, 0:1]) & (window[None, :] <= support[:, 1:2])
    return jnp.where(inside[None, :, :, None], filters, jnp.zeros_like(filters))


def filter_rows(basis_spectra, support):
    masked = mask_filters(basis_spectra, support)
    pairs = masked.reshape(K, HOUT // BANDS, SUPPORT, 2, MODES)
    pairs = jnp.pad(pairs, [(0, 0)] * 4 + [(0, SHARES * M12 - MODES)])
    pairs = pairs.reshape(K, HOUT // BANDS, SUPPORT, 2, BANDS, LANES * M12)
    start = lax.axis_index("azimuth") * M12
    here = lax.dynamic_slice_in_dim(pairs, start, M12, 5)
    here = jnp.moveaxis(here, 4, 0)
    here = lax.all_to_all(here, "polar", split_axis=0, concat_axis=0, tiled=True)
    here = jnp.moveaxis(here, 0, 1).reshape(K, HOUT, SUPPORT, 2, M12)
    re, im = here[:, :, :, 0], here[:, :, :, 1]
    rows = jnp.stack([jnp.stack([re, -im], axis=3), jnp.stack([im, re], axis=3)], axis=2)
    return rows.reshape(K * HOUT * 2, SUPPORT * 2 * M12)


def swap_bands(value):
    return lax.ppermute(value, "polar", [(0, 1), (1, 0)])


def local(fields, basis_spectra, support, weights, out_grad):
    members = lax.axis_size("ens")
    band = lax.axis_index("polar")
    wide, narrow = factor_tables()
    (sent,) = call(
        pack_body, [((LANES, CHUNK_IN, 128), BF16)], "pack", scratch=[pltpu.VMEM((48, C), F32)]
    )(fields[0], out_grad[0])
    landed = lax.all_to_all(sent, "azimuth", split_axis=0, concat_axis=0, tiled=True)

    tall, flat = call(
        wide_table_body, [((1536, 768), BF16), ((768, 1536), BF16)], "wide_table", nbytes=6 << 20
    )(*[jnp.asarray(a) for a in wide])
    inv, inv_t = call(
        narrow_table_body, [((4, 384, 512), BF16), ((4, 512, 384), BF16)], "narrow_table", nbytes=4 << 20
    )(*[jnp.asarray(a) for a in narrow])
    rows = filter_rows(basis_spectra, support)
    mix, mix_t = call(
        mixing_body,
        [((K, 256, 384), BF16), ((K, 384, 256), BF16)],
        "mixing",
        scratch=[pltpu.VMEM((K * 16, 384), F32)],
        nbytes=4 << 20,
    )(rows)

    (sent,) = call(spectra_body, [((SHARES, CHUNK_MID, 128), BF16)], "spectra", flops=600 << 20)(
        landed, flat, inv_t
    )
    landed = lax.all_to_all(sent, JOINT, split_axis=0, concat_axis=0, tiled=True)

    mine, other, sent = pl.pallas_call(
        middle_body,
        out_shape=[
            jax.ShapeDtypeStruct((LANES, K, 16, 128), BF16),
            jax.ShapeDtypeStruct((LANES, K, 16, 128), BF16),
            jax.ShapeDtypeStruct((SHARES, CHUNK_MID, 128), BF16),
        ],
        in_specs=[pl.BlockSpec(memory_space=pltpu.SMEM)] + [pl.BlockSpec(memory_space=pltpu.VMEM)] * 4,
        out_specs=[pl.BlockSpec(memory_space=pltpu.VMEM)] * 3,
        scratch_shapes=[
            pltpu.VMEM((256, 256), BF16),
            pltpu.VMEM((256, 256), F32),
            pltpu.VMEM((384, 256), F32),
        ],
        name="middle",
        cost_estimate=pl.CostEstimate(flops=2 << 30, bytes_accessed=6 << 20, transcendentals=0),
    )(band.astype(jnp.int32).reshape(1, 1), landed.reshape(HIN, 2, CHUNK_MID, 128), mix, mix_t, weights)
    landed = lax.all_to_all(sent, JOINT, split_axis=0, concat_axis=0, tiled=True)

    both = (mine.astype(F32) + swap_bands(other).astype(F32)).astype(BF16)
    parts = lax.all_to_all(both.reshape(LANES, K * 16, 128), "azimuth", split_axis=0, concat_axis=0, tiled=True)
    member = jnp.sum(parts.astype(F32), axis=0).astype(BF16)
    copies = jnp.broadcast_to(member[None], (members, K * 16, 128))
    copies = lax.all_to_all(copies, "ens", split_axis=0, concat_axis=0, tiled=True)
    half = jnp.sum(copies.astype(F32), axis=0)
    far = swap_bands(half)
    weight_grad = jnp.concatenate(
        [jnp.where(band == 0, half, far), jnp.where(band == 0, far, half)], axis=1
    ).reshape(K, 16, C)

    (sent,) = call(fields_body, [((LANES, CHUNK_IN, 128), BF16)], "fields", flops=600 << 20)(
        landed, tall, inv
    )
    landed = lax.all_to_all(sent, "azimuth", split_axis=0, concat_axis=0, tiled=True)
    field_grad, conv_out = call(
        unpack_body, [((8, WPART, C), BF16), ((4, VPART, C), BF16)], "unpack"
    )(landed)
    return (conv_out[None], field_grad[None], weight_grad)


def solution(mesh):
    placed = (
        P("ens", "polar", "azimuth", None),
        P(None, "polar", None, None),
        P("polar", None),
        P(),
        P("ens", "polar", "azimuth", None),
    )
    return jax.shard_map(
        local,
        mesh=mesh,
        in_specs=placed,
        out_specs=(
            P("ens", "polar", "azimuth", None),
            P("ens", "polar", "azimuth", None),
            P(None, "azimuth", None),
        ),
        check_vma=False,
    )
```

profile of v0, /device:TPU:2, one launch (start us, length us, event | category | flops | bytes accessed | tf_op | source)
XLA Modules:
  0.0 132.2 jit_solution(2833709493009395129)
XLA Ops:
  4.9 3.2 %all-to-all-start.2 = ((bf16[2,2,2160]{2,1,0:T(2,128)(2,1)}), bf16[2,2,2160]{2,1,0:T(2,128)(2,1)S(1)}, u32[]{:S(2)}, u32[]{:S(2)}) async-start(bf16[2,2,2160]{2,1,0:T(2,128)(2,1)} %reshape.86), calls=%async_computation.2 | async-start | bytes 34816 | tf_op jit(solution)/shard_map/all_to_all | solution.py:247
  9.6 1.9 %pack.1 = bf16[16,120,128]{2,1,0:T(8,128)(2,1)} custom-call(bf16[8,90,256]{2,1,0:T(8,128)(2,1)} %bitcast.27, bf16[4,45,256]{2,1,0:T(8,128)(2,1)} %bitcast.31), custom_call_target="tpu_custom_call" | custom-call | bytes 1048576 | tf_op jit(solution)/shard_map/pack/pallas_call | solution.py:63
  11.5 7.5 %all-to-all-start = ((bf16[16,120,128]{2,1,0:T(8,128)(2,1)}), bf16[16,120,128]{2,1,0:T(8,128)(2,1)S(1)}, u32[]{:S(2)}, u32[]{:S(2)}) async-start(bf16[16,120,128]{2,1,0:T(8,128)(2,1)} %pack.1), calls=%async_computation | async-start | bytes 983040 | tf_op jit(solution)/shard_map/all_to_all | solution.py:265
  19.3 4.7 %wide_table.1 = (bf16[1536,768]{1,0:T(8,128)(2,1)}, bf16[768,1536]{1,0:T(8,128)(2,1)}) custom-call(f32[16,768]{1,0:T(8,128)} %constant.41.clone.u1, f32[16,768]{1,0:T(8,128)} %constant.42.clone.u2, f32[96,768]{1,0:T(8,128)} %constant.43.clone.f1, f32[96,768]{1,0:T(8,128)} %constant.44.clone.f2), custom_call_target="tpu_custom_call" | custom-call | bytes 6291456 | tf_op jit(solution)/shard_map/wide_table/pallas_call | solution.py:63
  24.0 3.6 %narrow_table.1 = (bf16[4,384,512]{2,1,0:T(8,128)(2,1)}, bf16[4,512,384]{2,1,0:T(8,128)(2,1)}) custom-call(f32[16,512]{1,0:T(8,128)} %constant.45.clone.ca, f32[16,512]{1,0:T(8,128)} %constant.46.clone.sa, f32[24,512]{1,0:T(8,128)} %constant.47.clone.f0c, f32[24,512]{1,0:T(8,128)} %constant.48.clone.f0s, f32[24,512]{1,0:T(8,128)} %constant.49.clone.f1c, ...), custom_call_target="tpu_custom_call" | custom-call | bytes 4194304 | tf_op jit(solution)/shard_map/narrow_table/pallas_call | solution.py:63
  27.6 1.9 %all-to-all-done.r_ref = bf16[16,120,128]{2,1,0:T(8,128)(2,1)S(1)} async-done(((bf16[16,120,128]{2,1,0:T(8,128)(2,1)}), bf16[16,120,128]{2,1,0:T(8,128)(2,1)S(1)}, u32[]{:S(2)}, u32[]{:S(2)}) %all-to-all-start) | async-done | bytes 491552 | tf_op jit(solution)/shard_map/all_to_all | solution.py:265
  30.2 4.2 %spectra.1 = bf16[32,40,128]{2,1,0:T(8,128)(2,1)} custom-call(bf16[16,120,128]{2,1,0:T(8,128)(2,1)} %copy-done, bf16[768,1536]{1,0:T(8,128)(2,1)} %get-tuple-element.14.t_ref, bf16[4,512,384]{2,1,0:T(8,128)(2,1)} %get-tuple-element.15.vt_ref), custom_call_target="tpu_custom_call" | custom-call | flops 629145600 | bytes 1048576 | tf_op jit(solution)/shard_map/spectra/pallas_call | solution.py:63
  34.4 5.5 %all-to-all-start.1 = ((bf16[32,40,128]{2,1,0:T(8,128)(2,1)}), bf16[32,40,128]{2,1,0:T(8,128)(2,1)S(1)}, u32[]{:S(2)}, u32[]{:S(2)}) async-start(bf16[32,40,128]{2,1,0:T(8,128)(2,1)} %spectra.1), calls=%async_computation.1 | async-start | bytes 655360 | tf_op jit(solution)/shard_map/all_to_all | solution.py:285
  41.3 3.2 %mixing.1 = (bf16[9,256,384]{2,1,0:T(8,128)(2,1)}, bf16[9,384,256]{2,1,0:T(8,128)(2,1)}) custom-call(bf16[144,120]{1,0:T(8,128)(2,1)} %reshape.83.b_ref), custom_call_target="tpu_custom_call" | custom-call | bytes 4194304 | tf_op jit(solution)/shard_map/mixing/pallas_call | solution.py:63
  44.5 3.9 %all-to-all-done.1 = bf16[32,40,128]{2,1,0:T(8,128)(2,1)S(1)} async-done(((bf16[32,40,128]{2,1,0:T(8,128)(2,1)}), bf16[32,40,128]{2,1,0:T(8,128)(2,1)S(1)}, u32[]{:S(2)}, u32[]{:S(2)}) %all-to-all-start.1) | async-done | bytes 327712 | tf_op jit(solution)/shard_map/all_to_all | solution.py:285
  49.2 6.6 %middle.1 = (bf16[16,9,16,128]{3,2,1,0:T(8,128)(2,1)}, bf16[16,9,16,128]{3,2,1,0:T(8,128)(2,1)}, bf16[32,40,128]{2,1,0:T(8,128)(2,1)}) custom-call(s32[1,1]{1,0:T(1,128)} %bitcast.band_ref, bf16[16,2,40,128]{3,2,1,0:T(8,128)(2,1)} %bitcast.32, bf16[9,256,384]{2,1,0:T(8,128)(2,1)} %get-tuple-element.16.a_ref, bf16[9,384,256]{2,1,0:T(8,128)(2,1)} %get-tuple-element.17.at_ref, ...), custom_call_target="tpu_custom_call" | custom-call | flops 2147483648 | bytes 6291456 | tf_op jit(solution)/shard_map/middle/pallas_call | solution.py:287
  55.8 2.2 %collective-permute-done = bf16[16,9,16,128]{3,2,1,0:T(8,128)(2,1)S(1)} collective-permute-done((bf16[16,9,16,128]{3,2,1,0:T(8,128)(2,1)}, bf16[16,9,16,128]{3,2,1,0:T(8,128)(2,1)S(1)}, u32[]{:S(2)}, u32[]{:S(2)}) %collective-permute-start) | collective-permute-done | bytes 589856 | tf_op jit(solution)/shard_map/ppermute | solution.py:255
  58.0 1.2 add_convert_fusion
  59.2 15.7 %all_to_all.35 = bf16[16,144,128]{2,1,0:T(8,128)(2,1)S(1)} all-to-all(bf16[16,144,128]{2,1,0:T(8,128)(2,1)S(1)} %bitcast.26), channel_id=1, replica_groups=mesh['ens'=8,'polar'=2,'azimuth'=16] {'azimuth'}, dimensions={0} | all-to-all | bytes 1179648 | tf_op jit(solution)/shard_map/all_to_all | solution.py:307
  74.9 5.0 %all-to-all-start.3 = ((bf16[32,40,128]{2,1,0:T(8,128)(2,1)}), bf16[32,40,128]{2,1,0:T(8,128)(2,1)S(1)}, u32[]{:S(2)}, u32[]{:S(2)}) async-start(bf16[32,40,128]{2,1,0:T(8,128)(2,1)} %get-tuple-element.18), calls=%async_computation.3 | async-start | bytes 655360 | tf_op jit(solution)/shard_map/all_to_all | solution.py:304
  80.0 8.5 %all-to-all-done.3.r_ref = bf16[32,40,128]{2,1,0:T(8,128)(2,1)S(1)} async-done(((bf16[32,40,128]{2,1,0:T(8,128)(2,1)}), bf16[32,40,128]{2,1,0:T(8,128)(2,1)S(1)}, u32[]{:S(2)}, u32[]{:S(2)}) %all-to-all-start.3) | async-done | bytes 327712 | tf_op jit(solution)/shard_map/all_to_all | solution.py:304
  89.4 8.5 %all-to-all-start.6 = ((bf16[8,144,128]{2,1,0:T(8,128)(2,1)}), bf16[8,144,128]{2,1,0:T(8,128)(2,1)S(1)}, u32[]{:S(2)}, u32[]{:S(2)}) async-start(bf16[8,144,128]{2,1,0:T(8,128)(2,1)} %broadcast_in_dim.30), calls=%async_computation.6 | async-start | bytes 589824 | tf_op jit(solution)/shard_map/all_to_all | solution.py:310
  97.8 4.2 %fields.1 = bf16[16,120,128]{2,1,0:T(8,128)(2,1)} custom-call(bf16[32,40,128]{2,1,0:T(8,128)(2,1)} %copy-done.2, bf16[1536,768]{1,0:T(8,128)(2,1)} %get-tuple-element.19.tt_ref, bf16[4,384,512]{2,1,0:T(8,128)(2,1)} %get-tuple-element.20.v_ref), custom_call_target="tpu_custom_call" | custom-call | flops 629145600 | bytes 1048576 | tf_op jit(solution)/shard_map/fields/pallas_call | solution.py:63
  102.0 7.8 %all-to-all-done.6 = bf16[8,144,128]{2,1,0:T(8,128)(2,1)S(1)} async-done(((bf16[8,144,128]{2,1,0:T(8,128)(2,1)}), bf16[8,144,128]{2,1,0:T(8,128)(2,1)S(1)}, u32[]{:S(2)}, u32[]{:S(2)}) %all-to-all-start.6) | async-done | bytes 294944 | tf_op jit(solution)/shard_map/all_to_all | solution.py:310
  109.8 5.6 %all-to-all-start.4 = ((bf16[16,120,128]{2,1,0:T(8,128)(2,1)}), bf16[16,120,128]{2,1,0:T(8,128)(2,1)S(1)}, u32[]{:S(2)}, u32[]{:S(2)}) async-start(bf16[16,120,128]{2,1,0:T(8,128)(2,1)} %fields.1), calls=%async_computation.4 | async-start | bytes 983040 | tf_op jit(solution)/shard_map/all_to_all | solution.py:320
  115.5 9.8 %all-to-all-done.4.r_ref = bf16[16,120,128]{2,1,0:T(8,128)(2,1)S(1)} async-done(((bf16[16,120,128]{2,1,0:T(8,128)(2,1)}), bf16[16,120,128]{2,1,0:T(8,128)(2,1)S(1)}, u32[]{:S(2)}, u32[]{:S(2)}) %all-to-all-start.4) | async-done | bytes 491552 | tf_op jit(solution)/shard_map/all_to_all | solution.py:320
  126.1 1.9 %unpack.1 = (bf16[8,90,256]{2,1,0:T(8,128)(2,1)}, bf16[4,45,256]{2,1,0:T(8,128)(2,1)}) custom-call(bf16[16,120,128]{2,1,0:T(8,128)(2,1)} %copy-done.1), custom_call_target="tpu_custom_call" | custom-call | bytes 1048576 | tf_op jit(solution)/shard_map/unpack/pallas_call | solution.py:63
  128.0 1.6 %copy.43 = bf16[1,4,45,256]{3,1,2,0:T(4,128)(2,1)} copy(bf16[1,4,45,256]{3,2,1,0:T(8,128)(2,1)} %bitcast.34) | data formatting | bytes 184320
  129.5 1.9 %copy.44 = bf16[1,8,90,256]{3,1,2,0:T(8,128)(2,1)} copy(bf16[1,8,90,256]{3,2,1,0:T(8,128)(2,1)} %bitcast.30) | data formatting | bytes 737280
  (40 shorter events, 11.3 us)
Async XLA Ops:
  2.5 5.6 %copy-start.3 = (bf16[1,8,90,256]{3,1,2,0:T(8,128)(2,1)S(1)}, bf16[1,8,90,256]{3,1,2,0:T(8,128)(2,1)}, u32[]{:S(2)}) copy-start(bf16[1,8,90,256]{3,1,2,0:T(8,128)(2,1)} %param.15) | copy-start | bytes 1105924
  3.1 5.9 %copy-start.5 = (bf16[1,4,45,256]{3,1,2,0:T(4,128)(2,1)S(1)}, bf16[1,4,45,256]{3,1,2,0:T(4,128)(2,1)}, u32[]{:S(2)}) copy-start(bf16[1,4,45,256]{3,1,2,0:T(4,128)(2,1)} %param.19) | copy-start | bytes 276484
  4.9 6.6 %all-to-all-start.2 = ((bf16[2,2,2160]{2,1,0:T(2,128)(2,1)}), bf16[2,2,2160]{2,1,0:T(2,128)(2,1)S(1)}, u32[]{:S(2)}, u32[]{:S(2)}) async-start(bf16[2,2,2160]{2,1,0:T(2,128)(2,1)} %reshape.86), calls=%async_computation.2 | async-start | bytes 34816 | tf_op jit(solution)/shard_map/all_to_all | solution.py:247
  11.5 17.9 %all-to-all-start = ((bf16[16,120,128]{2,1,0:T(8,128)(2,1)}), bf16[16,120,128]{2,1,0:T(8,128)(2,1)S(1)}, u32[]{:S(2)}, u32[]{:S(2)}) async-start(bf16[16,120,128]{2,1,0:T(8,128)(2,1)} %pack.1), calls=%async_computation | async-start | bytes 983040 | tf_op jit(solution)/shard_map/all_to_all | solution.py:265
  29.5 0.8 copy-start
  34.4 14.0 %all-to-all-start.1 = ((bf16[32,40,128]{2,1,0:T(8,128)(2,1)}), bf16[32,40,128]{2,1,0:T(8,128)(2,1)S(1)}, u32[]{:S(2)}, u32[]{:S(2)}) async-start(bf16[32,40,128]{2,1,0:T(8,128)(2,1)} %spectra.1), calls=%async_computation.1 | async-start | bytes 655360 | tf_op jit(solution)/shard_map/all_to_all | solution.py:285
  48.4 0.7 copy-start.4
  55.8 2.2 %collective-permute-start = (bf16[16,9,16,128]{3,2,1,0:T(8,128)(2,1)}, bf16[16,9,16,128]{3,2,1,0:T(8,128)(2,1)S(1)}, u32[]{:S(2)}, u32[]{:S(2)}) collective-permute-start(bf16[16,9,16,128]{3,2,1,0:T(8,128)(2,1)} %get-tuple-element.24), channel_id=1, source_target_pairs={{0,16},{16,0},{1,17},{17,1},{2,18},{18,2},{3,19},{19,3},{4,20},{20... | collective-permute-start | bytes 1769480 | tf_op jit(solution)/shard_map/ppermute | solution.py:255
  74.9 13.6 %all-to-all-start.3 = ((bf16[32,40,128]{2,1,0:T(8,128)(2,1)}), bf16[32,40,128]{2,1,0:T(8,128)(2,1)S(1)}, u32[]{:S(2)}, u32[]{:S(2)}) async-start(bf16[32,40,128]{2,1,0:T(8,128)(2,1)} %get-tuple-element.18), calls=%async_computation.3 | async-start | bytes 655360 | tf_op jit(solution)/shard_map/all_to_all | solution.py:304
  88.5 9.3 %copy-start.2 = (bf16[32,40,128]{2,1,0:T(8,128)(2,1)}, bf16[32,40,128]{2,1,0:T(8,128)(2,1)S(1)}, u32[]{:S(2)}) copy-start(bf16[32,40,128]{2,1,0:T(8,128)(2,1)S(1)} %all-to-all-done.3.r_ref) | copy-start | bytes 983044
  89.4 20.4 %all-to-all-start.6 = ((bf16[8,144,128]{2,1,0:T(8,128)(2,1)}), bf16[8,144,128]{2,1,0:T(8,128)(2,1)S(1)}, u32[]{:S(2)}, u32[]{:S(2)}) async-start(bf16[8,144,128]{2,1,0:T(8,128)(2,1)} %broadcast_in_dim.30), calls=%async_computation.6 | async-start | bytes 589824 | tf_op jit(solution)/shard_map/all_to_all | solution.py:310
  109.8 15.5 %all-to-all-start.4 = ((bf16[16,120,128]{2,1,0:T(8,128)(2,1)}), bf16[16,120,128]{2,1,0:T(8,128)(2,1)S(1)}, u32[]{:S(2)}, u32[]{:S(2)}) async-start(bf16[16,120,128]{2,1,0:T(8,128)(2,1)} %fields.1), calls=%async_computation.4 | async-start | bytes 983040 | tf_op jit(solution)/shard_map/all_to_all | solution.py:320
  115.4 16.1 %collective-permute-start.1 = (f32[144,128]{1,0:T(8,128)S(1)}, f32[144,128]{1,0:T(8,128)S(1)}, u32[]{:S(2)}, u32[]{:S(2)}) collective-permute-start(f32[144,128]{1,0:T(8,128)S(1)} %convert_reduce_fusion), channel_id=1, source_target_pairs={{0,16},{16,0},{1,17},{17,1},{2,18},{18,2},{3,19},{19,3},{4,20},{20... | collective-permute-start | bytes 221192 | tf_op jit(solution)/shard_map/ppermute | solution.py:255
  125.3 0.8 copy-start.1
where the time goes:
time: 134 us; the launch traced here: 132 us
  starting transfers between devices  35.3 us (26%)
  waiting for transfers between devices  34.1 us (25%)
  Pallas kernels  30.3 us (23%)
  blocking collectives  15.7 us (12%)
  local copies, waits for them, and re-layouts  12.5 us (9%)
  other arithmetic  3.39 us (3%)
    pallas_call x7, Pallas kernels, run(): pl.pallas_call(body, out_shape=[jax.ShapeDtypeStruct(s, d) for s, d in ou...  23.7 us
    all_to_all x1, blocking collectives, local(): lax.all_to_all(both.reshape(LANES, K * 16, 128), 'azimuth', split_axis=0,...  15.7 us
    all_to_all x2, starting transfers between devices, local(): lax.all_to_all(sent, 'azimuth', split_axis=0, concat_axis=0, tiled=True)  13 us
    all_to_all x2, waiting for transfers between devices, local(): lax.all_to_all(sent, JOINT, split_axis=0, concat_axis=0, tiled=True)  12.4 us
    all_to_all x2, waiting for transfers between devices, local(): lax.all_to_all(sent, 'azimuth', split_axis=0, concat_axis=0, tiled=True)  11.7 us
    all_to_all x2, starting transfers between devices, local(): lax.all_to_all(sent, JOINT, split_axis=0, concat_axis=0, tiled=True)  10.5 us
    all_to_all x1, starting transfers between devices, local(): lax.all_to_all(copies, 'ens', split_axis=0, concat_axis=0, tiled=True)  8.47 us
    unnamed x18, local copies, waits for them, and re-layouts  8.35 us
  transfers between devices with their start and end apart: 8, of which 6 were waited for; matrix products, arithmetic and copies ran while one was open for 5% of the time, Pallas kernels for 15%

commit v1 on v0

v1 whole, which is shorter than its diff:
```python
import math

import jax
import jax.numpy as jnp
import numpy as np
from jax import lax
from jax.experimental import pallas as pl
from jax.experimental.pallas import tpu as pltpu
from jax.sharding import PartitionSpec as P

WIN, WOUT, MODES = 1440, 720, 360
K, C, SUPPORT = 9, 256, 5
HOUT, HIN = 8, 16
LANES, BANDS = 16, 2
SHARES = LANES * BANDS
HALF = LANES // 2
M12, M16 = 12, 16
WPART, WROWS = 90, 96
VPART, VROWS = 45, 24
CHUNK_IN = WROWS + VROWS
CHUNK_MID = M16 + 2 * M12
CHUNK_OUT = 2 * CHUNK_MID + 16 * K
F32, BF16 = jnp.float32, jnp.bfloat16
JOINT = ("polar", "azimuth")


def factor_tables():
    def build(slots, part, steps, period, scale):
        mode_all, keep, imag = slots
        parts = []
        for e in range(BANDS):
            mode = mode_all + e
            ok = keep & (mode < MODES)
            alpha = 2 * math.pi * ((mode[None, :] * (part * np.arange(HALF)[:, None])) % period) / period
            beta = 2 * math.pi * ((mode[None, :] * steps[:, None]) % period) / period
            ok = ok[None, :] & (steps[:, None] < part)
            size = np.where(mode == 0, 1.0, 2.0)[None, :] / WIN if scale else 1.0
            parts.append(
                (
                    np.where(imag[None, :], -np.sin(alpha), np.cos(alpha)),
                    np.where(imag[None, :], -np.cos(alpha), -np.sin(alpha)),
                    np.where(ok, size * np.cos(beta), 0.0),
                    np.where(ok, size * np.sin(beta), 0.0),
                )
            )
        return [np.stack(group).astype(np.float32) for group in zip(*parts)]

    a, ri, i = np.meshgrid(np.arange(LANES), np.arange(2), np.arange(M12), indexing="ij")
    slots = ((2 * (M12 * a + i)).reshape(-1), np.ones(a.size, bool), ri.reshape(-1) == 1)
    wide = build(slots, WPART, np.arange(WROWS), WIN, False)
    ri, a, i = np.meshgrid(np.arange(2), np.arange(LANES), np.arange(M16), indexing="ij")
    slots = ((2 * (M12 * a + i)).reshape(-1), i.reshape(-1) < M12, ri.reshape(-1) == 1)
    narrow = build(slots, VPART, np.arange(2 * VROWS), WOUT, True)
    return wide, narrow


def call(body, outs, name, flops=0, scratch=(), nbytes=1 << 20, vmem=16, smem=0):
    def run(*args):
        places = [pl.BlockSpec(memory_space=pltpu.SMEM)] * smem
        places += [pl.BlockSpec(memory_space=pltpu.VMEM)] * (len(args) - smem)
        return pl.pallas_call(
            body,
            out_shape=[jax.ShapeDtypeStruct(s, d) for s, d in outs],
            in_specs=places,
            out_specs=[pl.BlockSpec(memory_space=pltpu.VMEM)] * len(outs),
            scratch_shapes=list(scratch),
            name=name,
            compiler_params=pltpu.CompilerParams(vmem_limit_bytes=vmem << 20),
            cost_estimate=pl.CostEstimate(flops=flops, bytes_accessed=nbytes, transcendentals=0),
        )(*args)

    return run


def low_half(shape):
    return lax.broadcasted_iota(jnp.int32, shape, len(shape) - 1) < 64


def swap64(value):
    return pltpu.roll(value, 64, value.ndim - 1)


def dot(a, b):
    return jnp.dot(a, b, preferred_element_type=F32)


def one_hot(shape, row_of_column):
    row = lax.broadcasted_iota(jnp.int32, shape, 0)
    column = lax.broadcasted_iota(jnp.int32, shape, 1)
    return jnp.where(row == row_of_column(column), 1.0, 0.0).astype(BF16)


def row_of_latitude(column):
    return 16 * (column % 8) + column // 8


def row_of_output(column):
    return 48 * (column % 4) + column // 4


def pack_body(f_ref, g_ref, o_ref, flat_ref):
    for j in range(6):
        count = min(128, 8 * WPART - 128 * j)
        order = one_hot((128, count), row_of_latitude)
        block = dot(order, f_ref[128 * j : 128 * j + count, :]).astype(BF16)
        for r in range(8):
            for h in range(2):
                piece = block[16 * r : 16 * (r + 1), 128 * h : 128 * (h + 1)]
                o_ref[2 * r + h, 16 * j : 16 * (j + 1), :] = piece
    for v in range(VPART):
        flat_ref[4 * v : 4 * (v + 1), :] = g_ref[v].astype(F32)
    flat_ref[4 * VPART : 192, :] = jnp.zeros((192 - 4 * VPART, C), F32)
    rows = dot(one_hot((192, 192), row_of_output), flat_ref[...].astype(BF16))
    keep = low_half((VROWS, 128))
    for o in range(4):
        for i in range(2):
            cols = slice(128 * i, 128 * (i + 1))
            top, bottom = rows[48 * o : 48 * o + 24, cols], rows[48 * o + 24 : 48 * o + 48, cols]
            even = jnp.where(keep, top, swap64(bottom))
            odd = jnp.where(keep, swap64(top), bottom)
            o_ref[4 * o + 2 * i, WROWS:CHUNK_IN, :] = even.astype(BF16)
            o_ref[4 * o + 2 * i + 1, WROWS:CHUNK_IN, :] = odd.astype(BF16)


def flip(source, target, rows, columns):
    for i in range(rows // 128):
        for j in range(columns // 128):
            piece = source[128 * i : 128 * (i + 1), 128 * j : 128 * (j + 1)].astype(F32)
            target[128 * j : 128 * (j + 1), 128 * i : 128 * (i + 1)] = piece.T.astype(BF16)


def table_body(wu1, wu2, wf1, wf2, nu1, nu2, nf1, nf2, w_ref, wt_ref, v_ref, vt_ref):
    for e in range(BANDS):
        for b in range(HALF):
            one, two = wu1[e, b : b + 1, :], wu2[e, b : b + 1, :]
            block = one * wf1[e] + two * wf2[e]
            w_ref[e, WROWS * b : WROWS * (b + 1), :] = block.astype(BF16)
            one, two = nu1[e, b : b + 1, :], nu2[e, b : b + 1, :]
            for part in range(2):
                rows = slice(VROWS * part, VROWS * (part + 1))
                block = one * nf1[e, rows, :] + two * nf2[e, rows, :]
                start = VROWS * (HALF * part + b)
                v_ref[e, start : start + VROWS, :] = block.astype(BF16)
        flip(w_ref.at[e], wt_ref.at[e], HALF * WROWS, 2 * LANES * M12)
        flip(v_ref.at[e], vt_ref.at[e], 2 * HALF * VROWS, 2 * LANES * M16)


def spectra_body(r_ref, wt_ref, vt_ref, o_ref):
    left = r_ref[0:HALF, 0:WROWS, :].reshape(HALF * WROWS, 128).astype(F32)
    right = r_ref[HALF:LANES, 0:WROWS, :].reshape(HALF * WROWS, 128).astype(F32)
    g_left = r_ref[0:HALF, WROWS:CHUNK_IN, :].reshape(HALF * VROWS, 128).astype(F32)
    g_right = r_ref[HALF:LANES, WROWS:CHUNK_IN, :].reshape(HALF * VROWS, 128).astype(F32)
    keep = low_half((HALF * VROWS, 128))
    for e in range(BANDS):
        x = (left + right if e == 0 else left - right).astype(BF16)
        g = g_left + g_right if e == 0 else g_left - g_right
        turned = swap64(g)
        both = jnp.concatenate([jnp.where(keep, g, turned), jnp.where(keep, turned, g)], axis=0).astype(BF16)
        shares = slice(LANES * e, LANES * (e + 1))
        o_ref[shares, M16:CHUNK_MID, :] = dot(wt_ref[e], x).astype(BF16).reshape(LANES, 2 * M12, 128)
        got = dot(vt_ref[e], both)
        count = LANES * M16
        out = jnp.where(low_half((count, 128)), got[:count], got[count:])
        o_ref[shares, 0:M16, :] = out.astype(BF16).reshape(LANES, M16, 128)


def mixing_body(b_ref, a_ref, at_ref, p_ref):
    rows, width = K * 16, HIN * 2 * M12
    row = lax.broadcasted_iota(jnp.int32, (120, width), 0)
    lane = lax.broadcasted_iota(jnp.int32, (120, width), 1)
    owner = (lax.broadcasted_iota(jnp.int32, (rows, width), 0) // 2) % HOUT
    total = jnp.zeros((rows, width), F32)
    for o in range(HOUT):
        shift = jnp.where(lane - row == 48 * (o - 1), 1.0, 0.0).astype(BF16)
        total = jnp.where(owner == o, dot(b_ref[...], shift), total)
    p_ref[...] = total
    mode = lax.broadcasted_iota(jnp.int32, (M16, width), 1) % M12
    same = lax.broadcasted_iota(jnp.int32, (M16, width), 0) == mode
    for i in range(rows):
        block = jnp.where(same, jnp.broadcast_to(p_ref[i : i + 1, :], (M16, width)), 0.0)
        a_ref[i // 16, M16 * (i % 16) : M16 * (i % 16 + 1), :] = block.astype(BF16)
    spot = lax.broadcasted_iota(jnp.int32, (16, 256), 1) // M16
    spread = jnp.where(lax.broadcasted_iota(jnp.int32, (16, 256), 0) == spot, 1.0, 0.0).astype(BF16)
    left = lax.broadcasted_iota(jnp.int32, (width, 256), 0) % M12
    right = lax.broadcasted_iota(jnp.int32, (width, 256), 1) % M16
    for k in range(K):
        part = p_ref[16 * k : 16 * (k + 1), :].astype(BF16)
        grown = lax.dot_general(part, spread, (((0,), (0,)), ((), ())), preferred_element_type=F32)
        at_ref[k] = jnp.where(left == right, grown, 0.0).astype(BF16)


def middle_body(band_ref, r_ref, a_ref, at_ref, w_ref, mine_ref, other_ref, gs_ref, out_ref, sg_ref):
    keep = low_half((M16, 128))
    for o in range(HOUT):
        for i in range(2):
            first = r_ref[2 * o + i, 0, 0:M16, :].astype(F32)
            second = r_ref[2 * o + i, 1, 0:M16, :].astype(F32)
            cols = slice(128 * i, 128 * (i + 1))
            gs_ref[32 * o : 32 * o + 16, cols] = jnp.where(keep, first, swap64(second)).astype(BF16)
            gs_ref[32 * o + 16 : 32 * o + 32, cols] = jnp.where(keep, swap64(first), second).astype(BF16)
    rows = HIN * 2 * M12
    x = jnp.concatenate(
        [r_ref[:, h, M16:CHUNK_MID, :].reshape(rows, 128) for h in range(2)], axis=1
    )
    gs = gs_ref[...]
    low = band_ref[0, 0] == 0

    for k in range(K):
        mixed = dot(a_ref[k], x).astype(BF16)
        out_now = dot(mixed, w_ref[k])
        grad = lax.dot_general(mixed, gs, (((0,), (0,)), ((), ())), preferred_element_type=F32)
        where_to = (slice(None), slice(CHUNK_MID + 16 * k, CHUNK_MID + 16 * (k + 1)), slice(None))
        shape = (LANES, 16, 128)
        mine_ref[where_to] = jnp.where(low, grad[:, :128], grad[:, 128:]).astype(BF16).reshape(shape)
        other_ref[where_to] = jnp.where(low, grad[:, 128:], grad[:, :128]).astype(BF16).reshape(shape)
        back = lax.dot_general(gs, w_ref[k], (((1,), (1,)), ((), ())), preferred_element_type=F32)
        sg_now = dot(at_ref[k], back.astype(BF16))
        if k == 0:
            out_ref[...] = out_now
            sg_ref[...] = sg_now
        else:
            out_ref[...] += out_now
            sg_ref[...] += sg_now

    def output_rows(n):
        o, q = n // 4, n % 4
        cols = slice(128 * (q // 2), 128 * (q // 2 + 1))
        re = out_ref[32 * o : 32 * o + 16, cols]
        im = out_ref[32 * o + 16 : 32 * o + 32, cols]
        return jnp.where(keep, re, swap64(im)) if q % 2 == 0 else jnp.where(keep, swap64(re), im)

    def field_rows(n):
        r, h = n // 2, n % 2
        return sg_ref[24 * r : 24 * (r + 1), 128 * h : 128 * (h + 1)]

    for a in range(LANES):
        for rows, make in ((slice(0, M16), output_rows), (slice(M16, CHUNK_MID), field_rows)):
            first, second = make(a), make(a + LANES)
            mine_ref[a, rows, :] = jnp.where(low, first, second).astype(BF16)
            other_ref[a, rows, :] = jnp.where(low, second, first).astype(BF16)


def merge_body(band_ref, mine_ref, got_ref, o_ref):
    low = band_ref[0, 0] == 0
    for a in range(LANES):
        mine, got = mine_ref[a, 0:CHUNK_MID, :].astype(F32), got_ref[a, 0:CHUNK_MID, :].astype(F32)
        o_ref[a, 0:CHUNK_MID, :] = jnp.where(low, mine, got).astype(BF16)
        o_ref[a, CHUNK_MID : 2 * CHUNK_MID, :] = jnp.where(low, got, mine).astype(BF16)
        mine, got = mine_ref[a, CHUNK_MID:, :].astype(F32), got_ref[a, CHUNK_MID:, :].astype(F32)
        o_ref[a, 2 * CHUNK_MID :, :] = (mine + got).astype(BF16)


def fields_body(r_ref, w_ref, v_ref, o_ref):
    fields, outs = [], []
    for e in range(BANDS):
        start = CHUNK_MID * e
        sg = r_ref[:, start + M16 : start + CHUNK_MID, :].reshape(LANES * 2 * M12, 128)
        fields.append(dot(w_ref[e], sg))
        c = r_ref[:, start : start + M16, :].reshape(LANES * M16, 128).astype(F32)
        turned = swap64(c)
        keep = low_half(c.shape)
        both = jnp.concatenate([jnp.where(keep, c, turned), jnp.where(keep, turned, c)], axis=0).astype(BF16)
        got = dot(v_ref[e], both)
        count = HALF * VROWS
        outs.append(jnp.where(low_half((count, 128)), got[:count], got[count:]))
    for side in range(2):
        lanes = slice(HALF * side, HALF * (side + 1))
        field = fields[0] + fields[1] if side == 0 else fields[0] - fields[1]
        o_ref[lanes, 0:WROWS, :] = field.astype(BF16).reshape(HALF, WROWS, 128)
        out = outs[0] + outs[1] if side == 0 else outs[0] - outs[1]
        o_ref[lanes, WROWS:CHUNK_IN, :] = out.astype(BF16).reshape(HALF, VROWS, 128)


def unpack_body(r_ref, f_ref, c_ref, flat_ref):
    for j in range(6):
        count = min(128, 8 * WPART - 128 * j)
        halves = [
            jnp.concatenate([r_ref[2 * r + h, 16 * j : 16 * (j + 1), :] for r in range(8)], axis=0)
            for h in range(2)
        ]
        order = one_hot((128, count), row_of_latitude)
        block = lax.dot_general(
            order, jnp.concatenate(halves, axis=1), (((0,), (0,)), ((), ())), preferred_element_type=F32
        )
        f_ref[128 * j : 128 * j + count, :] = block.astype(BF16)
    keep = low_half((VROWS, 128))
    for o in range(4):
        for i in range(2):
            even = r_ref[4 * o + 2 * i, WROWS:CHUNK_IN, :].astype(F32)
            odd = r_ref[4 * o + 2 * i + 1, WROWS:CHUNK_IN, :].astype(F32)
            cols = slice(128 * i, 128 * (i + 1))
            flat_ref[48 * o : 48 * o + 24, cols] = jnp.where(keep, even, swap64(odd))
            flat_ref[48 * o + 24 : 48 * o + 48, cols] = jnp.where(keep, swap64(even), odd)
    rows = lax.dot_general(
        one_hot((192, 192), row_of_output),
        flat_ref[...].astype(BF16),
        (((0,), (0,)), ((), ())),
        preferred_element_type=F32,
    )
    for v in range(VPART):
        c_ref[v] = rows[4 * v : 4 * (v + 1), :].astype(BF16)


def mask_filters(filters, support):
    window = jnp.arange(filters.shape[2], dtype=jnp.int32)
    inside = (window[None, :] >= support[:, 0:1]) & (window[None, :] <= support[:, 1:2])
    return jnp.where(inside[None, :, :, None], filters, jnp.zeros_like(filters))


def swap_bands(value):
    return lax.ppermute(value, "polar", [(0, 1), (1, 0)])


def filter_rows(basis_spectra, support, low):
    masked = mask_filters(basis_spectra, support)
    pairs = masked.reshape(K, HOUT // BANDS, SUPPORT, 2, MODES)
    pairs = jnp.pad(pairs, [(0, 0)] * 4 + [(0, SHARES * M12 - MODES)])
    start = lax.axis_index("azimuth") * 2 * M12
    here = lax.dynamic_slice_in_dim(pairs, start, 2 * M12, 4).reshape(pairs.shape[:4] + (M12, 2))
    mine = jnp.where(low, here[..., 0], here[..., 1])
    got = swap_bands(jnp.where(low, here[..., 1], here[..., 0]))
    here = jnp.concatenate([jnp.where(low, mine, got), jnp.where(low, got, mine)], axis=1)
    re, im = here[:, :, :, 0], here[:, :, :, 1]
    rows = jnp.stack([jnp.stack([re, -im], axis=3), jnp.stack([im, re], axis=3)], axis=2)
    return rows.reshape(K * HOUT * 2, SUPPORT * 2 * M12)


def local(fields, basis_spectra, support, weights, out_grad):
    band = lax.axis_index("polar")
    low = band == 0
    spot = band.astype(jnp.int32).reshape(1, 1)
    wide, narrow = factor_tables()
    (sent,) = call(
        pack_body, [((LANES, CHUNK_IN, 128), BF16)], "pack", scratch=[pltpu.VMEM((192, C), F32)], vmem=8
    )(jnp.swapaxes(fields[0], 0, 1).reshape(8 * WPART, C), jnp.swapaxes(out_grad[0], 0, 1))
    landed = lax.all_to_all(sent, "azimuth", split_axis=0, concat_axis=0, tiled=True)

    filters, limits, sent = lax.optimization_barrier((basis_spectra, support, sent))
    rows = filter_rows(filters, limits, low)
    tables = [jnp.asarray(a) for a in wide + narrow]
    tables, sent = lax.optimization_barrier((tables, sent))
    tall, flat, inv, inv_t = call(
        table_body,
        [((2, 768, 384), BF16), ((2, 384, 768), BF16), ((2, 384, 512), BF16), ((2, 512, 384), BF16)],
        "tables",
        nbytes=5 << 20,
    )(*tables)
    mix, mix_t = call(
        mixing_body,
        [((K, 256, 384), BF16), ((K, 384, 256), BF16)],
        "mixing",
        scratch=[pltpu.VMEM((K * 16, 384), F32)],
        nbytes=4 << 20,
    )(rows)

    (sent,) = call(spectra_body, [((SHARES, CHUNK_MID, 128), BF16)], "spectra", flops=300 << 20)(
        landed, flat, inv_t
    )
    landed = lax.all_to_all(sent, JOINT, split_axis=0, concat_axis=0, tiled=True)

    chunk = (LANES, CHUNK_MID + 16 * K, 128)
    mine, other = call(
        middle_body,
        [(chunk, BF16), (chunk, BF16)],
        "middle",
        flops=2 << 30,
        nbytes=6 << 20,
        scratch=[pltpu.VMEM((256, 256), BF16), pltpu.VMEM((256, 256), F32), pltpu.VMEM((384, 256), F32)],
        smem=1,
        vmem=24,
    )(spot, landed.reshape(HIN, 2, CHUNK_MID, 128), mix, mix_t, weights)
    got = swap_bands(other)
    (sent,) = call(merge_body, [((LANES, CHUNK_OUT, 128), BF16)], "merge", nbytes=2 << 20, smem=1, vmem=8)(
        spot, mine, got
    )
    landed = lax.all_to_all(sent, "azimuth", split_axis=0, concat_axis=0, tiled=True)

    half = jnp.sum(landed[:, 2 * CHUNK_MID :, :].astype(F32), axis=0)
    for step in (1, 2, 4):
        half = half + lax.ppermute(half, "ens", [(i, i ^ step) for i in range(lax.axis_size("ens"))])
    far = swap_bands(half)
    weight_grad = jnp.concatenate([jnp.where(low, half, far), jnp.where(low, far, half)], axis=1)

    (sent,) = call(fields_body, [((LANES, CHUNK_IN, 128), BF16)], "fields", flops=300 << 20)(
        landed, tall, inv
    )
    landed = lax.all_to_all(sent, "azimuth", split_axis=0, concat_axis=0, tiled=True)
    field_grad, conv_out = call(
        unpack_body,
        [((8 * WPART, C), BF16), ((VPART, 4, C), BF16)],
        "unpack",
        scratch=[pltpu.VMEM((192, C), F32)],
        vmem=8,
    )(landed)
    field_grad = jnp.swapaxes(field_grad.reshape(WPART, 8, C), 0, 1)
    return (jnp.swapaxes(conv_out, 0, 1)[None], field_grad[None], weight_grad.reshape(K, 16, C))


def solution(mesh):
    placed = (
        P("ens", "polar", "azimuth", None),
        P(None, "polar", None, None),
        P("polar", None),
        P(),
        P("ens", "polar", "azimuth", None),
    )
    return jax.shard_map(
        local,
        mesh=mesh,
        in_specs=placed,
        out_specs=(
            P("ens", "polar", "azimuth", None),
            P("ens", "polar", "azimuth", None),
            P(None, "azimuth", None),
        ),
        check_vma=False,
    )
```

time: 134 us -> 106 us (0.79)
  Pallas kernels: 30.3 us -> 11.2 us
  waiting for transfers between devices: 34.1 us -> 18.3 us
  local copies, waits for them, and re-layouts: 12.5 us -> 17.3 us
  blocking collectives: 15.7 us -> 19.3 us
  starting transfers between devices: 35.3 us -> 33.2 us
    ppermute x0 -> x3, starting transfers between devices: none -> 13.1 us  [local(): lax.ppermute(half, 'ens', [(i, i ^ step) for i in range(lax.axis_size('en...]
    pallas_call x7 -> x8, Pallas kernels: 23.7 us -> 11.2 us  [run(): pl.pallas_call(body, out_shape=[jax.ShapeDtypeStruct(s, d) for s, d in ou...]
    all_to_all x2 -> x0, starting transfers between devices: 11.7 us -> none  [the longest x1 8.47 us: local(): lax.all_to_all(copies, 'ens', split_axis=0, concat_axis=0, tiled=True)]
    all_to_all x2 -> x1, waiting for transfers between devices: 12.4 us -> 3.47 us  [local(): lax.all_to_all(sent, JOINT, split_axis=0, concat_axis=0, tiled=True)]
    all_to_all x2 -> x0, waiting for transfers between devices: 7.76 us -> none  [the longest x1 7.76 us: local(): lax.all_to_all(copies, 'ens', split_axis=0, concat_axis=0, tiled=True)]
    pallas_call x1 -> x0, Pallas kernels: 6.62 us -> none  [local(): pl.pallas_call(middle_body, out_shape=[jax.ShapeDtypeStruct((LANES, K, 16...]
    all_to_all x2, waiting for transfers between devices: 11.7 us -> 6.63 us  [local(): lax.all_to_all(sent, 'azimuth', split_axis=0, concat_axis=0, tiled=True)]
    ppermute x0 -> x3, waiting for transfers between devices: none -> 4.77 us  [local(): lax.ppermute(half, 'ens', [(i, i ^ step) for i in range(lax.axis_size('en...]
  transfers between devices with their start and end apart: 8 -> 9, of which waited for: 6 -> 6; matrix products, arithmetic and copies ran while one was open for 5% -> 11% of each run, Pallas kernels for 15% -> 4%
where the time goes in v1:
time: 106 us; the launch traced here: 105 us
  starting transfers between devices  33.2 us (31%)
  blocking collectives  19.3 us (18%)
  waiting for transfers between devices  18.3 us (17%)
  local copies, waits for them, and re-layouts  17.3 us (16%)
  Pallas kernels  11.2 us (11%)
  other arithmetic  4.7 us (4%)
    all_to_all x1, blocking collectives, local(): lax.all_to_all(sent, 'azimuth', split_axis=0, concat_axis=0, tiled=True)  19.3 us
    ppermute x3, starting transfers between devices, local(): lax.ppermute(half, 'ens', [(i, i ^ step) for i in range(lax.axis_size('en...  13.1 us
    all_to_all x2, starting transfers between devices, local(): lax.all_to_all(sent, 'azimuth', split_axis=0, concat_axis=0, tiled=True)  12.3 us
    pallas_call x8, Pallas kernels, run(): pl.pallas_call(body, out_shape=[jax.ShapeDtypeStruct(s, d) for s, d in ou...  11.2 us
    unnamed x38, local copies, waits for them, and re-layouts  10.6 us
    all_to_all x1, starting transfers between devices, local(): lax.all_to_all(sent, JOINT, split_axis=0, concat_axis=0, tiled=True)  7.48 us
    all_to_all x2, waiting for transfers between devices, local(): lax.all_to_all(sent, 'azimuth', split_axis=0, concat_axis=0, tiled=True)  6.63 us
    ppermute x3, waiting for transfers between devices, local(): lax.ppermute(half, 'ens', [(i, i ^ step) for i in range(lax.axis_size('en...  4.77 us
  transfers between devices with their start and end apart: 9, of which 6 were waited for; matrix products, arithmetic and copies ran while one was open for 11% of the time, Pallas kernels for 4%

profile of v1, /device:TPU:2, one launch (start us, length us, event | category | flops | bytes accessed | tf_op | source)
XLA Modules:
  0.0 104.9 jit_solution(2551246625120127509)
XLA Ops:
  2.5 1.2 %pack.1 = bf16[16,120,128]{2,1,0:T(8,128)(2,1)} custom-call(bf16[720,256]{1,0:T(8,128)(2,1)S(1)} %bitcast.33, bf16[45,4,256]{2,1,0:T(4,128)(2,1)S(1)} %bitcast.35), custom_call_target="tpu_custom_call" | custom-call | bytes 1048576 | tf_op jit(solution)/shard_map/pack/pallas_call | solution.py:61
  3.7 7.5 %all-to-all-start = ((bf16[16,120,128]{2,1,0:T(8,128)(2,1)}), bf16[16,120,128]{2,1,0:T(8,128)(2,1)S(1)}, u32[]{:S(2)}, u32[]{:S(2)}) async-start(bf16[16,120,128]{2,1,0:T(8,128)(2,1)} %pack.1), calls=%async_computation | async-start | bytes 983040 | tf_op jit(solution)/shard_map/all_to_all | solution.py:336
  11.4 3.2 %copy.31 = bf16[9,4,5,720]{0,3,2,1:T(8,128)(2,1)} copy(bf16[9,4,5,720]{3,1,2,0:T(4,128)(2,1)S(1)} %broadcast_select_fusion.2) | data formatting | bytes 518400 | tf_op jit(solution)/shard_map/reshape | solution.py:316
  20.1 1.3 %tables.1 = (bf16[2,768,384]{2,1,0:T(8,128)(2,1)S(1)}, bf16[2,384,768]{2,1,0:T(8,128)(2,1)S(1)}, bf16[2,384,512]{2,1,0:T(8,128)(2,1)S(1)}, bf16[2,512,384]{2,1,0:T(8,128)(2,1)S(1)}) custom-call(f32[2,8,384]{2,1,0:T(8,128)S(1)} %copy-done.12, f32[2,8,384]{2,1,0:T(8,128)S(1)} %copy-done.13, f32[2,96,384]{2,1,0:T(8,128)S(1)} %copy-done.5, ...), custom_call_target="tpu_custom_call" | custom-call | bytes 5242880 | tf_op jit(solution)/shard_map/tables/pallas_call | solution.py:61
  24.3 1.1 %copy-done.3 = bf16[2,512,384]{2,1,0:T(8,128)(2,1)S(1)} copy-done((bf16[2,512,384]{2,1,0:T(8,128)(2,1)S(1)}, bf16[2,512,384]{2,1,0:T(8,128)(2,1)}, u32[]{:S(2)}) %copy-start.3) | copy-done | bytes 786456
  25.4 1.5 %spectra.1 = bf16[32,40,128]{2,1,0:T(8,128)(2,1)} custom-call(bf16[16,120,128]{2,1,0:T(8,128)(2,1)S(1)} %all-to-all-done.r_ref, bf16[2,384,768]{2,1,0:T(8,128)(2,1)S(1)} %get-tuple-element.31.wt_ref, bf16[2,512,384]{2,1,0:T(8,128)(2,1)S(1)} %copy-done.3), custom_call_target="tpu_custom_call" | custom-call | flops 314572800 | bytes 1048576 | tf_op jit(solution)/shard_map/spectra/pallas_call | solution.py:61
  26.9 7.5 %all-to-all-start.1 = ((bf16[32,40,128]{2,1,0:T(8,128)(2,1)}), bf16[32,40,128]{2,1,0:T(8,128)(2,1)S(1)}, u32[]{:S(2)}, u32[]{:S(2)}) async-start(bf16[32,40,128]{2,1,0:T(8,128)(2,1)} %spectra.1), calls=%async_computation.1 | async-start | bytes 655360 | tf_op jit(solution)/shard_map/all_to_all | solution.py:359
  36.9 1.3 %mixing.1 = (bf16[9,256,384]{2,1,0:T(8,128)(2,1)S(1)}, bf16[9,384,256]{2,1,0:T(8,128)(2,1)S(1)}) custom-call(bf16[144,120]{1,0:T(8,128)(2,1)S(1)} %reshape.86.b_ref), custom_call_target="tpu_custom_call" | custom-call | bytes 4194304 | tf_op jit(solution)/shard_map/mixing/pallas_call | solution.py:61
  38.2 1.2 %copy-done.14 = bf16[9,384,256]{2,1,0:T(8,128)(2,1)} copy-done((bf16[9,384,256]{2,1,0:T(8,128)(2,1)}, bf16[9,384,256]{2,1,0:T(8,128)(2,1)S(1)}, u32[]{:S(2)}) %copy-start.14) | copy-done | bytes 1769496
  39.4 3.5 %all-to-all-done.1 = bf16[32,40,128]{2,1,0:T(8,128)(2,1)S(1)} async-done(((bf16[32,40,128]{2,1,0:T(8,128)(2,1)}), bf16[32,40,128]{2,1,0:T(8,128)(2,1)S(1)}, u32[]{:S(2)}, u32[]{:S(2)}) %all-to-all-start.1) | async-done | bytes 327712 | tf_op jit(solution)/shard_map/all_to_all | solution.py:359
  42.9 1.5 %copy-done.15 = bf16[9,384,256]{2,1,0:T(8,128)(2,1)S(1)} copy-done((bf16[9,384,256]{2,1,0:T(8,128)(2,1)S(1)}, bf16[9,384,256]{2,1,0:T(8,128)(2,1)}, u32[]{:S(2)}) %copy-start.15) | copy-done | bytes 1769496
  44.4 1.3 %copy-done.16 = bf16[9,256,256]{2,1,0:T(8,128)(2,1)S(1)} copy-done((bf16[9,256,256]{2,1,0:T(8,128)(2,1)S(1)}, bf16[9,256,256]{2,1,0:T(8,128)(2,1)}, u32[]{:S(2)}) %copy-start.16) | copy-done | bytes 1179672
  45.7 3.3 %middle.1 = (bf16[16,184,128]{2,1,0:T(8,128)(2,1)S(1)}, bf16[16,184,128]{2,1,0:T(8,128)(2,1)S(1)}) custom-call(s32[1,1]{1,0:T(1,128)} %bitcast.band_ref, bf16[16,2,40,128]{3,2,1,0:T(8,128)(2,1)S(1)} %bitcast.34, bf16[9,256,384]{2,1,0:T(8,128)(2,1)S(1)} %get-tuple-element.35.a_ref, bf16[9,384,256]{2,1,0:T(8,128)(2,1)S(1)} %copy-done.15, ...), custom_call_target="tpu_custom_call" | custom-call | flops 2147483648 | bytes 6291456 | tf_op jit(solution)/shard_map/middle/pallas_call | solution.py:61
  49.2 2.2 %collective-permute-done.1.got_ref = bf16[16,184,128]{2,1,0:T(8,128)(2,1)S(1)} collective-permute-done((bf16[16,184,128]{2,1,0:T(8,128)(2,1)S(1)}, bf16[16,184,128]{2,1,0:T(8,128)(2,1)S(1)}, u32[]{:S(2)}, u32[]{:S(2)}) %collective-permute-start.1) | collective-permute-done | bytes 753696 | tf_op jit(solution)/shard_map/ppermute | solution.py:311
  51.7 19.3 %all_to_all.20.r_ref = bf16[16,224,128]{2,1,0:T(8,128)(2,1)S(1)} all-to-all(bf16[16,224,128]{2,1,0:T(8,128)(2,1)S(1)} %merge.1), channel_id=1, replica_groups=mesh['ens'=8,'polar'=2,'azimuth'=16] {'azimuth'}, dimensions={0} | all-to-all | bytes 1835008 | tf_op jit(solution)/shard_map/all_to_all | solution.py:376
  71.0 2.0 %collective-permute-start.2 = (f32[144,128]{1,0:T(8,128)S(1)}, f32[144,128]{1,0:T(8,128)S(1)}, u32[]{:S(2)}, u32[]{:S(2)}) collective-permute-start(f32[144,128]{1,0:T(8,128)S(1)} %convert_reduce_fusion), channel_id=1, source_target_pairs={{0,32},{32,0},{64,96},{96,64},{128,160},{160,128},{192,224},{224,1... | collective-permute-start | bytes 221192 | tf_op jit(solution)/shard_map/ppermute | solution.py:380
  73.0 2.4 %collective-permute-done.2 = f32[144,128]{1,0:T(8,128)S(1)} collective-permute-done((f32[144,128]{1,0:T(8,128)S(1)}, f32[144,128]{1,0:T(8,128)S(1)}, u32[]{:S(2)}, u32[]{:S(2)}) %collective-permute-start.2) | collective-permute-done | bytes 73760 | tf_op jit(solution)/shard_map/ppermute | solution.py:380
  75.5 3.4 %collective-permute-start.3 = (f32[144,128]{1,0:T(8,128)S(1)}, f32[144,128]{1,0:T(8,128)S(1)}, u32[]{:S(2)}, u32[]{:S(2)}) collective-permute-start(f32[144,128]{1,0:T(8,128)S(1)} %add.15), channel_id=1, source_target_pairs={{0,64},{32,96},{64,0},{96,32},{128,192},{160,224},{192,128},{224,1... | collective-permute-start | bytes 221192 | tf_op jit(solution)/shard_map/ppermute | solution.py:380
  78.8 2.3 %collective-permute-done.3 = f32[144,128]{1,0:T(8,128)S(1)} collective-permute-done((f32[144,128]{1,0:T(8,128)S(1)}, f32[144,128]{1,0:T(8,128)S(1)}, u32[]{:S(2)}, u32[]{:S(2)}) %collective-permute-start.3) | collective-permute-done | bytes 73760 | tf_op jit(solution)/shard_map/ppermute | solution.py:380
  81.2 7.7 %collective-permute-start.4 = (f32[144,128]{1,0:T(8,128)S(1)}, f32[144,128]{1,0:T(8,128)S(1)}, u32[]{:S(2)}, u32[]{:S(2)}) collective-permute-start(f32[144,128]{1,0:T(8,128)S(1)} %add.16), channel_id=1, source_target_pairs={{0,128},{32,160},{64,192},{96,224},{128,0},{160,32},{192,64},{224,... | collective-permute-start | bytes 221192 | tf_op jit(solution)/shard_map/ppermute | solution.py:380
  88.9 1.4 %fields.1 = bf16[16,120,128]{2,1,0:T(8,128)(2,1)} custom-call(bf16[16,224,128]{2,1,0:T(8,128)(2,1)S(1)} %all_to_all.20.r_ref, bf16[2,768,384]{2,1,0:T(8,128)(2,1)S(1)} %get-tuple-element.39.w_ref, bf16[2,384,512]{2,1,0:T(8,128)(2,1)S(1)} %copy-done.1), custom_call_target="tpu_custom_call" | custom-call | flops 314572800 | bytes 1048576 | tf_op jit(solution)/shard_map/fields/pallas_call | solution.py:61
  90.3 4.8 %all-to-all-start.3 = ((bf16[16,120,128]{2,1,0:T(8,128)(2,1)}), bf16[16,120,128]{2,1,0:T(8,128)(2,1)S(1)}, u32[]{:S(2)}, u32[]{:S(2)}) async-start(bf16[16,120,128]{2,1,0:T(8,128)(2,1)} %fields.1), calls=%async_computation.3 | async-start | bytes 983040 | tf_op jit(solution)/shard_map/all_to_all | solution.py:387
  95.3 1.3 %collective-permute-done.5 = f32[144,128]{1,0:T(8,128)S(1)} collective-permute-done((f32[144,128]{1,0:T(8,128)S(1)}, f32[144,128]{1,0:T(8,128)S(1)}, u32[]{:S(2)}, u32[]{:S(2)}) %collective-permute-start.5) | collective-permute-done | bytes 73760 | tf_op jit(solution)/shard_map/ppermute | solution.py:311
  97.2 6.6 %all-to-all-done.3.r_ref = bf16[16,120,128]{2,1,0:T(8,128)(2,1)S(1)} async-done(((bf16[16,120,128]{2,1,0:T(8,128)(2,1)}), bf16[16,120,128]{2,1,0:T(8,128)(2,1)S(1)}, u32[]{:S(2)}, u32[]{:S(2)}) %all-to-all-start.3) | async-done | bytes 491552 | tf_op jit(solution)/shard_map/all_to_all | solution.py:387
  (61 shorter events, 15.4 us)
Async XLA Ops:
  0.6 10.5 %copy-start.18 = (s32[4,2]{0,1:T(2,128)S(1)}, s32[4,2]{0,1:T(2,128)}, u32[]{:S(2)}) copy-start(s32[4,2]{0,1:T(2,128)} %param.15) | copy-start | bytes 100
  0.6 1.0 copy-start.4
  2.5 8.7 %copy-start.17 = (bf16[9,4,5,720]{3,1,2,0:T(4,128)(2,1)S(1)}, bf16[9,4,5,720]{3,1,2,0:T(4,128)(2,1)}, u32[]{:S(2)}) copy-start(bf16[9,4,5,720]{3,1,2,0:T(4,128)(2,1)} %param.14) | copy-start | bytes 777604
  3.7 20.6 %all-to-all-start = ((bf16[16,120,128]{2,1,0:T(8,128)(2,1)}), bf16[16,120,128]{2,1,0:T(8,128)(2,1)S(1)}, u32[]{:S(2)}, u32[]{:S(2)}) async-start(bf16[16,120,128]{2,1,0:T(8,128)(2,1)} %pack.1), calls=%async_computation | async-start | bytes 983040 | tf_op jit(solution)/shard_map/all_to_all | solution.py:336
  14.6 3.7 %copy-start.10 = (f32[2,8,512]{2,1,0:T(8,128)S(1)}, f32[2,8,512]{2,1,0:T(8,128)}, u32[]{:S(2)}) copy-start(f32[2,8,512]{2,1,0:T(8,128)} %constant.42.clone.nu1) | copy-start | bytes 98308
  14.6 3.7 %copy-start.11 = (f32[2,8,512]{2,1,0:T(8,128)S(1)}, f32[2,8,512]{2,1,0:T(8,128)}, u32[]{:S(2)}) copy-start(f32[2,8,512]{2,1,0:T(8,128)} %constant.43.clone.nu2) | copy-start | bytes 98308
  14.6 3.7 %copy-start.12 = (f32[2,8,384]{2,1,0:T(8,128)S(1)}, f32[2,8,384]{2,1,0:T(8,128)}, u32[]{:S(2)}) copy-start(f32[2,8,384]{2,1,0:T(8,128)} %constant.38.clone.wu1) | copy-start | bytes 73732
  14.6 3.7 %copy-start.13 = (f32[2,8,384]{2,1,0:T(8,128)S(1)}, f32[2,8,384]{2,1,0:T(8,128)}, u32[]{:S(2)}) copy-start(f32[2,8,384]{2,1,0:T(8,128)} %constant.39.clone.wu2) | copy-start | bytes 73732
  15.6 2.6 %copy-start.5 = (f32[2,96,384]{2,1,0:T(8,128)S(1)}, f32[2,96,384]{2,1,0:T(8,128)}, u32[]{:S(2)}) copy-start(f32[2,96,384]{2,1,0:T(8,128)} %constant.40.clone.wf1) | copy-start | bytes 884740
  15.7 2.6 %copy-start.6 = (f32[2,96,384]{2,1,0:T(8,128)S(1)}, f32[2,96,384]{2,1,0:T(8,128)}, u32[]{:S(2)}) copy-start(f32[2,96,384]{2,1,0:T(8,128)} %constant.41.clone.wf2) | copy-start | bytes 884740
  17.2 6.0 %collective-permute-start = (bf16[9,4,5,2,12]{4,3,2,1,0:T(2,128)(2,1)}, bf16[9,4,5,2,12]{4,3,2,1,0:T(2,128)(2,1)}, u32[]{:S(2)}, u32[]{:S(2)}) collective-permute-start(bf16[9,4,5,2,12]{4,3,2,1,0:T(2,128)(2,1)} %bitcast.12), channel_id=1, source_target_pairs={{0,16},{16,0},{1,17},{17,1},{2,18},{18,2},{3,19},{19,3},{4,20},{20... | collective-permute-start | bytes 25928 | tf_op jit(solution)/shard_map/ppermute | solution.py:311
  18.3 0.9 copy-start.7
  24.3 1.1 %copy-start.3 = (bf16[2,512,384]{2,1,0:T(8,128)(2,1)S(1)}, bf16[2,512,384]{2,1,0:T(8,128)(2,1)}, u32[]{:S(2)}) copy-start(bf16[2,512,384]{2,1,0:T(8,128)(2,1)} %copy-done.2) | copy-start | bytes 2359300
  26.9 16.0 %all-to-all-start.1 = ((bf16[32,40,128]{2,1,0:T(8,128)(2,1)}), bf16[32,40,128]{2,1,0:T(8,128)(2,1)S(1)}, u32[]{:S(2)}, u32[]{:S(2)}) async-start(bf16[32,40,128]{2,1,0:T(8,128)(2,1)} %spectra.1), calls=%async_computation.1 | async-start | bytes 655360 | tf_op jit(solution)/shard_map/all_to_all | solution.py:359
  38.2 1.2 %copy-start.14 = (bf16[9,384,256]{2,1,0:T(8,128)(2,1)}, bf16[9,384,256]{2,1,0:T(8,128)(2,1)S(1)}, u32[]{:S(2)}) copy-start(bf16[9,384,256]{2,1,0:T(8,128)(2,1)S(1)} %get-tuple-element.36.at_ref) | copy-start | bytes 5308420
  42.9 1.5 %copy-start.15 = (bf16[9,384,256]{2,1,0:T(8,128)(2,1)S(1)}, bf16[9,384,256]{2,1,0:T(8,128)(2,1)}, u32[]{:S(2)}) copy-start(bf16[9,384,256]{2,1,0:T(8,128)(2,1)} %copy-done.14) | copy-start | bytes 5308420
  44.4 1.3 %copy-start.16 = (bf16[9,256,256]{2,1,0:T(8,128)(2,1)S(1)}, bf16[9,256,256]{2,1,0:T(8,128)(2,1)}, u32[]{:S(2)}) copy-start(bf16[9,256,256]{2,1,0:T(8,128)(2,1)} %w_ref.1) | copy-start | bytes 3538948
  49.0 2.5 %collective-permute-start.1 = (bf16[16,184,128]{2,1,0:T(8,128)(2,1)S(1)}, bf16[16,184,128]{2,1,0:T(8,128)(2,1)S(1)}, u32[]{:S(2)}, u32[]{:S(2)}) collective-permute-start(bf16[16,184,128]{2,1,0:T(8,128)(2,1)S(1)} %get-tuple-element.38), channel_id=1, source_target_pairs={{0,16},{16,0},{1,17},{17,1},{2,18},{18,2},{3,19},{19,3},{4,20},{20... | collective-permute-start | bytes 2261000 | tf_op jit(solution)/shard_map/ppermute | solution.py:311
  51.7 37.2 %copy-start.1 = (bf16[2,384,512]{2,1,0:T(8,128)(2,1)S(1)}, bf16[2,384,512]{2,1,0:T(8,128)(2,1)}, u32[]{:S(2)}) copy-start(bf16[2,384,512]{2,1,0:T(8,128)(2,1)} %copy-done) | copy-start | bytes 2359300
  71.0 4.4 %collective-permute-start.2 = (f32[144,128]{1,0:T(8,128)S(1)}, f32[144,128]{1,0:T(8,128)S(1)}, u32[]{:S(2)}, u32[]{:S(2)}) collective-permute-start(f32[144,128]{1,0:T(8,128)S(1)} %convert_reduce_fusion), channel_id=1, source_target_pairs={{0,32},{32,0},{64,96},{96,64},{128,160},{160,128},{192,224},{224,1... | collective-permute-start | bytes 221192 | tf_op jit(solution)/shard_map/ppermute | solution.py:380
  75.5 5.7 %collective-permute-start.3 = (f32[144,128]{1,0:T(8,128)S(1)}, f32[144,128]{1,0:T(8,128)S(1)}, u32[]{:S(2)}, u32[]{:S(2)}) collective-permute-start(f32[144,128]{1,0:T(8,128)S(1)} %add.15), channel_id=1, source_target_pairs={{0,64},{32,96},{64,0},{96,32},{128,192},{160,224},{192,128},{224,1... | collective-permute-start | bytes 221192 | tf_op jit(solution)/shard_map/ppermute | solution.py:380
  81.2 14.0 %collective-permute-start.4 = (f32[144,128]{1,0:T(8,128)S(1)}, f32[144,128]{1,0:T(8,128)S(1)}, u32[]{:S(2)}, u32[]{:S(2)}) collective-permute-start(f32[144,128]{1,0:T(8,128)S(1)} %add.16), channel_id=1, source_target_pairs={{0,128},{32,160},{64,192},{96,224},{128,0},{160,32},{192,64},{224,... | collective-permute-start | bytes 221192 | tf_op jit(solution)/shard_map/ppermute | solution.py:380
  90.3 13.5 %all-to-all-start.3 = ((bf16[16,120,128]{2,1,0:T(8,128)(2,1)}), bf16[16,120,128]{2,1,0:T(8,128)(2,1)S(1)}, u32[]{:S(2)}, u32[]{:S(2)}) async-start(bf16[16,120,128]{2,1,0:T(8,128)(2,1)} %fields.1), calls=%async_computation.3 | async-start | bytes 983040 | tf_op jit(solution)/shard_map/all_to_all | solution.py:387
  95.2 1.4 %collective-permute-start.5 = (f32[144,128]{1,0:T(8,128)S(1)}, f32[144,128]{1,0:T(8,128)S(1)}, u32[]{:S(2)}, u32[]{:S(2)}) collective-permute-start(f32[144,128]{1,0:T(8,128)S(1)} %add.17), channel_id=1, source_target_pairs={{0,16},{16,0},{1,17},{17,1},{2,18},{18,2},{3,19},{19,3},{4,20},{20... | collective-permute-start | bytes 221192 | tf_op jit(solution)/shard_map/ppermute | solution.py:311
  (4 other events, 3.6 us)

commit v2 on v1

--- a/solution.py
+++ b/solution.py
@@ -7,6 +7,7 @@
 from jax.experimental import pallas as pl
 from jax.experimental.pallas import tpu as pltpu
 from jax.sharding import PartitionSpec as P
+
 
 WIN, WOUT, MODES = 1440, 720, 360
 K, C, SUPPORT = 9, 256, 5
@@ -54,22 +55,32 @@
     return wide, narrow
 
 
-def call(body, outs, name, flops=0, scratch=(), nbytes=1 << 20, vmem=16, smem=0):
-    def run(*args):
-        places = [pl.BlockSpec(memory_space=pltpu.SMEM)] * smem
-        places += [pl.BlockSpec(memory_space=pltpu.VMEM)] * (len(args) - smem)
-        return pl.pallas_call(
-            body,
-            out_shape=[jax.ShapeDtypeStruct(s, d) for s, d in outs],
-            in_specs=places,
-            out_specs=[pl.BlockSpec(memory_space=pltpu.VMEM)] * len(outs),
-            scratch_shapes=list(scratch),
-            name=name,
-            compiler_params=pltpu.CompilerParams(vmem_limit_bytes=vmem << 20),
-            cost_estimate=pl.CostEstimate(flops=flops, bytes_accessed=nbytes, transcendentals=0),
-        )(*args)
-
-    return run
+HBM = pl.BlockSpec(memory_space=pltpu.HBM)
+VMEM = pl.BlockSpec(memory_space=pltpu.VMEM)
+SMEM = pl.BlockSpec(memory_space=pltpu.SMEM)
+
+
+def call(body, places, outs, flops=0, scratch=(), nbytes=1 << 20, vmem=16):
+    return pl.pallas_call(
+        body,
+        out_shape=[jax.ShapeDtypeStruct(s, d) for s, d in outs],
+        in_specs=places,
+        out_specs=[VMEM] * len(outs),
+        scratch_shapes=list(scratch),
+        compiler_params=pltpu.CompilerParams(vmem_limit_bytes=vmem << 20),
+        cost_estimate=pl.CostEstimate(flops=flops, bytes_accessed=nbytes, transcendentals=0),
+    )
+
+
+def in_hbm(value):
+    return pltpu.with_memory_space_constraint(value, pltpu.HBM)
+
+
+def fetch(sources, targets, sems):
+    copies = [pltpu.make_async_copy(s, t, sems.at[n]) for n, (s, t) in enumerate(zip(sources, targets))]
+    for copy in copies:
+        copy.start()
+    return copies
 
 
 def low_half(shape):
@@ -98,7 +109,9 @@
     return 48 * (column % 4) + column // 4
 
 
-def pack_body(f_ref, g_ref, o_ref, flat_ref):
+def pack_body(f_hbm, g_hbm, o_ref, f_ref, g_ref, flat_ref, sems):
+    copies = fetch((f_hbm, g_hbm), (f_ref, g_ref), sems)
+    copies[0].wait()
     for j in range(6):
         count = min(128, 8 * WPART - 128 * j)
         order = one_hot((128, count), row_of_latitude)
@@ -107,6 +120,7 @@
             for h in range(2):
                 piece = block[16 * r : 16 * (r + 1), 128 * h : 128 * (h + 1)]
                 o_ref[2 * r + h, 16 * j : 16 * (j + 1), :] = piece
+    copies[1].wait()
     for v in range(VPART):
         flat_ref[4 * v : 4 * (v + 1), :] = g_ref[v].astype(F32)
     flat_ref[4 * VPART : 192, :] = jnp.zeros((192 - 4 * VPART, C), F32)
@@ -129,18 +143,35 @@
             target[128 * j : 128 * (j + 1), 128 * i : 128 * (i + 1)] = piece.T.astype(BF16)
 
 
-def table_body(wu1, wu2, wf1, wf2, nu1, nu2, nf1, nf2, w_ref, wt_ref, v_ref, vt_ref):
+def fill_tables(w, v, w_ref, v_ref):
     for e in range(BANDS):
         for b in range(HALF):
-            one, two = wu1[e, b : b + 1, :], wu2[e, b : b + 1, :]
-            block = one * wf1[e] + two * wf2[e]
+            one, two = w[0][e, b : b + 1, :], w[1][e, b : b + 1, :]
+            block = one * w[2][e] + two * w[3][e]
             w_ref[e, WROWS * b : WROWS * (b + 1), :] = block.astype(BF16)
-            one, two = nu1[e, b : b + 1, :], nu2[e, b : b + 1, :]
+            one, two = v[0][e, b : b + 1, :], v[1][e, b : b + 1, :]
             for part in range(2):
                 rows = slice(VROWS * part, VROWS * (part + 1))
-                block = one * nf1[e, rows, :] + two * nf2[e, rows, :]
+                block = one * v[2][e, rows, :] + two * v[3][e, rows, :]
                 start = VROWS * (HALF * part + b)
                 v_ref[e, start : start + VROWS, :] = block.astype(BF16)
+
+
+def table_body(*refs):
+    factors, (w_ref, v_ref) = refs[:8], refs[8:10]
+    held, sems = refs[10:18], refs[18]
+    for copy in fetch(factors, held, sems):
+        copy.wait()
+    fill_tables(held[:4], held[4:], w_ref, v_ref)
+
+
+def flipped_table_body(*refs):
+    factors, (wt_ref, vt_ref) = refs[:8], refs[8:10]
+    held, (w_ref, v_ref, sems) = refs[10:18], refs[18:]
+    for copy in fetch(factors, held, sems):
+        copy.wait()
+    fill_tables(held[:4], held[4:], w_ref, v_ref)
+    for e in range(BANDS):
         flip(w_ref.at[e], wt_ref.at[e], HALF * WROWS, 2 * LANES * M12)
         flip(v_ref.at[e], vt_ref.at[e], 2 * HALF * VROWS, 2 * LANES * M16)
 
@@ -164,15 +195,60 @@
         o_ref[shares, 0:M16, :] = out.astype(BF16).reshape(LANES, M16, 128)
 
 
-def mixing_body(b_ref, a_ref, at_ref, p_ref):
-    rows, width = K * 16, HIN * 2 * M12
-    row = lax.broadcasted_iota(jnp.int32, (120, width), 0)
-    lane = lax.broadcasted_iota(jnp.int32, (120, width), 1)
-    owner = (lax.broadcasted_iota(jnp.int32, (rows, width), 0) // 2) % HOUT
+def filter_body(spot_ref, support_ref, p_hbm, mine_ref, other_ref, p_ref, flat_ref, sems):
+    (copy,) = fetch((p_hbm,), (p_ref,), sems)
+    rows = K * SUPPORT * 4
+    band, start = spot_ref[0, 0], 2 * M12 * spot_ref[0, 1]
+    line = lax.broadcasted_iota(jnp.int32, (WOUT, 128), 0)
+    slot = lax.broadcasted_iota(jnp.int32, (WOUT, 128), 1)
+    place = slot % 64
+    parity = jnp.where(slot < 64, band, 1 - band)
+    mode = start + 2 * (place % M12) + parity
+    hit = (line == mode + MODES * (place // M12)) & (place < 2 * M12) & (mode < MODES)
+    chosen = jnp.where(hit, 1.0, 0.0).astype(BF16)
+    row = lax.broadcasted_iota(jnp.int32, (rows, 128), 0)
+    window, output = (row // 4) % SUPPORT, row % 4
+    first = jnp.zeros((rows, 128), jnp.int32)
+    last = jnp.zeros((rows, 128), jnp.int32)
+    for o in range(4):
+        first = jnp.where(output == o, support_ref[o, 0], first)
+        last = jnp.where(output == o, support_ref[o, 1], last)
+    copy.wait()
+    for n in range(K * SUPPORT):
+        flat_ref[4 * n : 4 * (n + 1), :] = p_ref[n].astype(F32)
+    got = dot(flat_ref[0:rows, :].astype(BF16), chosen)
+    got = jnp.where((window >= first) & (window <= last), got, 0.0)
+    mine_ref[...] = got.astype(BF16)
+    other_ref[...] = swap64(got).astype(BF16)
+
+
+def mixing_body(spot_ref, mine_ref, got_ref, a_ref, at_ref, p_ref):
+    rows, width, count = K * 16, HIN * 2 * M12, K * SUPPORT * 4
+    low = spot_ref[0, 0] == 0
+    mine, got = mine_ref[...].astype(F32), got_ref[...].astype(F32)
+    halves = (jnp.where(low, mine, got).astype(BF16), jnp.where(low, got, mine).astype(BF16))
+    x = lax.broadcasted_iota(jnp.int32, (128, width), 0)
+    lane = lax.broadcasted_iota(jnp.int32, (128, width), 1)
+    same, cross = lane % M12, lane % (2 * M12) < M12
+    straight = x == same + jnp.where(cross, 0, M12)
+    turned = x == same + jnp.where(cross, M12, 0)
+    tiles = (
+        jnp.where(straight, jnp.where(cross, 1.0, -1.0), 0.0).astype(BF16),
+        jnp.where(turned, 1.0, 0.0).astype(BF16),
+    )
+    row = lax.broadcasted_iota(jnp.int32, (count, width), 0)
+    lane = lax.broadcasted_iota(jnp.int32, (count, width), 1)
+    reach = 2 * (row % 4) + (row // 4) % SUPPORT - 2 - lane // (2 * M12)
+    target = lax.broadcasted_iota(jnp.int32, (rows, count), 0)
+    source = lax.broadcasted_iota(jnp.int32, (rows, count), 1)
+    key = target - 16 * (source // 20) - 2 * (source % 4)
     total = jnp.zeros((rows, width), F32)
-    for o in range(HOUT):
-        shift = jnp.where(lane - row == 48 * (o - 1), 1.0, 0.0).astype(BF16)
-        total = jnp.where(owner == o, dot(b_ref[...], shift), total)
+    for half in range(2):
+        for ri in range(2):
+            spread = dot(halves[half], tiles[ri])
+            spread = jnp.where(reach == -8 * half, spread, 0.0).astype(BF16)
+            collect = jnp.where(key == 8 * half + ri, 1.0, 0.0).astype(BF16)
+            total = total + dot(collect, spread)
     p_ref[...] = total
     mode = lax.broadcasted_iota(jnp.int32, (M16, width), 1) % M12
     same = lax.broadcasted_iota(jnp.int32, (M16, width), 0) == mode
@@ -189,7 +265,13 @@
         at_ref[k] = jnp.where(left == right, grown, 0.0).astype(BF16)
 
 
-def middle_body(band_ref, r_ref, a_ref, at_ref, w_ref, mine_ref, other_ref, gs_ref, out_ref, sg_ref):
+def middle_body(
+    band_ref, r_ref, a_hbm, at_hbm, w_hbm, mine_ref, other_ref, gs_ref, out_ref, sg_ref, a_ref, at_ref, w_ref, sems
+):
+    copies = [
+        fetch((a_hbm.at[k], w_hbm.at[k], at_hbm.at[k]), (a_ref.at[k], w_ref.at[k], at_ref.at[k]), sems.at[k])
+        for k in range(K)
+    ]
     keep = low_half((M16, 128))
     for o in range(HOUT):
         for i in range(2):
@@ -206,6 +288,8 @@
     low = band_ref[0, 0] == 0
 
     for k in range(K):
+        for copy in copies[k]:
+            copy.wait()
         mixed = dot(a_ref[k], x).astype(BF16)
         out_now = dot(mixed, w_ref[k])
         grad = lax.dot_general(mixed, gs, (((0,), (0,)), ((), ())), preferred_element_type=F32)
@@ -301,96 +385,108 @@
         c_ref[v] = rows[4 * v : 4 * (v + 1), :].astype(BF16)
 
 
-def mask_filters(filters, support):
-    window = jnp.arange(filters.shape[2], dtype=jnp.int32)
-    inside = (window[None, :] >= support[:, 0:1]) & (window[None, :] <= support[:, 1:2])
-    return jnp.where(inside[None, :, :, None], filters, jnp.zeros_like(filters))
-
-
 def swap_bands(value):
     return lax.ppermute(value, "polar", [(0, 1), (1, 0)])
 
 
-def filter_rows(basis_spectra, support, low):
-    masked = mask_filters(basis_spectra, support)
-    pairs = masked.reshape(K, HOUT // BANDS, SUPPORT, 2, MODES)
-    pairs = jnp.pad(pairs, [(0, 0)] * 4 + [(0, SHARES * M12 - MODES)])
-    start = lax.axis_index("azimuth") * 2 * M12
-    here = lax.dynamic_slice_in_dim(pairs, start, 2 * M12, 4).reshape(pairs.shape[:4] + (M12, 2))
-    mine = jnp.where(low, here[..., 0], here[..., 1])
-    got = swap_bands(jnp.where(low, here[..., 1], here[..., 0]))
-    here = jnp.concatenate([jnp.where(low, mine, got), jnp.where(low, got, mine)], axis=1)
-    re, im = here[:, :, :, 0], here[:, :, :, 1]
-    rows = jnp.stack([jnp.stack([re, -im], axis=3), jnp.stack([im, re], axis=3)], axis=2)
-    return rows.reshape(K * HOUT * 2, SUPPORT * 2 * M12)
-
-
 def local(fields, basis_spectra, support, weights, out_grad):
-    band = lax.axis_index("polar")
+    band = lax.axis_index("polar").astype(jnp.int32)
     low = band == 0
-    spot = band.astype(jnp.int32).reshape(1, 1)
+    spot = jnp.stack([band, lax.axis_index("azimuth").astype(jnp.int32)]).reshape(1, 2)
     wide, narrow = factor_tables()
+    dma = pltpu.SemaphoreType.DMA
     (sent,) = call(
-        pack_body, [((LANES, CHUNK_IN, 128), BF16)], "pack", scratch=[pltpu.VMEM((192, C), F32)], vmem=8
-    )(jnp.swapaxes(fields[0], 0, 1).reshape(8 * WPART, C), jnp.swapaxes(out_grad[0], 0, 1))
+        pack_body,
+        [HBM, HBM],
+        [((LANES, CHUNK_IN, 128), BF16)],
+        scratch=[
+            pltpu.VMEM((8 * WPART, C), BF16),
+            pltpu.VMEM((VPART, 4, C), BF16),
+            pltpu.VMEM((192, C), F32),
+            dma((2,)),
+        ],
+    )(
+        in_hbm(jnp.swapaxes(fields[0], 0, 1).reshape(8 * WPART, C)), in_hbm(jnp.swapaxes(out_grad[0], 0, 1))
+    )
     landed = lax.all_to_all(sent, "azimuth", split_axis=0, concat_axis=0, tiled=True)
 
     filters, limits, sent = lax.optimization_barrier((basis_spectra, support, sent))
-    rows = filter_rows(filters, limits, low)
-    tables = [jnp.asarray(a) for a in wide + narrow]
-    tables, sent = lax.optimization_barrier((tables, sent))
-    tall, flat, inv, inv_t = call(
-        table_body,
-        [((2, 768, 384), BF16), ((2, 384, 768), BF16), ((2, 384, 512), BF16), ((2, 512, 384), BF16)],
-        "tables",
+    mine, other = call(
+        filter_body,
+        [SMEM, SMEM, HBM],
+        [((K * SUPPORT * 4, 128), BF16)] * 2,
+        scratch=[pltpu.VMEM((K * SUPPORT, 4, WOUT), BF16), pltpu.VMEM((184, WOUT), F32), dma((1,))],
+    )(spot, limits, in_hbm(jnp.swapaxes(filters, 1, 2).reshape(K * SUPPORT, 4, WOUT)))
+    got = swap_bands(other)
+    factors = [a for a in wide + narrow]
+    held = [pltpu.VMEM(a.shape, F32) for a in factors]
+    factors, sent = lax.optimization_barrier(([jnp.asarray(a) for a in factors], sent))
+    flat, inv_t = call(
+        flipped_table_body,
+        [HBM] * 8,
+        [((2, 384, 768), BF16), ((2, 512, 384), BF16)],
         nbytes=5 << 20,
-    )(*tables)
+        scratch=held + [pltpu.VMEM((2, 768, 384), BF16), pltpu.VMEM((2, 384, 512), BF16), dma((8,))],
+    )(*[in_hbm(a) for a in factors])
+
+    landed, mine, got = lax.optimization_barrier((landed, mine, got))
+    (sent,) = call(spectra_body, [VMEM] * 3, [((SHARES, CHUNK_MID, 128), BF16)], flops=300 << 20)(landed, flat, inv_t)
+    landed = lax.all_to_all(sent, JOINT, split_axis=0, concat_axis=0, tiled=True)
+    mine, got, sent = lax.optimization_barrier((mine, got, sent))
     mix, mix_t = call(
         mixing_body,
+        [SMEM, VMEM, VMEM],
         [((K, 256, 384), BF16), ((K, 384, 256), BF16)],
-        "mixing",
         scratch=[pltpu.VMEM((K * 16, 384), F32)],
         nbytes=4 << 20,
-    )(rows)
-
-    (sent,) = call(spectra_body, [((SHARES, CHUNK_MID, 128), BF16)], "spectra", flops=300 << 20)(
-        landed, flat, inv_t
-    )
-    landed = lax.all_to_all(sent, JOINT, split_axis=0, concat_axis=0, tiled=True)
+    )(spot, mine, got)
 
     chunk = (LANES, CHUNK_MID + 16 * K, 128)
     mine, other = call(
         middle_body,
+        [SMEM, VMEM, HBM, HBM, HBM],
         [(chunk, BF16), (chunk, BF16)],
-        "middle",
         flops=2 << 30,
         nbytes=6 << 20,
-        scratch=[pltpu.VMEM((256, 256), BF16), pltpu.VMEM((256, 256), F32), pltpu.VMEM((384, 256), F32)],
-        smem=1,
-        vmem=24,
-    )(spot, landed.reshape(HIN, 2, CHUNK_MID, 128), mix, mix_t, weights)
+        scratch=[
+            pltpu.VMEM((256, 256), BF16),
+            pltpu.VMEM((256, 256), F32),
+            pltpu.VMEM((384, 256), F32),
+            pltpu.VMEM((K, 256, 384), BF16),
+            pltpu.VMEM((K, 384, 256), BF16),
+            pltpu.VMEM((K, 256, 256), BF16),
+            dma((K, 3)),
+        ],
+        vmem=32,
+    )(spot, landed.reshape(HIN, 2, CHUNK_MID, 128), in_hbm(mix), in_hbm(mix_t), in_hbm(weights))
     got = swap_bands(other)
-    (sent,) = call(merge_body, [((LANES, CHUNK_OUT, 128), BF16)], "merge", nbytes=2 << 20, smem=1, vmem=8)(
-        spot, mine, got
-    )
+    (sent,) = call(merge_body, [SMEM, VMEM, VMEM], [((LANES, CHUNK_OUT, 128), BF16)], nbytes=2 << 20)(spot, mine, got)
     landed = lax.all_to_all(sent, "azimuth", split_axis=0, concat_axis=0, tiled=True)
 
+    factors, sent = lax.optimization_barrier((factors, sent))
+    tall, inv = call(
+        table_body,
+        [HBM] * 8,
+        [((2, 768, 384), BF16), ((2, 384, 512), BF16)],
+        nbytes=5 << 20,
+        scratch=held + [dma((8,))],
+    )(*[in_hbm(a) for a in factors])
+
+    landed, tall, inv = lax.optimization_barrier((landed, tall, inv))
+
+    def exchange(value, step):
+        return value + lax.ppermute(value, "ens", [(i, i ^ step) for i in range(lax.axis_size("ens"))])
+
     half = jnp.sum(landed[:, 2 * CHUNK_MID :, :].astype(F32), axis=0)
-    for step in (1, 2, 4):
-        half = half + lax.ppermute(half, "ens", [(i, i ^ step) for i in range(lax.axis_size("ens"))])
+    half = exchange(half, 1)
+    half = exchange(half, 2)
+    half = exchange(half, 4)
     far = swap_bands(half)
+    (sent,) = call(fields_body, [VMEM] * 3, [((LANES, CHUNK_IN, 128), BF16)], flops=300 << 20)(landed, tall, inv)
+    landed = lax.all_to_all(sent, "azimuth", split_axis=0, concat_axis=0, tiled=True)
     weight_grad = jnp.concatenate([jnp.where(low, half, far), jnp.where(low, far, half)], axis=1)
-
-    (sent,) = call(fields_body, [((LANES, CHUNK_IN, 128), BF16)], "fields", flops=300 << 20)(
-        landed, tall, inv
-    )
-    landed = lax.all_to_all(sent, "azimuth", split_axis=0, concat_axis=0, tiled=True)
     field_grad, conv_out = call(
-        unpack_body,
-        [((8 * WPART, C), BF16), ((VPART, 4, C), BF16)],
-        "unpack",
-        scratch=[pltpu.VMEM((192, C), F32)],
-        vmem=8,
+        unpack_body, [VMEM], [((8 * WPART, C), BF16), ((VPART, 4, C), BF16)], scratch=[pltpu.VMEM((192, C), F32)]
     )(landed)
     field_grad = jnp.swapaxes(field_grad.reshape(WPART, 8, C), 0, 1)
     return (jnp.swapaxes(conv_out, 0, 1)[None], field_grad[None], weight_grad.reshape(K, 16, C))

time: 106 us -> 101 us (0.953)
  blocking collectives: 19.3 us -> 0 us
  waiting for transfers between devices: 18.3 us -> 37.1 us
  local copies, waits for them, and re-layouts: 17.3 us -> 2.56 us
  Pallas kernels: 11.2 us -> 23.7 us
  other arithmetic: 4.7 us -> 0.88 us
  starting transfers between devices: 33.2 us -> 35.9 us
    all_to_all x1 -> x0, blocking collectives: 19.3 us -> none  [local(): lax.all_to_all(sent, 'azimuth', split_axis=0, concat_axis=0, tiled=True)]
    all_to_all x2 -> x3, waiting for transfers between devices: 6.63 us -> 24.9 us  [local(): lax.all_to_all(sent, 'azimuth', split_axis=0, concat_axis=0, tiled=True)]
    pallas_call x8 -> x10, Pallas kernels: 11.2 us -> 23.7 us  [the longest x1 7.21 us: local(): call(middle_body, [SMEM, VMEM, HBM, HBM, HBM], [(chunk, BF16), (chunk, BF...]
    unnamed x38 -> x6, local copies, waits for them, and re-layouts: 10.6 us -> 2.47 us
    all_to_all x2 -> x3, starting transfers between devices: 12.3 us -> 17.6 us  [local(): lax.all_to_all(sent, 'azimuth', split_axis=0, concat_axis=0, tiled=True)]
    reshape x2 -> x0, local copies, waits for them, and re-layouts: 3.38 us -> none  [the longest x1 3.16 us: filter_rows(): pairs = masked.reshape(K, HOUT // BANDS, SUPPORT, 2, MODES)]
    all_to_all x1, starting transfers between devices: 7.48 us -> 4.99 us  [local(): lax.all_to_all(sent, JOINT, split_axis=0, concat_axis=0, tiled=True)]
    select_n x2 -> x0, local copies, waits for them, and re-layouts: 1.98 us -> none  [the longest x1 0.99 us: filter_rows(): got = swap_bands(jnp.where(low, here[..., 1], here[..., 0]))]
  transfers between devices with their start and end apart: 9 -> 10, of which waited for: 6 -> 8; matrix products, arithmetic and copies ran while one was open for 11% -> 1% of each run, Pallas kernels for 4% -> 10%
where the time goes in v2:
time: 101 us
  waiting for transfers between devices  37.1 us (37%)
  starting transfers between devices  35.9 us (36%)
  Pallas kernels  23.7 us (23%)
  local copies, waits for them, and re-layouts  2.56 us (3%)
    all_to_all x3, waiting for transfers between devices, local(): lax.all_to_all(sent, 'azimuth', split_axis=0, concat_axis=0, tiled=True)  24.9 us
    all_to_all x3, starting transfers between devices, local(): lax.all_to_all(sent, 'azimuth', split_axis=0, concat_axis=0, tiled=True)  17.6 us
    ppermute x3, starting transfers between devices, exchange(): lax.ppermute(value, 'ens', [(i, i ^ step) for i in range(lax.axis_size('e...  13.1 us
    pallas_call x1, Pallas kernels, local(): call(middle_body, [SMEM, VMEM, HBM, HBM, HBM], [(chunk, BF16), (chunk, BF...  7.21 us
    all_to_all x1, starting transfers between devices, local(): lax.all_to_all(sent, JOINT, split_axis=0, concat_axis=0, tiled=True)  4.99 us
    ppermute x3, waiting for transfers between devices, exchange(): lax.ppermute(value, 'ens', [(i, i ^ step) for i in range(lax.axis_size('e...  4.78 us
    all_to_all x1, waiting for transfers between devices, local(): lax.all_to_all(sent, JOINT, split_axis=0, concat_axis=0, tiled=True)  3.93 us
    ppermute x3, waiting for transfers between devices, swap_bands(): return lax.ppermute(value, 'polar', [(0, 1), (1, 0)])  3.47 us
  transfers between devices with their start and end apart: 10, of which 8 were waited for; matrix products, arithmetic and copies ran while one was open for 1% of the time, Pallas kernels for 10%

profile of v2, /device:TPU:2, one launch (start us, length us, event | category | flops | bytes accessed | tf_op | source)
XLA Modules:
  0.0 100.9 jit_solution(9382678025938408565)
XLA Ops:
  0.6 2.3 %shard_map.148 = bf16[16,120,128]{2,1,0:T(8,128)(2,1)} custom-call(bf16[720,256]{1,0:T(8,128)(2,1)} %bitcast.26, bf16[45,4,256]{2,1,0:T(4,128)(2,1)} %bitcast.29), custom_call_target="tpu_custom_call" | custom-call | bytes 1048576 | tf_op jit(solution)/shard_map/pallas_call | solution.py:398
  3.0 7.5 %all-to-all-start = ((bf16[16,120,128]{2,1,0:T(8,128)(2,1)}), bf16[16,120,128]{2,1,0:T(8,128)(2,1)S(1)}, u32[]{:S(2)}, u32[]{:S(2)}) async-start(bf16[16,120,128]{2,1,0:T(8,128)(2,1)} %shard_map.148), calls=%async_computation | async-start | bytes 983040 | tf_op jit(solution)/shard_map/all_to_all | solution.py:411
  10.6 1.9 %shard_map.149 = (bf16[180,128]{1,0:T(8,128)(2,1)S(1)}, bf16[180,128]{1,0:T(8,128)(2,1)S(1)}) custom-call(s32[1,2]{1,0:T(1,128)S(1)} %add_bitcast_fusion.spot_ref.band_ref, s32[4,2]{1,0:T(4,128)S(1)} %copy.16.support_ref, bf16[45,4,720]{2,1,0:T(4,128)(2,1)} %bitcast.27), custom_call_target="tpu_custom_call" | custom-call | bytes 1048576 | tf_op jit(solution)/shard_map/pallas_call | solution.py:414
  12.6 2.6 %shard_map.150 = (bf16[2,384,768]{2,1,0:T(8,128)(2,1)S(1)}, bf16[2,512,384]{2,1,0:T(8,128)(2,1)S(1)}) custom-call(f32[2,8,384]{2,1,0:T(8,128)} %constant.29.clone.refs_0_, f32[2,8,384]{2,1,0:T(8,128)} %constant.30.clone.refs_1_, f32[2,96,384]{2,1,0:T(8,128)} %constant.31.clone.refs_2_, f32[2,96,384]{2,1,0:T(8,128)} %constant.32.clone.refs_3_, ...), custom_call_target="tpu_custom_call" | custom-call | bytes 5242880 | tf_op jit(solution)/shard_map/pallas_call | solution.py:424
  15.2 5.1 %all-to-all-done.r_ref = bf16[16,120,128]{2,1,0:T(8,128)(2,1)S(1)} async-done(((bf16[16,120,128]{2,1,0:T(8,128)(2,1)}), bf16[16,120,128]{2,1,0:T(8,128)(2,1)S(1)}, u32[]{:S(2)}, u32[]{:S(2)}) %all-to-all-start) | async-done | bytes 491552 | tf_op jit(solution)/shard_map/all_to_all | solution.py:411
  20.3 1.5 %shard_map.151 = bf16[32,40,128]{2,1,0:T(8,128)(2,1)} custom-call(bf16[16,120,128]{2,1,0:T(8,128)(2,1)S(1)} %all-to-all-done.r_ref, bf16[2,384,768]{2,1,0:T(8,128)(2,1)S(1)} %get-tuple-element.54.wt_ref, bf16[2,512,384]{2,1,0:T(8,128)(2,1)S(1)} %get-tuple-element.55.vt_ref), custom_call_target="tpu_custom_call" | custom-call | flops 314572800 | bytes 1048576 | tf_op jit(solution)/shard_map/pallas_call | solution.py:433
  21.7 5.0 %all-to-all-start.1 = ((bf16[32,40,128]{2,1,0:T(8,128)(2,1)}), bf16[32,40,128]{2,1,0:T(8,128)(2,1)S(1)}, u32[]{:S(2)}, u32[]{:S(2)}) async-start(bf16[32,40,128]{2,1,0:T(8,128)(2,1)} %shard_map.151), calls=%async_computation.1 | async-start | bytes 655360 | tf_op jit(solution)/shard_map/all_to_all | solution.py:434
  26.7 2.2 %shard_map.152 = (bf16[9,256,384]{2,1,0:T(8,128)(2,1)S(1)}, bf16[9,384,256]{2,1,0:T(8,128)(2,1)S(1)}) custom-call(s32[1,2]{1,0:T(1,128)S(1)} %add_bitcast_fusion.spot_ref.band_ref, bf16[180,128]{1,0:T(8,128)(2,1)S(1)} %get-tuple-element.58.mine_ref, bf16[180,128]{1,0:T(8,128)(2,1)S(1)} %collective-permute-done.got_ref), custom_call_target="tpu_custom_call" | custom-call | bytes 4194304 | tf_op jit(solution)/shard_map/pallas_call | solution.py:436
  31.4 3.9 %all-to-all-done.1 = bf16[32,40,128]{2,1,0:T(8,128)(2,1)S(1)} async-done(((bf16[32,40,128]{2,1,0:T(8,128)(2,1)}), bf16[32,40,128]{2,1,0:T(8,128)(2,1)S(1)}, u32[]{:S(2)}, u32[]{:S(2)}) %all-to-all-start.1) | async-done | bytes 327712 | tf_op jit(solution)/shard_map/all_to_all | solution.py:434
  35.4 7.2 %shard_map.153 = (bf16[16,184,128]{2,1,0:T(8,128)(2,1)S(1)}, bf16[16,184,128]{2,1,0:T(8,128)(2,1)S(1)}) custom-call(s32[1,2]{1,0:T(1,128)S(1)} %add_bitcast_fusion.spot_ref.band_ref, bf16[16,2,40,128]{3,2,1,0:T(8,128)(2,1)S(1)} %bitcast.25, bf16[9,256,384]{2,1,0:T(8,128)(2,1)} %copy-done, bf16[9,384,256]{2,1,0:T(8,128)(2,1)} %copy-done.1, ...), custom_call_target="tpu_custom_call" | custom-call | flops 2147483648 | bytes 6291456 | tf_op jit(solution)/shard_map/pallas_call | solution.py:445
  42.7 2.2 %collective-permute-done.1.got_ref = bf16[16,184,128]{2,1,0:T(8,128)(2,1)S(1)} collective-permute-done((bf16[16,184,128]{2,1,0:T(8,128)(2,1)S(1)}, bf16[16,184,128]{2,1,0:T(8,128)(2,1)S(1)}, u32[]{:S(2)}, u32[]{:S(2)}) %collective-permute-start.1) | collective-permute-done | bytes 753696 | tf_op jit(solution)/shard_map/ppermute | solution.py:389
  44.9 1.7 %shard_map.154 = bf16[16,224,128]{2,1,0:T(8,128)(2,1)} custom-call(s32[1,2]{1,0:T(1,128)S(1)} %add_bitcast_fusion.spot_ref.band_ref, bf16[16,184,128]{2,1,0:T(8,128)(2,1)S(1)} %get-tuple-element.62.mine_ref, bf16[16,184,128]{2,1,0:T(8,128)(2,1)S(1)} %collective-permute-done.1.got_ref), custom_call_target="tpu_custom_call" | custom-call | bytes 2097152 | tf_op jit(solution)/shard_map/pallas_call | solution.py:463
  46.6 5.0 %all-to-all-start.2 = ((bf16[16,224,128]{2,1,0:T(8,128)(2,1)}), bf16[16,224,128]{2,1,0:T(8,128)(2,1)S(1)}, u32[]{:S(2)}, u32[]{:S(2)}) async-start(bf16[16,224,128]{2,1,0:T(8,128)(2,1)} %shard_map.154), calls=%async_computation.2 | async-start | bytes 1835008 | tf_op jit(solution)/shard_map/all_to_all | solution.py:464
  51.6 1.8 %shard_map.155 = (bf16[2,768,384]{2,1,0:T(8,128)(2,1)S(1)}, bf16[2,384,512]{2,1,0:T(8,128)(2,1)S(1)}) custom-call(f32[2,8,384]{2,1,0:T(8,128)} %constant.29.clone.refs_0_, f32[2,8,384]{2,1,0:T(8,128)} %constant.30.clone.refs_1_, f32[2,96,384]{2,1,0:T(8,128)} %constant.31.clone.refs_2_, f32[2,96,384]{2,1,0:T(8,128)} %constant.32.clone.refs_3_, ...), custom_call_target="tpu_custom_call" | custom-call | bytes 5242880 | tf_op jit(solution)/shard_map/pallas_call | solution.py:467
  53.4 13.3 %all-to-all-done.2.r_ref = bf16[16,224,128]{2,1,0:T(8,128)(2,1)S(1)} async-done(((bf16[16,224,128]{2,1,0:T(8,128)(2,1)}), bf16[16,224,128]{2,1,0:T(8,128)(2,1)S(1)}, u32[]{:S(2)}, u32[]{:S(2)}) %all-to-all-start.2) | async-done | bytes 917536 | tf_op jit(solution)/shard_map/all_to_all | solution.py:464
  66.8 2.0 %collective-permute-start.2 = (f32[144,128]{1,0:T(8,128)S(1)}, f32[144,128]{1,0:T(8,128)S(1)}, u32[]{:S(2)}, u32[]{:S(2)}) collective-permute-start(f32[144,128]{1,0:T(8,128)S(1)} %convert_reduce_fusion), channel_id=1, source_target_pairs={{0,32},{32,0},{64,96},{96,64},{128,160},{160,128},{192,224},{224,1... | collective-permute-start | bytes 221192 | tf_op jit(solution)/shard_map/ppermute | solution.py:478
  68.7 2.4 %collective-permute-done.2 = f32[144,128]{1,0:T(8,128)S(1)} collective-permute-done((f32[144,128]{1,0:T(8,128)S(1)}, f32[144,128]{1,0:T(8,128)S(1)}, u32[]{:S(2)}, u32[]{:S(2)}) %collective-permute-start.2) | collective-permute-done | bytes 73760 | tf_op jit(solution)/shard_map/ppermute | solution.py:478
  71.2 3.4 %collective-permute-start.3 = (f32[144,128]{1,0:T(8,128)S(1)}, f32[144,128]{1,0:T(8,128)S(1)}, u32[]{:S(2)}, u32[]{:S(2)}) collective-permute-start(f32[144,128]{1,0:T(8,128)S(1)} %add.9), channel_id=1, source_target_pairs={{0,64},{32,96},{64,0},{96,32},{128,192},{160,224},{192,128},{224,1... | collective-permute-start | bytes 221192 | tf_op jit(solution)/shard_map/ppermute | solution.py:478
  74.6 2.3 %collective-permute-done.3 = f32[144,128]{1,0:T(8,128)S(1)} collective-permute-done((f32[144,128]{1,0:T(8,128)S(1)}, f32[144,128]{1,0:T(8,128)S(1)}, u32[]{:S(2)}, u32[]{:S(2)}) %collective-permute-start.3) | collective-permute-done | bytes 73760 | tf_op jit(solution)/shard_map/ppermute | solution.py:478
  76.9 7.7 %collective-permute-start.4 = (f32[144,128]{1,0:T(8,128)S(1)}, f32[144,128]{1,0:T(8,128)S(1)}, u32[]{:S(2)}, u32[]{:S(2)}) collective-permute-start(f32[144,128]{1,0:T(8,128)S(1)} %add.10), channel_id=1, source_target_pairs={{0,128},{32,160},{64,192},{96,224},{128,0},{160,32},{192,64},{224,... | collective-permute-start | bytes 221192 | tf_op jit(solution)/shard_map/ppermute | solution.py:478
  84.6 1.4 %shard_map.156 = bf16[16,120,128]{2,1,0:T(8,128)(2,1)} custom-call(bf16[16,224,128]{2,1,0:T(8,128)(2,1)S(1)} %all-to-all-done.2.r_ref, bf16[2,768,384]{2,1,0:T(8,128)(2,1)S(1)} %get-tuple-element.75.w_ref, bf16[2,384,512]{2,1,0:T(8,128)(2,1)S(1)} %get-tuple-element.76.v_ref), custom_call_target="tpu_custom_call" | custom-call | flops 314572800 | bytes 1048576 | tf_op jit(solution)/shard_map/pallas_call | solution.py:485
  86.1 5.1 %all-to-all-start.3 = ((bf16[16,120,128]{2,1,0:T(8,128)(2,1)}), bf16[16,120,128]{2,1,0:T(8,128)(2,1)S(1)}, u32[]{:S(2)}, u32[]{:S(2)}) async-start(bf16[16,120,128]{2,1,0:T(8,128)(2,1)} %shard_map.156), calls=%async_computation.3 | async-start | bytes 983040 | tf_op jit(solution)/shard_map/all_to_all | solution.py:486
  91.3 1.2 %collective-permute-done.5 = f32[144,128]{1,0:T(8,128)S(1)} collective-permute-done((f32[144,128]{1,0:T(8,128)S(1)}, f32[144,128]{1,0:T(8,128)S(1)}, u32[]{:S(2)}, u32[]{:S(2)}) %collective-permute-start.5) | collective-permute-done | bytes 73760 | tf_op jit(solution)/shard_map/ppermute | solution.py:389
  93.3 6.5 %all-to-all-done.3.r_ref = bf16[16,120,128]{2,1,0:T(8,128)(2,1)S(1)} async-done(((bf16[16,120,128]{2,1,0:T(8,128)(2,1)}), bf16[16,120,128]{2,1,0:T(8,128)(2,1)S(1)}, u32[]{:S(2)}, u32[]{:S(2)}) %all-to-all-start.3) | async-done | bytes 491552 | tf_op jit(solution)/shard_map/all_to_all | solution.py:486
  (20 shorter events, 4.8 us)
Async XLA Ops:
  0.6 9.8 %copy-start.2 = (s32[4,2]{0,1:T(2,128)S(1)}, s32[4,2]{0,1:T(2,128)}, u32[]{:S(2)}) copy-start(s32[4,2]{0,1:T(2,128)} %param.15) | copy-start | bytes 100
  3.0 17.3 %all-to-all-start = ((bf16[16,120,128]{2,1,0:T(8,128)(2,1)}), bf16[16,120,128]{2,1,0:T(8,128)(2,1)S(1)}, u32[]{:S(2)}, u32[]{:S(2)}) async-start(bf16[16,120,128]{2,1,0:T(8,128)(2,1)} %shard_map.148), calls=%async_computation | async-start | bytes 983040 | tf_op jit(solution)/shard_map/all_to_all | solution.py:411
  12.5 2.7 %collective-permute-start = (bf16[180,128]{1,0:T(8,128)(2,1)S(1)}, bf16[180,128]{1,0:T(8,128)(2,1)S(1)}, u32[]{:S(2)}, u32[]{:S(2)}) collective-permute-start(bf16[180,128]{1,0:T(8,128)(2,1)S(1)} %get-tuple-element.44), channel_id=1, source_target_pairs={{0,16},{16,0},{1,17},{17,1},{2,18},{18,2},{3,19},{19,3},{4,20},{20... | collective-permute-start | bytes 138248 | tf_op jit(solution)/shard_map/ppermute | solution.py:389
  21.7 13.6 %all-to-all-start.1 = ((bf16[32,40,128]{2,1,0:T(8,128)(2,1)}), bf16[32,40,128]{2,1,0:T(8,128)(2,1)S(1)}, u32[]{:S(2)}, u32[]{:S(2)}) async-start(bf16[32,40,128]{2,1,0:T(8,128)(2,1)} %shard_map.151), calls=%async_computation.1 | async-start | bytes 655360 | tf_op jit(solution)/shard_map/all_to_all | solution.py:434
  29.0 1.2 %copy-start = (bf16[9,256,384]{2,1,0:T(8,128)(2,1)}, bf16[9,256,384]{2,1,0:T(8,128)(2,1)S(1)}, u32[]{:S(2)}) copy-start(bf16[9,256,384]{2,1,0:T(8,128)(2,1)S(1)} %get-tuple-element.60.a_hbm) | copy-start | bytes 5308420
  30.2 1.2 %copy-start.1 = (bf16[9,384,256]{2,1,0:T(8,128)(2,1)}, bf16[9,384,256]{2,1,0:T(8,128)(2,1)S(1)}, u32[]{:S(2)}) copy-start(bf16[9,384,256]{2,1,0:T(8,128)(2,1)S(1)} %get-tuple-element.61.at_hbm) | copy-start | bytes 5308420
  42.6 2.3 %collective-permute-start.1 = (bf16[16,184,128]{2,1,0:T(8,128)(2,1)S(1)}, bf16[16,184,128]{2,1,0:T(8,128)(2,1)S(1)}, u32[]{:S(2)}, u32[]{:S(2)}) collective-permute-start(bf16[16,184,128]{2,1,0:T(8,128)(2,1)S(1)} %get-tuple-element.63), channel_id=1, source_target_pairs={{0,16},{16,0},{1,17},{17,1},{2,18},{18,2},{3,19},{19,3},{4,20},{20... | collective-permute-start | bytes 2261000 | tf_op jit(solution)/shard_map/ppermute | solution.py:389
  46.6 20.1 %all-to-all-start.2 = ((bf16[16,224,128]{2,1,0:T(8,128)(2,1)}), bf16[16,224,128]{2,1,0:T(8,128)(2,1)S(1)}, u32[]{:S(2)}, u32[]{:S(2)}) async-start(bf16[16,224,128]{2,1,0:T(8,128)(2,1)} %shard_map.154), calls=%async_computation.2 | async-start | bytes 1835008 | tf_op jit(solution)/shard_map/all_to_all | solution.py:464
  66.8 4.4 %collective-permute-start.2 = (f32[144,128]{1,0:T(8,128)S(1)}, f32[144,128]{1,0:T(8,128)S(1)}, u32[]{:S(2)}, u32[]{:S(2)}) collective-permute-start(f32[144,128]{1,0:T(8,128)S(1)} %convert_reduce_fusion), channel_id=1, source_target_pairs={{0,32},{32,0},{64,96},{96,64},{128,160},{160,128},{192,224},{224,1... | collective-permute-start | bytes 221192 | tf_op jit(solution)/shard_map/ppermute | solution.py:478
  71.2 5.7 %collective-permute-start.3 = (f32[144,128]{1,0:T(8,128)S(1)}, f32[144,128]{1,0:T(8,128)S(1)}, u32[]{:S(2)}, u32[]{:S(2)}) collective-permute-start(f32[144,128]{1,0:T(8,128)S(1)} %add.9), channel_id=1, source_target_pairs={{0,64},{32,96},{64,0},{96,32},{128,192},{160,224},{192,128},{224,1... | collective-permute-start | bytes 221192 | tf_op jit(solution)/shard_map/ppermute | solution.py:478
  76.9 14.3 %collective-permute-start.4 = (f32[144,128]{1,0:T(8,128)S(1)}, f32[144,128]{1,0:T(8,128)S(1)}, u32[]{:S(2)}, u32[]{:S(2)}) collective-permute-start(f32[144,128]{1,0:T(8,128)S(1)} %add.10), channel_id=1, source_target_pairs={{0,128},{32,160},{64,192},{96,224},{128,0},{160,32},{192,64},{224,... | collective-permute-start | bytes 221192 | tf_op jit(solution)/shard_map/ppermute | solution.py:478
  86.1 13.7 %all-to-all-start.3 = ((bf16[16,120,128]{2,1,0:T(8,128)(2,1)}), bf16[16,120,128]{2,1,0:T(8,128)(2,1)S(1)}, u32[]{:S(2)}, u32[]{:S(2)}) async-start(bf16[16,120,128]{2,1,0:T(8,128)(2,1)} %shard_map.156), calls=%async_computation.3 | async-start | bytes 983040 | tf_op jit(solution)/shard_map/all_to_all | solution.py:486
  91.2 1.4 %collective-permute-start.5 = (f32[144,128]{1,0:T(8,128)S(1)}, f32[144,128]{1,0:T(8,128)S(1)}, u32[]{:S(2)}, u32[]{:S(2)}) collective-permute-start(f32[144,128]{1,0:T(8,128)S(1)} %add.11), channel_id=1, source_target_pairs={{0,16},{16,0},{1,17},{17,1},{2,18},{18,2},{3,19},{19,3},{4,20},{20... | collective-permute-start | bytes 221192 | tf_op jit(solution)/shard_map/ppermute | solution.py:389

commit v3 on v2

--- a/solution.py
+++ b/solution.py
@@ -222,7 +222,7 @@
     other_ref[...] = swap64(got).astype(BF16)
 
 
-def mixing_body(spot_ref, mine_ref, got_ref, a_ref, at_ref, p_ref):
+def mixing_body(spot_ref, mine_ref, got_ref, p_ref):
     rows, width, count = K * 16, HIN * 2 * M12, K * SUPPORT * 4
     low = spot_ref[0, 0] == 0
     mine, got = mine_ref[...].astype(F32), got_ref[...].astype(F32)
@@ -250,28 +250,14 @@
             collect = jnp.where(key == 8 * half + ri, 1.0, 0.0).astype(BF16)
             total = total + dot(collect, spread)
     p_ref[...] = total
-    mode = lax.broadcasted_iota(jnp.int32, (M16, width), 1) % M12
-    same = lax.broadcasted_iota(jnp.int32, (M16, width), 0) == mode
-    for i in range(rows):
-        block = jnp.where(same, jnp.broadcast_to(p_ref[i : i + 1, :], (M16, width)), 0.0)
-        a_ref[i // 16, M16 * (i % 16) : M16 * (i % 16 + 1), :] = block.astype(BF16)
-    spot = lax.broadcasted_iota(jnp.int32, (16, 256), 1) // M16
-    spread = jnp.where(lax.broadcasted_iota(jnp.int32, (16, 256), 0) == spot, 1.0, 0.0).astype(BF16)
-    left = lax.broadcasted_iota(jnp.int32, (width, 256), 0) % M12
-    right = lax.broadcasted_iota(jnp.int32, (width, 256), 1) % M16
-    for k in range(K):
-        part = p_ref[16 * k : 16 * (k + 1), :].astype(BF16)
-        grown = lax.dot_general(part, spread, (((0,), (0,)), ((), ())), preferred_element_type=F32)
-        at_ref[k] = jnp.where(left == right, grown, 0.0).astype(BF16)
-
-
-def middle_body(
-    band_ref, r_ref, a_hbm, at_hbm, w_hbm, mine_ref, other_ref, gs_ref, out_ref, sg_ref, a_ref, at_ref, w_ref, sems
-):
-    copies = [
-        fetch((a_hbm.at[k], w_hbm.at[k], at_hbm.at[k]), (a_ref.at[k], w_ref.at[k], at_ref.at[k]), sems.at[k])
-        for k in range(K)
-    ]
+
+
+def row_of_share(column):
+    return 16 * (column % 16) + column // 16
+
+
+def middle_body(band_ref, r_ref, p_ref, w_hbm, mine_ref, other_ref, gs_ref, out_ref, sg_ref, w_ref, sems):
+    copies = fetch([w_hbm.at[k] for k in range(K)], [w_ref.at[k] for k in range(K)], sems)
     keep = low_half((M16, 128))
     for o in range(HOUT):
         for i in range(2):
@@ -280,17 +266,25 @@
             cols = slice(128 * i, 128 * (i + 1))
             gs_ref[32 * o : 32 * o + 16, cols] = jnp.where(keep, first, swap64(second)).astype(BF16)
             gs_ref[32 * o + 16 : 32 * o + 32, cols] = jnp.where(keep, swap64(first), second).astype(BF16)
-    rows = HIN * 2 * M12
+    used = M12 * 16
+    gs = dot(one_hot((used, 256), row_of_share), gs_ref[...]).astype(BF16)
+    width = HIN * 2 * M12
     x = jnp.concatenate(
-        [r_ref[:, h, M16:CHUNK_MID, :].reshape(rows, 128) for h in range(2)], axis=1
-    )
-    gs = gs_ref[...]
+        [r_ref[:, h, M16:CHUNK_MID, :].reshape(width, 128) for h in range(2)], axis=1
+    )
+    lane_mode = lax.broadcasted_iota(jnp.int32, (16, width), 1) % M12
+    diagonal = (
+        lax.broadcasted_iota(jnp.int32, (width, used), 0) % M12
+        == lax.broadcasted_iota(jnp.int32, (width, used), 1) // 16
+    )
+    spread = one_hot((16, used), lambda column: column % 16)
     low = band_ref[0, 0] == 0
 
     for k in range(K):
-        for copy in copies[k]:
-            copy.wait()
-        mixed = dot(a_ref[k], x).astype(BF16)
+        placed = p_ref[16 * k : 16 * (k + 1), :]
+        blocks = [jnp.where(lane_mode == m, placed, 0.0).astype(BF16) for m in range(M12)]
+        mixed = dot(jnp.concatenate(blocks, axis=0), x).astype(BF16)
+        copies[k].wait()
         out_now = dot(mixed, w_ref[k])
         grad = lax.dot_general(mixed, gs, (((0,), (0,)), ((), ())), preferred_element_type=F32)
         where_to = (slice(None), slice(CHUNK_MID + 16 * k, CHUNK_MID + 16 * (k + 1)), slice(None))
@@ -298,7 +292,10 @@
         mine_ref[where_to] = jnp.where(low, grad[:, :128], grad[:, 128:]).astype(BF16).reshape(shape)
         other_ref[where_to] = jnp.where(low, grad[:, 128:], grad[:, :128]).astype(BF16).reshape(shape)
         back = lax.dot_general(gs, w_ref[k], (((1,), (1,)), ((), ())), preferred_element_type=F32)
-        sg_now = dot(at_ref[k], back.astype(BF16))
+        grown = lax.dot_general(
+            placed.astype(BF16), spread, (((0,), (0,)), ((), ())), preferred_element_type=F32
+        )
+        sg_now = dot(jnp.where(diagonal, grown, 0.0).astype(BF16), back.astype(BF16))
         if k == 0:
             out_ref[...] = out_now
             sg_ref[...] = sg_now
@@ -306,11 +303,18 @@
             out_ref[...] += out_now
             sg_ref[...] += sg_now
 
+    ordered = lax.dot_general(
+        one_hot((used, 256), row_of_share),
+        out_ref[...].astype(BF16),
+        (((0,), (0,)), ((), ())),
+        preferred_element_type=F32,
+    )
+
     def output_rows(n):
         o, q = n // 4, n % 4
         cols = slice(128 * (q // 2), 128 * (q // 2 + 1))
-        re = out_ref[32 * o : 32 * o + 16, cols]
-        im = out_ref[32 * o + 16 : 32 * o + 32, cols]
+        re = ordered[32 * o : 32 * o + 16, cols]
+        im = ordered[32 * o + 16 : 32 * o + 32, cols]
         return jnp.where(keep, re, swap64(im)) if q % 2 == 0 else jnp.where(keep, swap64(re), im)
 
     def field_rows(n):
@@ -433,32 +437,23 @@
     (sent,) = call(spectra_body, [VMEM] * 3, [((SHARES, CHUNK_MID, 128), BF16)], flops=300 << 20)(landed, flat, inv_t)
     landed = lax.all_to_all(sent, JOINT, split_axis=0, concat_axis=0, tiled=True)
     mine, got, sent = lax.optimization_barrier((mine, got, sent))
-    mix, mix_t = call(
-        mixing_body,
-        [SMEM, VMEM, VMEM],
-        [((K, 256, 384), BF16), ((K, 384, 256), BF16)],
-        scratch=[pltpu.VMEM((K * 16, 384), F32)],
-        nbytes=4 << 20,
-    )(spot, mine, got)
+    (placed,) = call(mixing_body, [SMEM, VMEM, VMEM], [((K * 16, HIN * 2 * M12), F32)])(spot, mine, got)
 
     chunk = (LANES, CHUNK_MID + 16 * K, 128)
     mine, other = call(
         middle_body,
-        [SMEM, VMEM, HBM, HBM, HBM],
+        [SMEM, VMEM, VMEM, HBM],
         [(chunk, BF16), (chunk, BF16)],
         flops=2 << 30,
-        nbytes=6 << 20,
+        nbytes=3 << 20,
         scratch=[
             pltpu.VMEM((256, 256), BF16),
-            pltpu.VMEM((256, 256), F32),
+            pltpu.VMEM((192, 256), F32),
             pltpu.VMEM((384, 256), F32),
-            pltpu.VMEM((K, 256, 384), BF16),
-            pltpu.VMEM((K, 384, 256), BF16),
             pltpu.VMEM((K, 256, 256), BF16),
-            dma((K, 3)),
+            dma((K,)),
         ],
-        vmem=32,
-    )(spot, landed.reshape(HIN, 2, CHUNK_MID, 128), in_hbm(mix), in_hbm(mix_t), in_hbm(weights))
+    )(spot, landed.reshape(HIN, 2, CHUNK_MID, 128), placed, in_hbm(weights))
     got = swap_bands(other)
     (sent,) = call(merge_body, [SMEM, VMEM, VMEM], [((LANES, CHUNK_OUT, 128), BF16)], nbytes=2 << 20)(spot, mine, got)
     landed = lax.all_to_all(sent, "azimuth", split_axis=0, concat_axis=0, tiled=True)
@@ -474,14 +469,19 @@
 
     landed, tall, inv = lax.optimization_barrier((landed, tall, inv))
 
-    def exchange(value, step):
-        return value + lax.ppermute(value, "ens", [(i, i ^ step) for i in range(lax.axis_size("ens"))])
+    members = lax.axis_size("ens")
+
+    def partner(value, member_bit, band_bit):
+        pairs = [(i, i ^ (2 * member_bit + band_bit)) for i in range(2 * members)]
+        return lax.ppermute(value, ("ens", "polar"), pairs)
 
     half = jnp.sum(landed[:, 2 * CHUNK_MID :, :].astype(F32), axis=0)
-    half = exchange(half, 1)
-    half = exchange(half, 2)
-    half = exchange(half, 4)
-    far = swap_bands(half)
+    half = half + partner(half, 4, 0)
+    half = half + partner(half, 2, 0)
+    far = partner(half, 1, 1)
+    near = partner(half, 1, 0)
+    far = far + partner(half, 0, 1)
+    half = half + near
     (sent,) = call(fields_body, [VMEM] * 3, [((LANES, CHUNK_IN, 128), BF16)], flops=300 << 20)(landed, tall, inv)
     landed = lax.all_to_all(sent, "azimuth", split_axis=0, concat_axis=0, tiled=True)
     weight_grad = jnp.concatenate([jnp.where(low, half, far), jnp.where(low, far, half)], axis=1)

time: 101 us -> 95 us (0.941)
  Pallas kernels: 23.7 us -> 21.2 us
  local copies, waits for them, and re-layouts: 2.56 us -> 0.1 us
    all_to_all x3, waiting for transfers between devices: 24.9 us -> 20.3 us  [local(): lax.all_to_all(sent, 'azimuth', split_axis=0, concat_axis=0, tiled=True)]
    all_to_all x1, waiting for transfers between devices: 3.93 us -> 7.2 us  [local(): lax.all_to_all(sent, JOINT, split_axis=0, concat_axis=0, tiled=True)]
    unnamed x6 -> x2, local copies, waits for them, and re-layouts: 2.47 us -> 0.01 us
    pallas_call x2, Pallas kernels: 9.42 us -> 7 us  [the longest x1 5.58 us: local(): call(middle_body, [SMEM, VMEM, VMEM, HBM], [(chunk, BF16), (chunk, BF16)]...]
    ppermute x3 -> x5, waiting for transfers between devices: 4.78 us -> 6.54 us  [partner(): return lax.ppermute(value, ('ens', 'polar'), pairs)]
    ppermute x3 -> x2, waiting for transfers between devices: 3.47 us -> 2.23 us  [swap_bands(): return lax.ppermute(value, 'polar', [(0, 1), (1, 0)])]
    ppermute x3 -> x5, starting transfers between devices: 13.1 us -> 12.4 us  [partner(): return lax.ppermute(value, ('ens', 'polar'), pairs)]
  transfers between devices with their start and end apart: 10 -> 11, of which waited for: 8 -> 8; matrix products, arithmetic and copies ran while one was open for 1% -> 1% of each run, Pallas kernels for 10% -> 10%
where the time goes in v3:
time: 95 us; the launch traced here: 94.5 us
  waiting for transfers between devices  36.3 us (38%)
  starting transfers between devices  35.2 us (37%)
  Pallas kernels  21.2 us (22%)
    all_to_all x3, waiting for transfers between devices, local(): lax.all_to_all(sent, 'azimuth', split_axis=0, concat_axis=0, tiled=True)  20.3 us
    all_to_all x3, starting transfers between devices, local(): lax.all_to_all(sent, 'azimuth', split_axis=0, concat_axis=0, tiled=True)  17.7 us
    ppermute x5, starting transfers between devices, partner(): return lax.ppermute(value, ('ens', 'polar'), pairs)  12.4 us
    all_to_all x1, waiting for transfers between devices, local(): lax.all_to_all(sent, JOINT, split_axis=0, concat_axis=0, tiled=True)  7.2 us
    ppermute x5, waiting for transfers between devices, partner(): return lax.ppermute(value, ('ens', 'polar'), pairs)  6.54 us
    pallas_call x1, Pallas kernels, local(): call(middle_body, [SMEM, VMEM, VMEM, HBM], [(chunk, BF16), (chunk, BF16)]...  5.58 us
    all_to_all x1, starting transfers between devices, local(): lax.all_to_all(sent, JOINT, split_axis=0, concat_axis=0, tiled=True)  4.99 us
    pallas_call x1, Pallas kernels, local(): call(flipped_table_body, [HBM] * 8, [((2, 384, 768), BF16), ((2, 512, 384...  2.59 us
  transfers between devices with their start and end apart: 11, of which 8 were waited for; matrix products, arithmetic and copies ran while one was open for 1% of the time, Pallas kernels for 10%

profile of v3, /device:TPU:2, one launch (start us, length us, event | category | flops | bytes accessed | tf_op | source)
XLA Modules:
  0.0 94.5 jit_solution(6224475533555406321)
XLA Ops:
  0.6 2.3 %shard_map.148 = bf16[16,120,128]{2,1,0:T(8,128)(2,1)} custom-call(bf16[720,256]{1,0:T(8,128)(2,1)} %bitcast.26, bf16[45,4,256]{2,1,0:T(4,128)(2,1)} %bitcast.29), custom_call_target="tpu_custom_call" | custom-call | bytes 1048576 | tf_op jit(solution)/shard_map/pallas_call | solution.py:402
  3.0 7.5 %all-to-all-start = ((bf16[16,120,128]{2,1,0:T(8,128)(2,1)}), bf16[16,120,128]{2,1,0:T(8,128)(2,1)S(1)}, u32[]{:S(2)}, u32[]{:S(2)}) async-start(bf16[16,120,128]{2,1,0:T(8,128)(2,1)} %shard_map.148), calls=%async_computation | async-start | bytes 983040 | tf_op jit(solution)/shard_map/all_to_all | solution.py:415
  10.6 1.9 %shard_map.149 = (bf16[180,128]{1,0:T(8,128)(2,1)S(1)}, bf16[180,128]{1,0:T(8,128)(2,1)S(1)}) custom-call(s32[1,2]{1,0:T(1,128)S(1)} %add_bitcast_fusion.spot_ref.band_ref, s32[4,2]{1,0:T(4,128)S(1)} %copy.16.support_ref, bf16[45,4,720]{2,1,0:T(4,128)(2,1)} %bitcast.27), custom_call_target="tpu_custom_call" | custom-call | bytes 1048576 | tf_op jit(solution)/shard_map/pallas_call | solution.py:418
  12.6 2.6 %shard_map.150 = (bf16[2,384,768]{2,1,0:T(8,128)(2,1)S(1)}, bf16[2,512,384]{2,1,0:T(8,128)(2,1)S(1)}) custom-call(f32[2,8,384]{2,1,0:T(8,128)} %constant.29.clone.refs_0_, f32[2,8,384]{2,1,0:T(8,128)} %constant.30.clone.refs_1_, f32[2,96,384]{2,1,0:T(8,128)} %constant.31.clone.refs_2_, f32[2,96,384]{2,1,0:T(8,128)} %constant.32.clone.refs_3_, ...), custom_call_target="tpu_custom_call" | custom-call | bytes 5242880 | tf_op jit(solution)/shard_map/pallas_call | solution.py:428
  15.2 5.1 %all-to-all-done.r_ref = bf16[16,120,128]{2,1,0:T(8,128)(2,1)S(1)} async-done(((bf16[16,120,128]{2,1,0:T(8,128)(2,1)}), bf16[16,120,128]{2,1,0:T(8,128)(2,1)S(1)}, u32[]{:S(2)}, u32[]{:S(2)}) %all-to-all-start) | async-done | bytes 491552 | tf_op jit(solution)/shard_map/all_to_all | solution.py:415
  20.3 1.5 %shard_map.151 = bf16[32,40,128]{2,1,0:T(8,128)(2,1)} custom-call(bf16[16,120,128]{2,1,0:T(8,128)(2,1)S(1)} %all-to-all-done.r_ref, bf16[2,384,768]{2,1,0:T(8,128)(2,1)S(1)} %get-tuple-element.52.wt_ref, bf16[2,512,384]{2,1,0:T(8,128)(2,1)S(1)} %get-tuple-element.53.vt_ref), custom_call_target="tpu_custom_call" | custom-call | flops 314572800 | bytes 1048576 | tf_op jit(solution)/shard_map/pallas_call | solution.py:437
  21.7 5.0 %all-to-all-start.1 = ((bf16[32,40,128]{2,1,0:T(8,128)(2,1)}), bf16[32,40,128]{2,1,0:T(8,128)(2,1)S(1)}, u32[]{:S(2)}, u32[]{:S(2)}) async-start(bf16[32,40,128]{2,1,0:T(8,128)(2,1)} %shard_map.151), calls=%async_computation.1 | async-start | bytes 655360 | tf_op jit(solution)/shard_map/all_to_all | solution.py:438
  26.7 1.4 %shard_map.152.p_ref = f32[144,384]{1,0:T(8,128)S(1)} custom-call(s32[1,2]{1,0:T(1,128)S(1)} %add_bitcast_fusion.spot_ref.band_ref, bf16[180,128]{1,0:T(8,128)(2,1)S(1)} %get-tuple-element.56.mine_ref, bf16[180,128]{1,0:T(8,128)(2,1)S(1)} %collective-permute-done.got_ref), custom_call_target="tpu_custom_call" | custom-call | bytes 1048576 | tf_op jit(solution)/shard_map/pallas_call | solution.py:440
  28.2 7.2 %all-to-all-done.1 = bf16[32,40,128]{2,1,0:T(8,128)(2,1)S(1)} async-done(((bf16[32,40,128]{2,1,0:T(8,128)(2,1)}), bf16[32,40,128]{2,1,0:T(8,128)(2,1)S(1)}, u32[]{:S(2)}, u32[]{:S(2)}) %all-to-all-start.1) | async-done | bytes 327712 | tf_op jit(solution)/shard_map/all_to_all | solution.py:438
  35.4 5.6 %shard_map.153 = (bf16[16,184,128]{2,1,0:T(8,128)(2,1)S(1)}, bf16[16,184,128]{2,1,0:T(8,128)(2,1)S(1)}) custom-call(s32[1,2]{1,0:T(1,128)S(1)} %add_bitcast_fusion.spot_ref.band_ref, bf16[16,2,40,128]{3,2,1,0:T(8,128)(2,1)S(1)} %bitcast.25, f32[144,384]{1,0:T(8,128)S(1)} %shard_map.152.p_ref, bf16[9,256,256]{2,1,0:T(8,128)(2,1)} %w_hbm.1), custom_call_target="tpu_custom_call" | custom-call | flops 2147483648 | bytes 3145728 | tf_op jit(solution)/shard_map/pallas_call | solution.py:443
  41.1 2.2 %collective-permute-done.1.got_ref = bf16[16,184,128]{2,1,0:T(8,128)(2,1)S(1)} collective-permute-done((bf16[16,184,128]{2,1,0:T(8,128)(2,1)S(1)}, bf16[16,184,128]{2,1,0:T(8,128)(2,1)S(1)}, u32[]{:S(2)}, u32[]{:S(2)}) %collective-permute-start.1) | collective-permute-done | bytes 753696 | tf_op jit(solution)/shard_map/ppermute | solution.py:393
  43.3 1.7 %shard_map.154 = bf16[16,224,128]{2,1,0:T(8,128)(2,1)} custom-call(s32[1,2]{1,0:T(1,128)S(1)} %add_bitcast_fusion.spot_ref.band_ref, bf16[16,184,128]{2,1,0:T(8,128)(2,1)S(1)} %get-tuple-element.58.mine_ref, bf16[16,184,128]{2,1,0:T(8,128)(2,1)S(1)} %collective-permute-done.1.got_ref), custom_call_target="tpu_custom_call" | custom-call | bytes 2097152 | tf_op jit(solution)/shard_map/pallas_call | solution.py:458
  44.9 5.0 %all-to-all-start.2 = ((bf16[16,224,128]{2,1,0:T(8,128)(2,1)}), bf16[16,224,128]{2,1,0:T(8,128)(2,1)S(1)}, u32[]{:S(2)}, u32[]{:S(2)}) async-start(bf16[16,224,128]{2,1,0:T(8,128)(2,1)} %shard_map.154), calls=%async_computation.2 | async-start | bytes 1835008 | tf_op jit(solution)/shard_map/all_to_all | solution.py:459
  49.9 1.8 %shard_map.155 = (bf16[2,768,384]{2,1,0:T(8,128)(2,1)S(1)}, bf16[2,384,512]{2,1,0:T(8,128)(2,1)S(1)}) custom-call(f32[2,8,384]{2,1,0:T(8,128)} %constant.29.clone.refs_0_, f32[2,8,384]{2,1,0:T(8,128)} %constant.30.clone.refs_1_, f32[2,96,384]{2,1,0:T(8,128)} %constant.31.clone.refs_2_, f32[2,96,384]{2,1,0:T(8,128)} %constant.32.clone.refs_3_, ...), custom_call_target="tpu_custom_call" | custom-call | bytes 5242880 | tf_op jit(solution)/shard_map/pallas_call | solution.py:462
  51.8 13.3 %all-to-all-done.2.r_ref = bf16[16,224,128]{2,1,0:T(8,128)(2,1)S(1)} async-done(((bf16[16,224,128]{2,1,0:T(8,128)(2,1)}), bf16[16,224,128]{2,1,0:T(8,128)(2,1)S(1)}, u32[]{:S(2)}, u32[]{:S(2)}) %all-to-all-start.2) | async-done | bytes 917536 | tf_op jit(solution)/shard_map/all_to_all | solution.py:459
  65.1 7.3 %collective-permute-start.2 = (f32[144,128]{1,0:T(8,128)S(1)}, f32[144,128]{1,0:T(8,128)S(1)}, u32[]{:S(2)}, u32[]{:S(2)}) collective-permute-start(f32[144,128]{1,0:T(8,128)S(1)} %convert_reduce_fusion), channel_id=1, source_target_pairs={{0,128},{16,144},{32,160},{48,176},{64,192},{80,208},{96,224},{112... | collective-permute-start | bytes 221192 | tf_op jit(solution)/shard_map/ppermute | solution.py:476
  72.4 2.4 %collective-permute-done.2 = f32[144,128]{1,0:T(8,128)S(1)} collective-permute-done((f32[144,128]{1,0:T(8,128)S(1)}, f32[144,128]{1,0:T(8,128)S(1)}, u32[]{:S(2)}, u32[]{:S(2)}) %collective-permute-start.2) | collective-permute-done | bytes 73760 | tf_op jit(solution)/shard_map/ppermute | solution.py:476
  74.8 2.9 %collective-permute-start.3 = (f32[144,128]{1,0:T(8,128)S(1)}, f32[144,128]{1,0:T(8,128)S(1)}, u32[]{:S(2)}, u32[]{:S(2)}) collective-permute-start(f32[144,128]{1,0:T(8,128)S(1)} %add.12), channel_id=1, source_target_pairs={{0,64},{16,80},{32,96},{48,112},{64,0},{80,16},{96,32},{112,48},{1... | collective-permute-start | bytes 221192 | tf_op jit(solution)/shard_map/ppermute | solution.py:476
  77.7 1.4 %shard_map.156 = bf16[16,120,128]{2,1,0:T(8,128)(2,1)} custom-call(bf16[16,224,128]{2,1,0:T(8,128)(2,1)S(1)} %all-to-all-done.2.r_ref, bf16[2,768,384]{2,1,0:T(8,128)(2,1)S(1)} %get-tuple-element.71.w_ref, bf16[2,384,512]{2,1,0:T(8,128)(2,1)S(1)} %get-tuple-element.72.v_ref), custom_call_target="tpu_custom_call" | custom-call | flops 314572800 | bytes 1048576 | tf_op jit(solution)/shard_map/pallas_call | solution.py:485
  79.2 5.2 %all-to-all-start.3 = ((bf16[16,120,128]{2,1,0:T(8,128)(2,1)}), bf16[16,120,128]{2,1,0:T(8,128)(2,1)S(1)}, u32[]{:S(2)}, u32[]{:S(2)}) async-start(bf16[16,120,128]{2,1,0:T(8,128)(2,1)} %shard_map.156), calls=%async_computation.3 | async-start | bytes 983040 | tf_op jit(solution)/shard_map/all_to_all | solution.py:486
  86.6 1.9 %collective-permute-done.5 = f32[144,128]{1,0:T(8,128)S(1)} collective-permute-done((f32[144,128]{1,0:T(8,128)S(1)}, f32[144,128]{1,0:T(8,128)S(1)}, u32[]{:S(2)}, u32[]{:S(2)}) %collective-permute-start.5) | collective-permute-done | bytes 73760 | tf_op jit(solution)/shard_map/ppermute | solution.py:476
  88.5 2.2 %collective-permute-done.4 = f32[144,128]{1,0:T(8,128)S(1)} collective-permute-done((f32[144,128]{1,0:T(8,128)S(1)}, f32[144,128]{1,0:T(8,128)S(1)}, u32[]{:S(2)}, u32[]{:S(2)}) %collective-permute-start.4) | collective-permute-done | bytes 73760 | tf_op jit(solution)/shard_map/ppermute | solution.py:476
  91.4 2.0 %all-to-all-done.3.r_ref = bf16[16,120,128]{2,1,0:T(8,128)(2,1)S(1)} async-done(((bf16[16,120,128]{2,1,0:T(8,128)(2,1)}), bf16[16,120,128]{2,1,0:T(8,128)(2,1)S(1)}, u32[]{:S(2)}, u32[]{:S(2)}) %all-to-all-start.3) | async-done | bytes 491552 | tf_op jit(solution)/shard_map/all_to_all | solution.py:486
  93.4 1.1 %shard_map.157 = (bf16[720,256]{1,0:T(8,128)(2,1)}, bf16[45,4,256]{2,1,0:T(4,128)(2,1)}) custom-call(bf16[16,120,128]{2,1,0:T(8,128)(2,1)S(1)} %all-to-all-done.3.r_ref), custom_call_target="tpu_custom_call" | custom-call | bytes 1048576 | tf_op jit(solution)/shard_map/pallas_call | solution.py:488
  (17 shorter events, 3.4 us)
Async XLA Ops:
  0.6 9.8 %copy-start = (s32[4,2]{0,1:T(2,128)S(1)}, s32[4,2]{0,1:T(2,128)}, u32[]{:S(2)}) copy-start(s32[4,2]{0,1:T(2,128)} %param.15) | copy-start | bytes 100
  3.0 17.3 %all-to-all-start = ((bf16[16,120,128]{2,1,0:T(8,128)(2,1)}), bf16[16,120,128]{2,1,0:T(8,128)(2,1)S(1)}, u32[]{:S(2)}, u32[]{:S(2)}) async-start(bf16[16,120,128]{2,1,0:T(8,128)(2,1)} %shard_map.148), calls=%async_computation | async-start | bytes 983040 | tf_op jit(solution)/shard_map/all_to_all | solution.py:415
  12.5 2.7 %collective-permute-start = (bf16[180,128]{1,0:T(8,128)(2,1)S(1)}, bf16[180,128]{1,0:T(8,128)(2,1)S(1)}, u32[]{:S(2)}, u32[]{:S(2)}) collective-permute-start(bf16[180,128]{1,0:T(8,128)(2,1)S(1)} %get-tuple-element.42), channel_id=1, source_target_pairs={{0,16},{16,0},{1,17},{17,1},{2,18},{18,2},{3,19},{19,3},{4,20},{20... | collective-permute-start | bytes 138248 | tf_op jit(solution)/shard_map/ppermute | solution.py:393
  21.7 13.6 %all-to-all-start.1 = ((bf16[32,40,128]{2,1,0:T(8,128)(2,1)}), bf16[32,40,128]{2,1,0:T(8,128)(2,1)S(1)}, u32[]{:S(2)}, u32[]{:S(2)}) async-start(bf16[32,40,128]{2,1,0:T(8,128)(2,1)} %shard_map.151), calls=%async_computation.1 | async-start | bytes 655360 | tf_op jit(solution)/shard_map/all_to_all | solution.py:438
  41.0 2.3 %collective-permute-start.1 = (bf16[16,184,128]{2,1,0:T(8,128)(2,1)S(1)}, bf16[16,184,128]{2,1,0:T(8,128)(2,1)S(1)}, u32[]{:S(2)}, u32[]{:S(2)}) collective-permute-start(bf16[16,184,128]{2,1,0:T(8,128)(2,1)S(1)} %get-tuple-element.59), channel_id=1, source_target_pairs={{0,16},{16,0},{1,17},{17,1},{2,18},{18,2},{3,19},{19,3},{4,20},{20... | collective-permute-start | bytes 2261000 | tf_op jit(solution)/shard_map/ppermute | solution.py:393
  44.9 20.1 %all-to-all-start.2 = ((bf16[16,224,128]{2,1,0:T(8,128)(2,1)}), bf16[16,224,128]{2,1,0:T(8,128)(2,1)S(1)}, u32[]{:S(2)}, u32[]{:S(2)}) async-start(bf16[16,224,128]{2,1,0:T(8,128)(2,1)} %shard_map.154), calls=%async_computation.2 | async-start | bytes 1835008 | tf_op jit(solution)/shard_map/all_to_all | solution.py:459
  65.1 9.7 %collective-permute-start.2 = (f32[144,128]{1,0:T(8,128)S(1)}, f32[144,128]{1,0:T(8,128)S(1)}, u32[]{:S(2)}, u32[]{:S(2)}) collective-permute-start(f32[144,128]{1,0:T(8,128)S(1)} %convert_reduce_fusion), channel_id=1, source_target_pairs={{0,128},{16,144},{32,160},{48,176},{64,192},{80,208},{96,224},{112... | collective-permute-start | bytes 221192 | tf_op jit(solution)/shard_map/ppermute | solution.py:476
  74.8 9.5 %collective-permute-start.3 = (f32[144,128]{1,0:T(8,128)S(1)}, f32[144,128]{1,0:T(8,128)S(1)}, u32[]{:S(2)}, u32[]{:S(2)}) collective-permute-start(f32[144,128]{1,0:T(8,128)S(1)} %add.12), channel_id=1, source_target_pairs={{0,64},{16,80},{32,96},{48,112},{64,0},{80,16},{96,32},{112,48},{1... | collective-permute-start | bytes 221192 | tf_op jit(solution)/shard_map/ppermute | solution.py:476
  79.2 14.2 %all-to-all-start.3 = ((bf16[16,120,128]{2,1,0:T(8,128)(2,1)}), bf16[16,120,128]{2,1,0:T(8,128)(2,1)S(1)}, u32[]{:S(2)}, u32[]{:S(2)}) async-start(bf16[16,120,128]{2,1,0:T(8,128)(2,1)} %shard_map.156), calls=%async_computation.3 | async-start | bytes 983040 | tf_op jit(solution)/shard_map/all_to_all | solution.py:486
  84.4 2.2 %collective-permute-start.6 = (f32[144,128]{1,0:T(8,128)S(1)}, f32[144,128]{1,0:T(8,128)S(1)}, u32[]{:S(2)}, u32[]{:S(2)}) collective-permute-start(f32[144,128]{1,0:T(8,128)S(1)} %add.13), channel_id=1, source_target_pairs={{0,16},{16,0},{32,48},{48,32},{64,80},{80,64},{96,112},{112,96},{1... | collective-permute-start | bytes 221192 | tf_op jit(solution)/shard_map/ppermute | solution.py:476
  84.5 4.1 %collective-permute-start.5 = (f32[144,128]{1,0:T(8,128)S(1)}, f32[144,128]{1,0:T(8,128)S(1)}, u32[]{:S(2)}, u32[]{:S(2)}) collective-permute-start(f32[144,128]{1,0:T(8,128)S(1)} %add.13), channel_id=1, source_target_pairs={{0,48},{16,32},{32,16},{48,0},{64,112},{80,96},{96,80},{112,64},{1... | collective-permute-start | bytes 221192 | tf_op jit(solution)/shard_map/ppermute | solution.py:476
  85.5 5.2 %collective-permute-start.4 = (f32[144,128]{1,0:T(8,128)S(1)}, f32[144,128]{1,0:T(8,128)S(1)}, u32[]{:S(2)}, u32[]{:S(2)}) collective-permute-start(f32[144,128]{1,0:T(8,128)S(1)} %add.13), channel_id=1, source_target_pairs={{0,32},{16,48},{32,0},{48,16},{64,96},{80,112},{96,64},{112,80},{1... | collective-permute-start | bytes 221192 | tf_op jit(solution)/shard_map/ppermute | solution.py:476

commit v4 on v3

--- a/solution.py
+++ b/solution.py
@@ -60,12 +60,12 @@
 SMEM = pl.BlockSpec(memory_space=pltpu.SMEM)
 
 
-def call(body, places, outs, flops=0, scratch=(), nbytes=1 << 20, vmem=16):
+def call(body, places, outs, flops=0, scratch=(), nbytes=1 << 20, vmem=16, out_place=VMEM):
     return pl.pallas_call(
         body,
         out_shape=[jax.ShapeDtypeStruct(s, d) for s, d in outs],
         in_specs=places,
-        out_specs=[VMEM] * len(outs),
+        out_specs=[out_place] * len(outs),
         scratch_shapes=list(scratch),
         compiler_params=pltpu.CompilerParams(vmem_limit_bytes=vmem << 20),
         cost_estimate=pl.CostEstimate(flops=flops, bytes_accessed=nbytes, transcendentals=0),
@@ -222,7 +222,7 @@
     other_ref[...] = swap64(got).astype(BF16)
 
 
-def mixing_body(spot_ref, mine_ref, got_ref, p_ref):
+def mixing_body(spot_ref, mine_ref, got_ref, p_ref, at_ref):
     rows, width, count = K * 16, HIN * 2 * M12, K * SUPPORT * 4
     low = spot_ref[0, 0] == 0
     mine, got = mine_ref[...].astype(F32), got_ref[...].astype(F32)
@@ -250,13 +250,30 @@
             collect = jnp.where(key == 8 * half + ri, 1.0, 0.0).astype(BF16)
             total = total + dot(collect, spread)
     p_ref[...] = total
+    used = 16 * M12
+    for k in range(0, K, 2):
+        pair = min(2, K - k)
+        row = lax.broadcasted_iota(jnp.int32, (16 * pair, used * pair), 0)
+        column = lax.broadcasted_iota(jnp.int32, (16 * pair, used * pair), 1)
+        spread = jnp.where(row == 16 * (column // used) + column % 16, 1.0, 0.0).astype(BF16)
+        row = lax.broadcasted_iota(jnp.int32, (width, used * pair), 0) % M12
+        column = (lax.broadcasted_iota(jnp.int32, (width, used * pair), 1) // 16) % M12
+        grown = lax.dot_general(
+            p_ref[16 * k : 16 * (k + pair), :].astype(BF16),
+            spread,
+            (((0,), (0,)), ((), ())),
+            preferred_element_type=F32,
+        )
+        at_ref[:, used * k : used * (k + pair)] = jnp.where(row == column, grown, 0.0).astype(BF16)
 
 
 def row_of_share(column):
     return 16 * (column % 16) + column // 16
 
 
-def middle_body(band_ref, r_ref, p_ref, w_hbm, mine_ref, other_ref, gs_ref, out_ref, sg_ref, w_ref, sems):
+def middle_body(
+    band_ref, r_ref, p_ref, at_ref, w_hbm, mine_ref, other_ref, gs_ref, sg_ref, w_ref, mixed_ref, back_ref, sems
+):
     copies = fetch([w_hbm.at[k] for k in range(K)], [w_ref.at[k] for k in range(K)], sems)
     keep = low_half((M16, 128))
     for o in range(HOUT):
@@ -273,39 +290,26 @@
         [r_ref[:, h, M16:CHUNK_MID, :].reshape(width, 128) for h in range(2)], axis=1
     )
     lane_mode = lax.broadcasted_iota(jnp.int32, (16, width), 1) % M12
-    diagonal = (
-        lax.broadcasted_iota(jnp.int32, (width, used), 0) % M12
-        == lax.broadcasted_iota(jnp.int32, (width, used), 1) // 16
-    )
-    spread = one_hot((16, used), lambda column: column % 16)
     low = band_ref[0, 0] == 0
 
     for k in range(K):
         placed = p_ref[16 * k : 16 * (k + 1), :]
         blocks = [jnp.where(lane_mode == m, placed, 0.0).astype(BF16) for m in range(M12)]
         mixed = dot(jnp.concatenate(blocks, axis=0), x).astype(BF16)
-        copies[k].wait()
-        out_now = dot(mixed, w_ref[k])
+        mixed_ref[:, C * k : C * (k + 1)] = mixed
         grad = lax.dot_general(mixed, gs, (((0,), (0,)), ((), ())), preferred_element_type=F32)
         where_to = (slice(None), slice(CHUNK_MID + 16 * k, CHUNK_MID + 16 * (k + 1)), slice(None))
         shape = (LANES, 16, 128)
         mine_ref[where_to] = jnp.where(low, grad[:, :128], grad[:, 128:]).astype(BF16).reshape(shape)
         other_ref[where_to] = jnp.where(low, grad[:, 128:], grad[:, :128]).astype(BF16).reshape(shape)
+        copies[k].wait()
         back = lax.dot_general(gs, w_ref[k], (((1,), (1,)), ((), ())), preferred_element_type=F32)
-        grown = lax.dot_general(
-            placed.astype(BF16), spread, (((0,), (0,)), ((), ())), preferred_element_type=F32
-        )
-        sg_now = dot(jnp.where(diagonal, grown, 0.0).astype(BF16), back.astype(BF16))
-        if k == 0:
-            out_ref[...] = out_now
-            sg_ref[...] = sg_now
-        else:
-            out_ref[...] += out_now
-            sg_ref[...] += sg_now
-
+        back_ref[used * k : used * (k + 1), :] = back.astype(BF16)
+    out = dot(mixed_ref[...], w_ref[...].reshape(K * C, C)).astype(BF16)
+    sg_ref[...] = dot(at_ref[...], back_ref[...])
     ordered = lax.dot_general(
         one_hot((used, 256), row_of_share),
-        out_ref[...].astype(BF16),
+        out,
         (((0,), (0,)), ((), ())),
         preferred_element_type=F32,
     )
@@ -328,14 +332,21 @@
             other_ref[a, rows, :] = jnp.where(low, second, first).astype(BF16)
 
 
-def merge_body(band_ref, mine_ref, got_ref, o_ref):
+def merge_body(band_ref, mine_ref, got_ref, o_hbm, o_ref, sems):
     low = band_ref[0, 0] == 0
+    copies = []
     for a in range(LANES):
         mine, got = mine_ref[a, 0:CHUNK_MID, :].astype(F32), got_ref[a, 0:CHUNK_MID, :].astype(F32)
         o_ref[a, 0:CHUNK_MID, :] = jnp.where(low, mine, got).astype(BF16)
         o_ref[a, CHUNK_MID : 2 * CHUNK_MID, :] = jnp.where(low, got, mine).astype(BF16)
         mine, got = mine_ref[a, CHUNK_MID:, :].astype(F32), got_ref[a, CHUNK_MID:, :].astype(F32)
         o_ref[a, 2 * CHUNK_MID :, :] = (mine + got).astype(BF16)
+        if a % 4 == 3:
+            part = slice(a - 3, a + 1)
+            copies.append(pltpu.make_async_copy(o_ref.at[part], o_hbm.at[part], sems.at[a // 4]))
+            copies[-1].start()
+    for copy in copies:
+        copy.wait()
 
 
 def fields_body(r_ref, w_ref, v_ref, o_ref):
@@ -437,25 +448,35 @@
     (sent,) = call(spectra_body, [VMEM] * 3, [((SHARES, CHUNK_MID, 128), BF16)], flops=300 << 20)(landed, flat, inv_t)
     landed = lax.all_to_all(sent, JOINT, split_axis=0, concat_axis=0, tiled=True)
     mine, got, sent = lax.optimization_barrier((mine, got, sent))
-    (placed,) = call(mixing_body, [SMEM, VMEM, VMEM], [((K * 16, HIN * 2 * M12), F32)])(spot, mine, got)
+    placed, mix_t = call(
+        mixing_body, [SMEM, VMEM, VMEM], [((K * 16, HIN * 2 * M12), F32), ((HIN * 2 * M12, K * 192), BF16)]
+    )(spot, mine, got)
 
     chunk = (LANES, CHUNK_MID + 16 * K, 128)
     mine, other = call(
         middle_body,
-        [SMEM, VMEM, VMEM, HBM],
+        [SMEM, VMEM, VMEM, VMEM, HBM],
         [(chunk, BF16), (chunk, BF16)],
         flops=2 << 30,
         nbytes=3 << 20,
         scratch=[
             pltpu.VMEM((256, 256), BF16),
-            pltpu.VMEM((192, 256), F32),
             pltpu.VMEM((384, 256), F32),
             pltpu.VMEM((K, 256, 256), BF16),
+            pltpu.VMEM((192, K * C), BF16),
+            pltpu.VMEM((K * 192, 256), BF16),
             dma((K,)),
         ],
-    )(spot, landed.reshape(HIN, 2, CHUNK_MID, 128), placed, in_hbm(weights))
+    )(spot, landed.reshape(HIN, 2, CHUNK_MID, 128), placed, mix_t, in_hbm(weights))
     got = swap_bands(other)
-    (sent,) = call(merge_body, [SMEM, VMEM, VMEM], [((LANES, CHUNK_OUT, 128), BF16)], nbytes=2 << 20)(spot, mine, got)
+    (sent,) = call(
+        merge_body,
+        [SMEM, VMEM, VMEM],
+        [((LANES, CHUNK_OUT, 128), BF16)],
+        nbytes=2 << 20,
+        scratch=[pltpu.VMEM((LANES, CHUNK_OUT, 128), BF16), dma((4,))],
+        out_place=HBM,
+    )(spot, mine, got)
     landed = lax.all_to_all(sent, "azimuth", split_axis=0, concat_axis=0, tiled=True)
 
     factors, sent = lax.optimization_barrier((factors, sent))
@@ -475,13 +496,16 @@
         pairs = [(i, i ^ (2 * member_bit + band_bit)) for i in range(2 * members)]
         return lax.ppermute(value, ("ens", "polar"), pairs)
 
-    half = jnp.sum(landed[:, 2 * CHUNK_MID :, :].astype(F32), axis=0)
-    half = half + partner(half, 4, 0)
-    half = half + partner(half, 2, 0)
-    far = partner(half, 1, 1)
-    near = partner(half, 1, 0)
-    far = far + partner(half, 0, 1)
-    half = half + near
+    half = jnp.sum(landed[:, 2 * CHUNK_MID :, :].astype(F32), axis=0).astype(BF16)
+    got = partner(half, 1, 0)
+    half = (half.astype(F32) + got.astype(F32)).astype(BF16)
+    got = partner(half, 4, 0)
+    half = (half.astype(F32) + got.astype(F32)).astype(BF16)
+    cross = partner(half, 2, 1)
+    near = partner(half, 2, 0)
+    far = partner(half, 0, 1)
+    far = far.astype(F32) + cross.astype(F32)
+    half = half.astype(F32) + near.astype(F32)
     (sent,) = call(fields_body, [VMEM] * 3, [((LANES, CHUNK_IN, 128), BF16)], flops=300 << 20)(landed, tall, inv)
     landed = lax.all_to_all(sent, "azimuth", split_axis=0, concat_axis=0, tiled=True)
     weight_grad = jnp.concatenate([jnp.where(low, half, far), jnp.where(low, far, half)], axis=1)

time: 95 us -> 94.2 us (level)
  waiting for transfers between devices: 36.3 us -> 34.1 us
  Pallas kernels: 21.2 us -> 22.4 us
    ppermute x5, waiting for transfers between devices: 6.54 us -> 5.11 us  [partner(): return lax.ppermute(value, ('ens', 'polar'), pairs)]
    pallas_call x2, Pallas kernels: 7 us -> 8.21 us  [the longest x1 6.27 us: local(): call(middle_body, [SMEM, VMEM, VMEM, VMEM, HBM], [(chunk, BF16), (chunk,...]
where the time goes in v4:
time: 94.2 us; the launch traced here: 93.6 us
  starting transfers between devices  35.3 us (37%)
  waiting for transfers between devices  34.1 us (36%)
  Pallas kernels  22.4 us (24%)
    all_to_all x3, waiting for transfers between devices, local(): lax.all_to_all(sent, 'azimuth', split_axis=0, concat_axis=0, tiled=True)  20.1 us
    all_to_all x3, starting transfers between devices, local(): lax.all_to_all(sent, 'azimuth', split_axis=0, concat_axis=0, tiled=True)  17.6 us
    ppermute x5, starting transfers between devices, partner(): return lax.ppermute(value, ('ens', 'polar'), pairs)  12.6 us
    all_to_all x1, waiting for transfers between devices, local(): lax.all_to_all(sent, JOINT, split_axis=0, concat_axis=0, tiled=True)  6.68 us
    pallas_call x1, Pallas kernels, local(): call(middle_body, [SMEM, VMEM, VMEM, VMEM, HBM], [(chunk, BF16), (chunk,...  6.27 us
    ppermute x5, waiting for transfers between devices, partner(): return lax.ppermute(value, ('ens', 'polar'), pairs)  5.11 us
    all_to_all x1, starting transfers between devices, local(): lax.all_to_all(sent, JOINT, split_axis=0, concat_axis=0, tiled=True)  4.99 us
    pallas_call x1, Pallas kernels, local(): call(flipped_table_body, [HBM] * 8, [((2, 384, 768), BF16), ((2, 512, 384...  2.59 us
  transfers between devices with their start and end apart: 11, of which 8 were waited for; matrix products, arithmetic and copies ran while one was open for 1% of the time, Pallas kernels for 10%

profile of v4, /device:TPU:2, one launch (start us, length us, event | category | flops | bytes accessed | tf_op | source)
XLA Modules:
  0.0 93.6 jit_solution(16322907275866749649)
XLA Ops:
  0.6 2.3 %shard_map.148 = bf16[16,120,128]{2,1,0:T(8,128)(2,1)} custom-call(bf16[720,256]{1,0:T(8,128)(2,1)} %bitcast.26, bf16[45,4,256]{2,1,0:T(4,128)(2,1)} %bitcast.29), custom_call_target="tpu_custom_call" | custom-call | bytes 1048576 | tf_op jit(solution)/shard_map/pallas_call | solution.py:413
  3.0 7.5 %all-to-all-start = ((bf16[16,120,128]{2,1,0:T(8,128)(2,1)}), bf16[16,120,128]{2,1,0:T(8,128)(2,1)S(1)}, u32[]{:S(2)}, u32[]{:S(2)}) async-start(bf16[16,120,128]{2,1,0:T(8,128)(2,1)} %shard_map.148), calls=%async_computation | async-start | bytes 983040 | tf_op jit(solution)/shard_map/all_to_all | solution.py:426
  10.6 1.9 %shard_map.149 = (bf16[180,128]{1,0:T(8,128)(2,1)S(1)}, bf16[180,128]{1,0:T(8,128)(2,1)S(1)}) custom-call(s32[1,2]{1,0:T(1,128)S(1)} %add_bitcast_fusion.spot_ref.band_ref, s32[4,2]{1,0:T(4,128)S(1)} %copy.16.support_ref, bf16[45,4,720]{2,1,0:T(4,128)(2,1)} %bitcast.27), custom_call_target="tpu_custom_call" | custom-call | bytes 1048576 | tf_op jit(solution)/shard_map/pallas_call | solution.py:429
  12.6 2.6 %shard_map.150 = (bf16[2,384,768]{2,1,0:T(8,128)(2,1)S(1)}, bf16[2,512,384]{2,1,0:T(8,128)(2,1)S(1)}) custom-call(f32[2,8,384]{2,1,0:T(8,128)} %constant.30.clone.refs_0_, f32[2,8,384]{2,1,0:T(8,128)} %constant.31.clone.refs_1_, f32[2,96,384]{2,1,0:T(8,128)} %constant.32.clone.refs_2_, f32[2,96,384]{2,1,0:T(8,128)} %constant.33.clone.refs_3_, ...), custom_call_target="tpu_custom_call" | custom-call | bytes 5242880 | tf_op jit(solution)/shard_map/pallas_call | solution.py:439
  15.2 5.1 %all-to-all-done.r_ref = bf16[16,120,128]{2,1,0:T(8,128)(2,1)S(1)} async-done(((bf16[16,120,128]{2,1,0:T(8,128)(2,1)}), bf16[16,120,128]{2,1,0:T(8,128)(2,1)S(1)}, u32[]{:S(2)}, u32[]{:S(2)}) %all-to-all-start) | async-done | bytes 491552 | tf_op jit(solution)/shard_map/all_to_all | solution.py:426
  20.3 1.5 %shard_map.151 = bf16[32,40,128]{2,1,0:T(8,128)(2,1)} custom-call(bf16[16,120,128]{2,1,0:T(8,128)(2,1)S(1)} %all-to-all-done.r_ref, bf16[2,384,768]{2,1,0:T(8,128)(2,1)S(1)} %get-tuple-element.54.wt_ref, bf16[2,512,384]{2,1,0:T(8,128)(2,1)S(1)} %get-tuple-element.55.vt_ref), custom_call_target="tpu_custom_call" | custom-call | flops 314572800 | bytes 1048576 | tf_op jit(solution)/shard_map/pallas_call | solution.py:448
  21.8 5.0 %all-to-all-start.1 = ((bf16[32,40,128]{2,1,0:T(8,128)(2,1)}), bf16[32,40,128]{2,1,0:T(8,128)(2,1)S(1)}, u32[]{:S(2)}, u32[]{:S(2)}) async-start(bf16[32,40,128]{2,1,0:T(8,128)(2,1)} %shard_map.151), calls=%async_computation.1 | async-start | bytes 655360 | tf_op jit(solution)/shard_map/all_to_all | solution.py:449
  26.7 1.9 %shard_map.152 = (f32[144,384]{1,0:T(8,128)S(1)}, bf16[384,1728]{1,0:T(8,128)(2,1)S(1)}) custom-call(s32[1,2]{1,0:T(1,128)S(1)} %add_bitcast_fusion.spot_ref.band_ref, bf16[180,128]{1,0:T(8,128)(2,1)S(1)} %get-tuple-element.58.mine_ref, bf16[180,128]{1,0:T(8,128)(2,1)S(1)} %collective-permute-done.got_ref), custom_call_target="tpu_custom_call" | custom-call | bytes 1048576 | tf_op jit(solution)/shard_map/pallas_call | solution.py:451
  28.7 6.7 %all-to-all-done.1 = bf16[32,40,128]{2,1,0:T(8,128)(2,1)S(1)} async-done(((bf16[32,40,128]{2,1,0:T(8,128)(2,1)}), bf16[32,40,128]{2,1,0:T(8,128)(2,1)S(1)}, u32[]{:S(2)}, u32[]{:S(2)}) %all-to-all-start.1) | async-done | bytes 327712 | tf_op jit(solution)/shard_map/all_to_all | solution.py:449
  35.4 6.3 %shard_map.153 = (bf16[16,184,128]{2,1,0:T(8,128)(2,1)S(1)}, bf16[16,184,128]{2,1,0:T(8,128)(2,1)S(1)}) custom-call(s32[1,2]{1,0:T(1,128)S(1)} %add_bitcast_fusion.spot_ref.band_ref, bf16[16,2,40,128]{3,2,1,0:T(8,128)(2,1)S(1)} %bitcast.25, f32[144,384]{1,0:T(8,128)S(1)} %get-tuple-element.60.p_ref, bf16[384,1728]{1,0:T(8,128)(2,1)S(1)} %get-tuple-element.61.at_ref, ...), custom_call_target="tpu_custom_call" | custom-call | flops 2147483648 | bytes 3145728 | tf_op jit(solution)/shard_map/pallas_call | solution.py:456
  41.7 2.2 %collective-permute-done.1.got_ref = bf16[16,184,128]{2,1,0:T(8,128)(2,1)S(1)} collective-permute-done((bf16[16,184,128]{2,1,0:T(8,128)(2,1)S(1)}, bf16[16,184,128]{2,1,0:T(8,128)(2,1)S(1)}, u32[]{:S(2)}, u32[]{:S(2)}) %collective-permute-start.1) | collective-permute-done | bytes 753696 | tf_op jit(solution)/shard_map/ppermute | solution.py:404
  44.0 1.6 %shard_map.154 = bf16[16,224,128]{2,1,0:T(8,128)(2,1)} custom-call(s32[1,2]{1,0:T(1,128)S(1)} %add_bitcast_fusion.spot_ref.band_ref, bf16[16,184,128]{2,1,0:T(8,128)(2,1)S(1)} %get-tuple-element.62.mine_ref, bf16[16,184,128]{2,1,0:T(8,128)(2,1)S(1)} %collective-permute-done.1.got_ref), custom_call_target="tpu_custom_call" | custom-call | bytes 2097152 | tf_op jit(solution)/shard_map/pallas_call | solution.py:472
  45.5 5.0 %all-to-all-start.2 = ((bf16[16,224,128]{2,1,0:T(8,128)(2,1)}), bf16[16,224,128]{2,1,0:T(8,128)(2,1)S(1)}, u32[]{:S(2)}, u32[]{:S(2)}) async-start(bf16[16,224,128]{2,1,0:T(8,128)(2,1)} %shard_map.154), calls=%async_computation.2 | async-start | bytes 1835008 | tf_op jit(solution)/shard_map/all_to_all | solution.py:480
  50.5 1.8 %shard_map.155 = (bf16[2,768,384]{2,1,0:T(8,128)(2,1)S(1)}, bf16[2,384,512]{2,1,0:T(8,128)(2,1)S(1)}) custom-call(f32[2,8,384]{2,1,0:T(8,128)} %constant.30.clone.refs_0_, f32[2,8,384]{2,1,0:T(8,128)} %constant.31.clone.refs_1_, f32[2,96,384]{2,1,0:T(8,128)} %constant.32.clone.refs_2_, f32[2,96,384]{2,1,0:T(8,128)} %constant.33.clone.refs_3_, ...), custom_call_target="tpu_custom_call" | custom-call | bytes 5242880 | tf_op jit(solution)/shard_map/pallas_call | solution.py:483
  52.4 13.3 %all-to-all-done.2.r_ref = bf16[16,224,128]{2,1,0:T(8,128)(2,1)S(1)} async-done(((bf16[16,224,128]{2,1,0:T(8,128)(2,1)}), bf16[16,224,128]{2,1,0:T(8,128)(2,1)S(1)}, u32[]{:S(2)}, u32[]{:S(2)}) %all-to-all-start.2) | async-done | bytes 917536 | tf_op jit(solution)/shard_map/all_to_all | solution.py:480
  65.7 2.0 %collective-permute-start.2 = (bf16[144,128]{1,0:T(8,128)(2,1)S(1)}, bf16[144,128]{1,0:T(8,128)(2,1)S(1)}, u32[]{:S(2)}, u32[]{:S(2)}) collective-permute-start(bf16[144,128]{1,0:T(8,128)(2,1)S(1)} %slice_reduce_fusion), channel_id=1, source_target_pairs={{0,32},{16,48},{32,0},{48,16},{64,96},{80,112},{96,64},{112,80},{1... | collective-permute-start | bytes 110600 | tf_op jit(solution)/shard_map/ppermute | solution.py:497
  67.7 2.1 %collective-permute-done.2 = bf16[144,128]{1,0:T(8,128)(2,1)S(1)} collective-permute-done((bf16[144,128]{1,0:T(8,128)(2,1)S(1)}, bf16[144,128]{1,0:T(8,128)(2,1)S(1)}, u32[]{:S(2)}, u32[]{:S(2)}) %collective-permute-start.2) | collective-permute-done | bytes 36896 | tf_op jit(solution)/shard_map/ppermute | solution.py:497
  69.8 7.4 %collective-permute-start.3 = (bf16[144,128]{1,0:T(8,128)(2,1)S(1)}, bf16[144,128]{1,0:T(8,128)(2,1)S(1)}, u32[]{:S(2)}, u32[]{:S(2)}) collective-permute-start(bf16[144,128]{1,0:T(8,128)(2,1)S(1)} %add_convert_fusion.1), channel_id=1, source_target_pairs={{0,128},{16,144},{32,160},{48,176},{64,192},{80,208},{96,224},{112... | collective-permute-start | bytes 110600 | tf_op jit(solution)/shard_map/ppermute | solution.py:497
  77.2 1.5 %shard_map.156 = bf16[16,120,128]{2,1,0:T(8,128)(2,1)} custom-call(bf16[16,224,128]{2,1,0:T(8,128)(2,1)S(1)} %all-to-all-done.2.r_ref, bf16[2,768,384]{2,1,0:T(8,128)(2,1)S(1)} %get-tuple-element.75.w_ref, bf16[2,384,512]{2,1,0:T(8,128)(2,1)S(1)} %get-tuple-element.76.v_ref), custom_call_target="tpu_custom_call" | custom-call | flops 314572800 | bytes 1048576 | tf_op jit(solution)/shard_map/pallas_call | solution.py:509
  78.7 5.1 %all-to-all-start.3 = ((bf16[16,120,128]{2,1,0:T(8,128)(2,1)}), bf16[16,120,128]{2,1,0:T(8,128)(2,1)S(1)}, u32[]{:S(2)}, u32[]{:S(2)}) async-start(bf16[16,120,128]{2,1,0:T(8,128)(2,1)} %shard_map.156), calls=%async_computation.3 | async-start | bytes 983040 | tf_op jit(solution)/shard_map/all_to_all | solution.py:510
  85.1 1.8 %collective-permute-start.4 = (bf16[144,128]{1,0:T(8,128)(2,1)S(1)}, bf16[144,128]{1,0:T(8,128)(2,1)S(1)}, u32[]{:S(2)}, u32[]{:S(2)}) collective-permute-start(bf16[144,128]{1,0:T(8,128)(2,1)S(1)} %add_convert_fusion), channel_id=1, source_target_pairs={{0,64},{16,80},{32,96},{48,112},{64,0},{80,16},{96,32},{112,48},{1... | collective-permute-start | bytes 110600 | tf_op jit(solution)/shard_map/ppermute | solution.py:497
  86.9 1.2 %collective-permute-done.6 = bf16[144,128]{1,0:T(8,128)(2,1)S(1)} collective-permute-done((bf16[144,128]{1,0:T(8,128)(2,1)S(1)}, bf16[144,128]{1,0:T(8,128)(2,1)S(1)}, u32[]{:S(2)}, u32[]{:S(2)}) %collective-permute-start.6) | collective-permute-done | bytes 36896 | tf_op jit(solution)/shard_map/ppermute | solution.py:497
  88.2 1.8 %collective-permute-done.4 = bf16[144,128]{1,0:T(8,128)(2,1)S(1)} collective-permute-done((bf16[144,128]{1,0:T(8,128)(2,1)S(1)}, bf16[144,128]{1,0:T(8,128)(2,1)S(1)}, u32[]{:S(2)}, u32[]{:S(2)}) %collective-permute-start.4) | collective-permute-done | bytes 36896 | tf_op jit(solution)/shard_map/ppermute | solution.py:497
  90.7 1.8 %all-to-all-done.3.r_ref = bf16[16,120,128]{2,1,0:T(8,128)(2,1)S(1)} async-done(((bf16[16,120,128]{2,1,0:T(8,128)(2,1)}), bf16[16,120,128]{2,1,0:T(8,128)(2,1)S(1)}, u32[]{:S(2)}, u32[]{:S(2)}) %all-to-all-start.3) | async-done | bytes 491552 | tf_op jit(solution)/shard_map/all_to_all | solution.py:510
  (17 shorter events, 3.6 us)
Async XLA Ops:
  0.6 9.8 %copy-start = (s32[4,2]{0,1:T(2,128)S(1)}, s32[4,2]{0,1:T(2,128)}, u32[]{:S(2)}) copy-start(s32[4,2]{0,1:T(2,128)} %param.15) | copy-start | bytes 100
  3.0 17.3 %all-to-all-start = ((bf16[16,120,128]{2,1,0:T(8,128)(2,1)}), bf16[16,120,128]{2,1,0:T(8,128)(2,1)S(1)}, u32[]{:S(2)}, u32[]{:S(2)}) async-start(bf16[16,120,128]{2,1,0:T(8,128)(2,1)} %shard_map.148), calls=%async_computation | async-start | bytes 983040 | tf_op jit(solution)/shard_map/all_to_all | solution.py:426
  12.5 2.7 %collective-permute-start = (bf16[180,128]{1,0:T(8,128)(2,1)S(1)}, bf16[180,128]{1,0:T(8,128)(2,1)S(1)}, u32[]{:S(2)}, u32[]{:S(2)}) collective-permute-start(bf16[180,128]{1,0:T(8,128)(2,1)S(1)} %get-tuple-element.44), channel_id=1, source_target_pairs={{0,16},{16,0},{1,17},{17,1},{2,18},{18,2},{3,19},{19,3},{4,20},{20... | collective-permute-start | bytes 138248 | tf_op jit(solution)/shard_map/ppermute | solution.py:404
  21.8 13.6 %all-to-all-start.1 = ((bf16[32,40,128]{2,1,0:T(8,128)(2,1)}), bf16[32,40,128]{2,1,0:T(8,128)(2,1)S(1)}, u32[]{:S(2)}, u32[]{:S(2)}) async-start(bf16[32,40,128]{2,1,0:T(8,128)(2,1)} %shard_map.151), calls=%async_computation.1 | async-start | bytes 655360 | tf_op jit(solution)/shard_map/all_to_all | solution.py:449
  41.6 2.3 %collective-permute-start.1 = (bf16[16,184,128]{2,1,0:T(8,128)(2,1)S(1)}, bf16[16,184,128]{2,1,0:T(8,128)(2,1)S(1)}, u32[]{:S(2)}, u32[]{:S(2)}) collective-permute-start(bf16[16,184,128]{2,1,0:T(8,128)(2,1)S(1)} %get-tuple-element.63), channel_id=1, source_target_pairs={{0,16},{16,0},{1,17},{17,1},{2,18},{18,2},{3,19},{19,3},{4,20},{20... | collective-permute-start | bytes 2261000 | tf_op jit(solution)/shard_map/ppermute | solution.py:404
  45.5 20.1 %all-to-all-start.2 = ((bf16[16,224,128]{2,1,0:T(8,128)(2,1)}), bf16[16,224,128]{2,1,0:T(8,128)(2,1)S(1)}, u32[]{:S(2)}, u32[]{:S(2)}) async-start(bf16[16,224,128]{2,1,0:T(8,128)(2,1)} %shard_map.154), calls=%async_computation.2 | async-start | bytes 1835008 | tf_op jit(solution)/shard_map/all_to_all | solution.py:480
  65.7 4.0 %collective-permute-start.2 = (bf16[144,128]{1,0:T(8,128)(2,1)S(1)}, bf16[144,128]{1,0:T(8,128)(2,1)S(1)}, u32[]{:S(2)}, u32[]{:S(2)}) collective-permute-start(bf16[144,128]{1,0:T(8,128)(2,1)S(1)} %slice_reduce_fusion), channel_id=1, source_target_pairs={{0,32},{16,48},{32,0},{48,16},{64,96},{80,112},{96,64},{112,80},{1... | collective-permute-start | bytes 110600 | tf_op jit(solution)/shard_map/ppermute | solution.py:497
  69.8 14.0 %collective-permute-start.3 = (bf16[144,128]{1,0:T(8,128)(2,1)S(1)}, bf16[144,128]{1,0:T(8,128)(2,1)S(1)}, u32[]{:S(2)}, u32[]{:S(2)}) collective-permute-start(bf16[144,128]{1,0:T(8,128)(2,1)S(1)} %add_convert_fusion.1), channel_id=1, source_target_pairs={{0,128},{16,144},{32,160},{48,176},{64,192},{80,208},{96,224},{112... | collective-permute-start | bytes 110600 | tf_op jit(solution)/shard_map/ppermute | solution.py:497
  78.7 13.8 %all-to-all-start.3 = ((bf16[16,120,128]{2,1,0:T(8,128)(2,1)}), bf16[16,120,128]{2,1,0:T(8,128)(2,1)S(1)}, u32[]{:S(2)}, u32[]{:S(2)}) async-start(bf16[16,120,128]{2,1,0:T(8,128)(2,1)} %shard_map.156), calls=%async_computation.3 | async-start | bytes 983040 | tf_op jit(solution)/shard_map/all_to_all | solution.py:510
  83.8 4.4 %collective-permute-start.6 = (bf16[144,128]{1,0:T(8,128)(2,1)S(1)}, bf16[144,128]{1,0:T(8,128)(2,1)S(1)}, u32[]{:S(2)}, u32[]{:S(2)}) collective-permute-start(bf16[144,128]{1,0:T(8,128)(2,1)S(1)} %add_convert_fusion), channel_id=1, source_target_pairs={{0,80},{16,64},{32,112},{48,96},{64,16},{80,0},{96,48},{112,32},{1... | collective-permute-start | bytes 110600 | tf_op jit(solution)/shard_map/ppermute | solution.py:497
  83.9 4.3 %collective-permute-start.5 = (bf16[144,128]{1,0:T(8,128)(2,1)S(1)}, bf16[144,128]{1,0:T(8,128)(2,1)S(1)}, u32[]{:S(2)}, u32[]{:S(2)}) collective-permute-start(bf16[144,128]{1,0:T(8,128)(2,1)S(1)} %add_convert_fusion), channel_id=1, source_target_pairs={{0,16},{16,0},{32,48},{48,32},{64,80},{80,64},{96,112},{112,96},{1... | collective-permute-start | bytes 110600 | tf_op jit(solution)/shard_map/ppermute | solution.py:497
  85.1 4.9 %collective-permute-start.4 = (bf16[144,128]{1,0:T(8,128)(2,1)S(1)}, bf16[144,128]{1,0:T(8,128)(2,1)S(1)}, u32[]{:S(2)}, u32[]{:S(2)}) collective-permute-start(bf16[144,128]{1,0:T(8,128)(2,1)S(1)} %add_convert_fusion), channel_id=1, source_target_pairs={{0,64},{16,80},{32,96},{48,112},{64,0},{80,16},{96,32},{112,48},{1... | collective-permute-start | bytes 110600 | tf_op jit(solution)/shard_map/ppermute | solution.py:497

commit v5 on v3

--- a/solution.py
+++ b/solution.py
@@ -60,12 +60,12 @@
 SMEM = pl.BlockSpec(memory_space=pltpu.SMEM)
 
 
-def call(body, places, outs, flops=0, scratch=(), nbytes=1 << 20, vmem=16):
+def call(body, places, outs, flops=0, scratch=(), nbytes=1 << 20, vmem=16, out_place=VMEM):
     return pl.pallas_call(
         body,
         out_shape=[jax.ShapeDtypeStruct(s, d) for s, d in outs],
         in_specs=places,
-        out_specs=[VMEM] * len(outs),
+        out_specs=[out_place] * len(outs),
         scratch_shapes=list(scratch),
         compiler_params=pltpu.CompilerParams(vmem_limit_bytes=vmem << 20),
         cost_estimate=pl.CostEstimate(flops=flops, bytes_accessed=nbytes, transcendentals=0),
@@ -222,7 +222,8 @@
     other_ref[...] = swap64(got).astype(BF16)
 
 
-def mixing_body(spot_ref, mine_ref, got_ref, p_ref):
+def mixing_body(spot_ref, mine_ref, got_ref, w_hbm, p_ref, w_ref, sems):
+    (copy,) = fetch((w_hbm,), (w_ref,), sems)
     rows, width, count = K * 16, HIN * 2 * M12, K * SUPPORT * 4
     low = spot_ref[0, 0] == 0
     mine, got = mine_ref[...].astype(F32), got_ref[...].astype(F32)
@@ -250,14 +251,14 @@
             collect = jnp.where(key == 8 * half + ri, 1.0, 0.0).astype(BF16)
             total = total + dot(collect, spread)
     p_ref[...] = total
+    copy.wait()
 
 
 def row_of_share(column):
     return 16 * (column % 16) + column // 16
 
 
-def middle_body(band_ref, r_ref, p_ref, w_hbm, mine_ref, other_ref, gs_ref, out_ref, sg_ref, w_ref, sems):
-    copies = fetch([w_hbm.at[k] for k in range(K)], [w_ref.at[k] for k in range(K)], sems)
+def middle_body(band_ref, r_ref, p_ref, w_ref, mine_ref, other_ref, gs_ref, out_ref, sg_ref):
     keep = low_half((M16, 128))
     for o in range(HOUT):
         for i in range(2):
@@ -284,7 +285,6 @@
         placed = p_ref[16 * k : 16 * (k + 1), :]
         blocks = [jnp.where(lane_mode == m, placed, 0.0).astype(BF16) for m in range(M12)]
         mixed = dot(jnp.concatenate(blocks, axis=0), x).astype(BF16)
-        copies[k].wait()
         out_now = dot(mixed, w_ref[k])
         grad = lax.dot_general(mixed, gs, (((0,), (0,)), ((), ())), preferred_element_type=F32)
         where_to = (slice(None), slice(CHUNK_MID + 16 * k, CHUNK_MID + 16 * (k + 1)), slice(None))
@@ -328,14 +328,21 @@
             other_ref[a, rows, :] = jnp.where(low, second, first).astype(BF16)
 
 
-def merge_body(band_ref, mine_ref, got_ref, o_ref):
+def merge_body(band_ref, mine_ref, got_ref, o_hbm, o_ref, sems):
     low = band_ref[0, 0] == 0
+    copies = []
     for a in range(LANES):
         mine, got = mine_ref[a, 0:CHUNK_MID, :].astype(F32), got_ref[a, 0:CHUNK_MID, :].astype(F32)
         o_ref[a, 0:CHUNK_MID, :] = jnp.where(low, mine, got).astype(BF16)
         o_ref[a, CHUNK_MID : 2 * CHUNK_MID, :] = jnp.where(low, got, mine).astype(BF16)
         mine, got = mine_ref[a, CHUNK_MID:, :].astype(F32), got_ref[a, CHUNK_MID:, :].astype(F32)
         o_ref[a, 2 * CHUNK_MID :, :] = (mine + got).astype(BF16)
+        if a % 4 == 3:
+            part = slice(a - 3, a + 1)
+            copies.append(pltpu.make_async_copy(o_ref.at[part], o_hbm.at[part], sems.at[a // 4]))
+            copies[-1].start()
+    for copy in copies:
+        copy.wait()
 
 
 def fields_body(r_ref, w_ref, v_ref, o_ref):
@@ -437,12 +444,14 @@
     (sent,) = call(spectra_body, [VMEM] * 3, [((SHARES, CHUNK_MID, 128), BF16)], flops=300 << 20)(landed, flat, inv_t)
     landed = lax.all_to_all(sent, JOINT, split_axis=0, concat_axis=0, tiled=True)
     mine, got, sent = lax.optimization_barrier((mine, got, sent))
-    (placed,) = call(mixing_body, [SMEM, VMEM, VMEM], [((K * 16, HIN * 2 * M12), F32)])(spot, mine, got)
+    placed, staged = call(
+        mixing_body, [SMEM, VMEM, VMEM, HBM], [((K * 16, HIN * 2 * M12), F32), ((K, C, C), BF16)], scratch=[dma((1,))]
+    )(spot, mine, got, in_hbm(weights))
 
     chunk = (LANES, CHUNK_MID + 16 * K, 128)
     mine, other = call(
         middle_body,
-        [SMEM, VMEM, VMEM, HBM],
+        [SMEM, VMEM, VMEM, VMEM],
         [(chunk, BF16), (chunk, BF16)],
         flops=2 << 30,
         nbytes=3 << 20,
@@ -450,12 +459,17 @@
             pltpu.VMEM((256, 256), BF16),
             pltpu.VMEM((192, 256), F32),
             pltpu.VMEM((384, 256), F32),
-            pltpu.VMEM((K, 256, 256), BF16),
-            dma((K,)),
         ],
-    )(spot, landed.reshape(HIN, 2, CHUNK_MID, 128), placed, in_hbm(weights))
+    )(spot, landed.reshape(HIN, 2, CHUNK_MID, 128), placed, staged)
     got = swap_bands(other)
-    (sent,) = call(merge_body, [SMEM, VMEM, VMEM], [((LANES, CHUNK_OUT, 128), BF16)], nbytes=2 << 20)(spot, mine, got)
+    (sent,) = call(
+        merge_body,
+        [SMEM, VMEM, VMEM],
+        [((LANES, CHUNK_OUT, 128), BF16)],
+        nbytes=2 << 20,
+        scratch=[pltpu.VMEM((LANES, CHUNK_OUT, 128), BF16), dma((4,))],
+        out_place=HBM,
+    )(spot, mine, got)
     landed = lax.all_to_all(sent, "azimuth", split_axis=0, concat_axis=0, tiled=True)
 
     factors, sent = lax.optimization_barrier((factors, sent))
@@ -471,17 +485,19 @@
 
     members = lax.axis_size("ens")
 
-    def partner(value, member_bit, band_bit):
-        pairs = [(i, i ^ (2 * member_bit + band_bit)) for i in range(2 * members)]
-        return lax.ppermute(value, ("ens", "polar"), pairs)
-
-    half = jnp.sum(landed[:, 2 * CHUNK_MID :, :].astype(F32), axis=0)
-    half = half + partner(half, 4, 0)
-    half = half + partner(half, 2, 0)
-    far = partner(half, 1, 1)
-    near = partner(half, 1, 0)
-    far = far + partner(half, 0, 1)
-    half = half + near
+    def send(value, offset_even, offset_odd):
+        offsets = (offset_even, offset_odd)
+        pairs = [(i, (i + offsets[i % 2]) % members) for i in range(members)]
+        return lax.ppermute(value, "ens", pairs)
+
+    half = jnp.sum(landed[:, 2 * CHUNK_MID :, :].astype(F32), axis=0).astype(BF16)
+    got = send(half, 1, -1)
+    pair = (half.astype(F32) + got.astype(F32)).astype(BF16)
+    beside = send(pair, -1, 1)
+    across = send(beside, 2, -2)
+    behind = send(beside, 1, -1)
+    half = (pair.astype(F32) + across.astype(F32)) + (beside.astype(F32) + behind.astype(F32))
+    far = swap_bands(half)
     (sent,) = call(fields_body, [VMEM] * 3, [((LANES, CHUNK_IN, 128), BF16)], flops=300 << 20)(landed, tall, inv)
     landed = lax.all_to_all(sent, "azimuth", split_axis=0, concat_axis=0, tiled=True)
     weight_grad = jnp.concatenate([jnp.where(low, half, far), jnp.where(low, far, half)], axis=1)

time: 95 us -> 95.9 us (level); the launches traced: 94.5 us -> 94.2 us
  waiting for transfers between devices: 36.3 us -> 39.2 us
  starting transfers between devices: 35.2 us -> 33.2 us
  Pallas kernels: 21.2 us -> 20.1 us
    all_to_all x3, waiting for transfers between devices: 20.3 us -> 24.9 us  [local(): lax.all_to_all(sent, 'azimuth', split_axis=0, concat_axis=0, tiled=True)]
    ppermute x5 -> x4, waiting for transfers between devices: 6.54 us -> 4 us  [send(): return lax.ppermute(value, 'ens', pairs)]
    ppermute x5 -> x4, starting transfers between devices: 12.4 us -> 10.5 us  [send(): return lax.ppermute(value, 'ens', pairs)]
    ppermute x2 -> x3, waiting for transfers between devices: 2.23 us -> 3.47 us  [swap_bands(): return lax.ppermute(value, 'polar', [(0, 1), (1, 0)])]
    pallas_call x2, Pallas kernels: 7 us -> 5.91 us  [the longest x1 4.09 us: local(): call(middle_body, [SMEM, VMEM, VMEM, VMEM], [(chunk, BF16), (chunk, BF16)...]
where the time goes in v5:
time: 95.9 us; the launch traced here: 94.2 us
  waiting for transfers between devices  39.2 us (41%)
  starting transfers between devices  33.2 us (35%)
  Pallas kernels  20.1 us (21%)
    all_to_all x3, waiting for transfers between devices, local(): lax.all_to_all(sent, 'azimuth', split_axis=0, concat_axis=0, tiled=True)  24.9 us
    all_to_all x3, starting transfers between devices, local(): lax.all_to_all(sent, 'azimuth', split_axis=0, concat_axis=0, tiled=True)  17.4 us
    ppermute x4, starting transfers between devices, send(): return lax.ppermute(value, 'ens', pairs)  10.5 us
    all_to_all x1, waiting for transfers between devices, local(): lax.all_to_all(sent, JOINT, split_axis=0, concat_axis=0, tiled=True)  6.8 us
    all_to_all x1, starting transfers between devices, local(): lax.all_to_all(sent, JOINT, split_axis=0, concat_axis=0, tiled=True)  4.99 us
    pallas_call x1, Pallas kernels, local(): call(middle_body, [SMEM, VMEM, VMEM, VMEM], [(chunk, BF16), (chunk, BF16)...  4.09 us
    ppermute x4, waiting for transfers between devices, send(): return lax.ppermute(value, 'ens', pairs)  4 us
    ppermute x3, waiting for transfers between devices, swap_bands(): return lax.ppermute(value, 'polar', [(0, 1), (1, 0)])  3.47 us
  transfers between devices with their start and end apart: 11, of which 8 were waited for; matrix products, arithmetic and copies ran while one was open for 1% of the time, Pallas kernels for 10%

profile of v5, /device:TPU:2, one launch (start us, length us, event | category | flops | bytes accessed | tf_op | source)
XLA Modules:
  0.0 94.2 jit_solution(10950740371534655552)
XLA Ops:
  0.6 2.3 %shard_map.148 = bf16[16,120,128]{2,1,0:T(8,128)(2,1)} custom-call(bf16[720,256]{1,0:T(8,128)(2,1)} %bitcast.26, bf16[45,4,256]{2,1,0:T(4,128)(2,1)} %bitcast.29), custom_call_target="tpu_custom_call" | custom-call | bytes 1048576 | tf_op jit(solution)/shard_map/pallas_call | solution.py:409
  3.0 7.5 %all-to-all-start = ((bf16[16,120,128]{2,1,0:T(8,128)(2,1)}), bf16[16,120,128]{2,1,0:T(8,128)(2,1)S(1)}, u32[]{:S(2)}, u32[]{:S(2)}) async-start(bf16[16,120,128]{2,1,0:T(8,128)(2,1)} %shard_map.148), calls=%async_computation | async-start | bytes 983040 | tf_op jit(solution)/shard_map/all_to_all | solution.py:422
  10.6 1.9 %shard_map.149 = (bf16[180,128]{1,0:T(8,128)(2,1)S(1)}, bf16[180,128]{1,0:T(8,128)(2,1)S(1)}) custom-call(s32[1,2]{1,0:T(1,128)S(1)} %add_bitcast_fusion.spot_ref.band_ref, s32[4,2]{1,0:T(4,128)S(1)} %copy.16.support_ref, bf16[45,4,720]{2,1,0:T(4,128)(2,1)} %bitcast.27), custom_call_target="tpu_custom_call" | custom-call | bytes 1048576 | tf_op jit(solution)/shard_map/pallas_call | solution.py:425
  12.6 2.6 %shard_map.150 = (bf16[2,384,768]{2,1,0:T(8,128)(2,1)S(1)}, bf16[2,512,384]{2,1,0:T(8,128)(2,1)S(1)}) custom-call(f32[2,8,384]{2,1,0:T(8,128)} %constant.30.clone.refs_0_, f32[2,8,384]{2,1,0:T(8,128)} %constant.31.clone.refs_1_, f32[2,96,384]{2,1,0:T(8,128)} %constant.32.clone.refs_2_, f32[2,96,384]{2,1,0:T(8,128)} %constant.33.clone.refs_3_, ...), custom_call_target="tpu_custom_call" | custom-call | bytes 5242880 | tf_op jit(solution)/shard_map/pallas_call | solution.py:435
  15.2 5.1 %all-to-all-done.r_ref = bf16[16,120,128]{2,1,0:T(8,128)(2,1)S(1)} async-done(((bf16[16,120,128]{2,1,0:T(8,128)(2,1)}), bf16[16,120,128]{2,1,0:T(8,128)(2,1)S(1)}, u32[]{:S(2)}, u32[]{:S(2)}) %all-to-all-start) | async-done | bytes 491552 | tf_op jit(solution)/shard_map/all_to_all | solution.py:422
  20.3 1.5 %shard_map.151 = bf16[32,40,128]{2,1,0:T(8,128)(2,1)} custom-call(bf16[16,120,128]{2,1,0:T(8,128)(2,1)S(1)} %all-to-all-done.r_ref, bf16[2,384,768]{2,1,0:T(8,128)(2,1)S(1)} %get-tuple-element.54.wt_ref, bf16[2,512,384]{2,1,0:T(8,128)(2,1)S(1)} %get-tuple-element.55.vt_ref), custom_call_target="tpu_custom_call" | custom-call | flops 314572800 | bytes 1048576 | tf_op jit(solution)/shard_map/pallas_call | solution.py:444
  21.8 5.0 %all-to-all-start.1 = ((bf16[32,40,128]{2,1,0:T(8,128)(2,1)}), bf16[32,40,128]{2,1,0:T(8,128)(2,1)S(1)}, u32[]{:S(2)}, u32[]{:S(2)}) async-start(bf16[32,40,128]{2,1,0:T(8,128)(2,1)} %shard_map.151), calls=%async_computation.1 | async-start | bytes 655360 | tf_op jit(solution)/shard_map/all_to_all | solution.py:445
  26.7 1.8 %shard_map.152 = (f32[144,384]{1,0:T(8,128)S(1)}, bf16[9,256,256]{2,1,0:T(8,128)(2,1)S(1)}) custom-call(s32[1,2]{1,0:T(1,128)S(1)} %add_bitcast_fusion.spot_ref.band_ref, bf16[180,128]{1,0:T(8,128)(2,1)S(1)} %get-tuple-element.58.mine_ref, bf16[180,128]{1,0:T(8,128)(2,1)S(1)} %collective-permute-done.got_ref, bf16[9,256,256]{2,1,0:T(8,128)(2,1)} %w_hbm.1), custom_call_target="tpu_custom_call" | custom-call | bytes 1048576 | tf_op jit(solution)/shard_map/pallas_call | solution.py:447
  28.6 6.8 %all-to-all-done.1 = bf16[32,40,128]{2,1,0:T(8,128)(2,1)S(1)} async-done(((bf16[32,40,128]{2,1,0:T(8,128)(2,1)}), bf16[32,40,128]{2,1,0:T(8,128)(2,1)S(1)}, u32[]{:S(2)}, u32[]{:S(2)}) %all-to-all-start.1) | async-done | bytes 327712 | tf_op jit(solution)/shard_map/all_to_all | solution.py:445
  35.4 4.1 %shard_map.153 = (bf16[16,184,128]{2,1,0:T(8,128)(2,1)S(1)}, bf16[16,184,128]{2,1,0:T(8,128)(2,1)S(1)}) custom-call(s32[1,2]{1,0:T(1,128)S(1)} %add_bitcast_fusion.spot_ref.band_ref, bf16[16,2,40,128]{3,2,1,0:T(8,128)(2,1)S(1)} %bitcast.25, f32[144,384]{1,0:T(8,128)S(1)} %get-tuple-element.60.p_ref, bf16[9,256,256]{2,1,0:T(8,128)(2,1)S(1)} %get-tuple-element.61.w_ref), custom_call_target="tpu_custom_call" | custom-call | flops 2147483648 | bytes 3145728 | tf_op jit(solution)/shard_map/pallas_call | solution.py:452
  39.6 2.2 %collective-permute-done.1.got_ref = bf16[16,184,128]{2,1,0:T(8,128)(2,1)S(1)} collective-permute-done((bf16[16,184,128]{2,1,0:T(8,128)(2,1)S(1)}, bf16[16,184,128]{2,1,0:T(8,128)(2,1)S(1)}, u32[]{:S(2)}, u32[]{:S(2)}) %collective-permute-start.1) | collective-permute-done | bytes 753696 | tf_op jit(solution)/shard_map/ppermute | solution.py:400
  41.8 1.6 %shard_map.154 = bf16[16,224,128]{2,1,0:T(8,128)(2,1)} custom-call(s32[1,2]{1,0:T(1,128)S(1)} %add_bitcast_fusion.spot_ref.band_ref, bf16[16,184,128]{2,1,0:T(8,128)(2,1)S(1)} %get-tuple-element.62.mine_ref, bf16[16,184,128]{2,1,0:T(8,128)(2,1)S(1)} %collective-permute-done.1.got_ref), custom_call_target="tpu_custom_call" | custom-call | bytes 2097152 | tf_op jit(solution)/shard_map/pallas_call | solution.py:465
  43.4 5.0 %all-to-all-start.2 = ((bf16[16,224,128]{2,1,0:T(8,128)(2,1)}), bf16[16,224,128]{2,1,0:T(8,128)(2,1)S(1)}, u32[]{:S(2)}, u32[]{:S(2)}) async-start(bf16[16,224,128]{2,1,0:T(8,128)(2,1)} %shard_map.154), calls=%async_computation.2 | async-start | bytes 1835008 | tf_op jit(solution)/shard_map/all_to_all | solution.py:473
  48.4 1.8 %shard_map.155 = (bf16[2,768,384]{2,1,0:T(8,128)(2,1)S(1)}, bf16[2,384,512]{2,1,0:T(8,128)(2,1)S(1)}) custom-call(f32[2,8,384]{2,1,0:T(8,128)} %constant.30.clone.refs_0_, f32[2,8,384]{2,1,0:T(8,128)} %constant.31.clone.refs_1_, f32[2,96,384]{2,1,0:T(8,128)} %constant.32.clone.refs_2_, f32[2,96,384]{2,1,0:T(8,128)} %constant.33.clone.refs_3_, ...), custom_call_target="tpu_custom_call" | custom-call | bytes 5242880 | tf_op jit(solution)/shard_map/pallas_call | solution.py:476
  50.2 13.3 %all-to-all-done.2.r_ref = bf16[16,224,128]{2,1,0:T(8,128)(2,1)S(1)} async-done(((bf16[16,224,128]{2,1,0:T(8,128)(2,1)}), bf16[16,224,128]{2,1,0:T(8,128)(2,1)S(1)}, u32[]{:S(2)}, u32[]{:S(2)}) %all-to-all-start.2) | async-done | bytes 917536 | tf_op jit(solution)/shard_map/all_to_all | solution.py:473
  63.5 2.0 %collective-permute-start.2 = (bf16[144,128]{1,0:T(8,128)(2,1)S(1)}, bf16[144,128]{1,0:T(8,128)(2,1)S(1)}, u32[]{:S(2)}, u32[]{:S(2)}) collective-permute-start(bf16[144,128]{1,0:T(8,128)(2,1)S(1)} %slice_reduce_fusion), channel_id=1, source_target_pairs={{0,32},{32,0},{64,96},{96,64},{128,160},{160,128},{192,224},{224,1... | collective-permute-start | bytes 110600 | tf_op jit(solution)/shard_map/ppermute | solution.py:491
  65.5 2.1 %collective-permute-done.2 = bf16[144,128]{1,0:T(8,128)(2,1)S(1)} collective-permute-done((bf16[144,128]{1,0:T(8,128)(2,1)S(1)}, bf16[144,128]{1,0:T(8,128)(2,1)S(1)}, u32[]{:S(2)}, u32[]{:S(2)}) %collective-permute-start.2) | collective-permute-done | bytes 36896 | tf_op jit(solution)/shard_map/ppermute | solution.py:491
  67.6 5.9 %collective-permute-start.3 = (bf16[144,128]{1,0:T(8,128)(2,1)S(1)}, bf16[144,128]{1,0:T(8,128)(2,1)S(1)}, u32[]{:S(2)}, u32[]{:S(2)}) collective-permute-start(bf16[144,128]{1,0:T(8,128)(2,1)S(1)} %add_convert_fusion), channel_id=1, source_target_pairs={{0,224},{32,64},{64,32},{96,128},{128,96},{160,192},{192,160},{224... | collective-permute-start | bytes 110600 | tf_op jit(solution)/shard_map/ppermute | solution.py:491
  73.5 1.9 %collective-permute-done.3 = bf16[144,128]{1,0:T(8,128)(2,1)S(1)} collective-permute-done((bf16[144,128]{1,0:T(8,128)(2,1)S(1)}, bf16[144,128]{1,0:T(8,128)(2,1)S(1)}, u32[]{:S(2)}, u32[]{:S(2)}) %collective-permute-start.3) | collective-permute-done | bytes 36896 | tf_op jit(solution)/shard_map/ppermute | solution.py:491
  75.5 2.6 %collective-permute-start.4 = (bf16[144,128]{1,0:T(8,128)(2,1)S(1)}, bf16[144,128]{1,0:T(8,128)(2,1)S(1)}, u32[]{:S(2)}, u32[]{:S(2)}) collective-permute-start(bf16[144,128]{1,0:T(8,128)(2,1)S(1)} %collective-permute-done.3), channel_id=1, source_target_pairs={{0,64},{32,224},{64,128},{96,32},{128,192},{160,96},{192,0},{224,1... | collective-permute-start | bytes 110600 | tf_op jit(solution)/shard_map/ppermute | solution.py:491
  78.0 1.5 %shard_map.156 = bf16[16,120,128]{2,1,0:T(8,128)(2,1)} custom-call(bf16[16,224,128]{2,1,0:T(8,128)(2,1)S(1)} %all-to-all-done.2.r_ref, bf16[2,768,384]{2,1,0:T(8,128)(2,1)S(1)} %get-tuple-element.75.w_ref, bf16[2,384,512]{2,1,0:T(8,128)(2,1)S(1)} %get-tuple-element.76.v_ref), custom_call_target="tpu_custom_call" | custom-call | flops 314572800 | bytes 1048576 | tf_op jit(solution)/shard_map/pallas_call | solution.py:501
  79.5 4.9 %all-to-all-start.3 = ((bf16[16,120,128]{2,1,0:T(8,128)(2,1)}), bf16[16,120,128]{2,1,0:T(8,128)(2,1)S(1)}, u32[]{:S(2)}, u32[]{:S(2)}) async-start(bf16[16,120,128]{2,1,0:T(8,128)(2,1)} %shard_map.156), calls=%async_computation.3 | async-start | bytes 983040 | tf_op jit(solution)/shard_map/all_to_all | solution.py:502
  84.6 1.2 %collective-permute-done.6 = f32[144,128]{1,0:T(8,128)S(1)} collective-permute-done((f32[144,128]{1,0:T(8,128)S(1)}, f32[144,128]{1,0:T(8,128)S(1)}, u32[]{:S(2)}, u32[]{:S(2)}) %collective-permute-start.6) | collective-permute-done | bytes 73760 | tf_op jit(solution)/shard_map/ppermute | solution.py:400
  86.5 6.6 %all-to-all-done.3.r_ref = bf16[16,120,128]{2,1,0:T(8,128)(2,1)S(1)} async-done(((bf16[16,120,128]{2,1,0:T(8,128)(2,1)}), bf16[16,120,128]{2,1,0:T(8,128)(2,1)S(1)}, u32[]{:S(2)}, u32[]{:S(2)}) %all-to-all-start.3) | async-done | bytes 491552 | tf_op jit(solution)/shard_map/all_to_all | solution.py:502
  (17 shorter events, 2.4 us)
Async XLA Ops:
  0.6 9.8 %copy-start = (s32[4,2]{0,1:T(2,128)S(1)}, s32[4,2]{0,1:T(2,128)}, u32[]{:S(2)}) copy-start(s32[4,2]{0,1:T(2,128)} %param.15) | copy-start | bytes 100
  3.0 17.3 %all-to-all-start = ((bf16[16,120,128]{2,1,0:T(8,128)(2,1)}), bf16[16,120,128]{2,1,0:T(8,128)(2,1)S(1)}, u32[]{:S(2)}, u32[]{:S(2)}) async-start(bf16[16,120,128]{2,1,0:T(8,128)(2,1)} %shard_map.148), calls=%async_computation | async-start | bytes 983040 | tf_op jit(solution)/shard_map/all_to_all | solution.py:422
  12.5 2.7 %collective-permute-start = (bf16[180,128]{1,0:T(8,128)(2,1)S(1)}, bf16[180,128]{1,0:T(8,128)(2,1)S(1)}, u32[]{:S(2)}, u32[]{:S(2)}) collective-permute-start(bf16[180,128]{1,0:T(8,128)(2,1)S(1)} %get-tuple-element.44), channel_id=1, source_target_pairs={{0,16},{16,0},{1,17},{17,1},{2,18},{18,2},{3,19},{19,3},{4,20},{20... | collective-permute-start | bytes 138248 | tf_op jit(solution)/shard_map/ppermute | solution.py:400
  21.8 13.6 %all-to-all-start.1 = ((bf16[32,40,128]{2,1,0:T(8,128)(2,1)}), bf16[32,40,128]{2,1,0:T(8,128)(2,1)S(1)}, u32[]{:S(2)}, u32[]{:S(2)}) async-start(bf16[32,40,128]{2,1,0:T(8,128)(2,1)} %shard_map.151), calls=%async_computation.1 | async-start | bytes 655360 | tf_op jit(solution)/shard_map/all_to_all | solution.py:445
  39.5 2.3 %collective-permute-start.1 = (bf16[16,184,128]{2,1,0:T(8,128)(2,1)S(1)}, bf16[16,184,128]{2,1,0:T(8,128)(2,1)S(1)}, u32[]{:S(2)}, u32[]{:S(2)}) collective-permute-start(bf16[16,184,128]{2,1,0:T(8,128)(2,1)S(1)} %get-tuple-element.63), channel_id=1, source_target_pairs={{0,16},{16,0},{1,17},{17,1},{2,18},{18,2},{3,19},{19,3},{4,20},{20... | collective-permute-start | bytes 2261000 | tf_op jit(solution)/shard_map/ppermute | solution.py:400
  43.4 20.1 %all-to-all-start.2 = ((bf16[16,224,128]{2,1,0:T(8,128)(2,1)}), bf16[16,224,128]{2,1,0:T(8,128)(2,1)S(1)}, u32[]{:S(2)}, u32[]{:S(2)}) async-start(bf16[16,224,128]{2,1,0:T(8,128)(2,1)} %shard_map.154), calls=%async_computation.2 | async-start | bytes 1835008 | tf_op jit(solution)/shard_map/all_to_all | solution.py:473
  63.5 4.0 %collective-permute-start.2 = (bf16[144,128]{1,0:T(8,128)(2,1)S(1)}, bf16[144,128]{1,0:T(8,128)(2,1)S(1)}, u32[]{:S(2)}, u32[]{:S(2)}) collective-permute-start(bf16[144,128]{1,0:T(8,128)(2,1)S(1)} %slice_reduce_fusion), channel_id=1, source_target_pairs={{0,32},{32,0},{64,96},{96,64},{128,160},{160,128},{192,224},{224,1... | collective-permute-start | bytes 110600 | tf_op jit(solution)/shard_map/ppermute | solution.py:491
  67.6 7.9 %collective-permute-start.3 = (bf16[144,128]{1,0:T(8,128)(2,1)S(1)}, bf16[144,128]{1,0:T(8,128)(2,1)S(1)}, u32[]{:S(2)}, u32[]{:S(2)}) collective-permute-start(bf16[144,128]{1,0:T(8,128)(2,1)S(1)} %add_convert_fusion), channel_id=1, source_target_pairs={{0,224},{32,64},{64,32},{96,128},{128,96},{160,192},{192,160},{224... | collective-permute-start | bytes 110600 | tf_op jit(solution)/shard_map/ppermute | solution.py:491
  75.5 9.0 %collective-permute-start.5 = (bf16[144,128]{1,0:T(8,128)(2,1)S(1)}, bf16[144,128]{1,0:T(8,128)(2,1)S(1)}, u32[]{:S(2)}, u32[]{:S(2)}) collective-permute-start(bf16[144,128]{1,0:T(8,128)(2,1)S(1)} %collective-permute-done.3), channel_id=1, source_target_pairs={{0,32},{32,0},{64,96},{96,64},{128,160},{160,128},{192,224},{224,1... | collective-permute-start | bytes 110600 | tf_op jit(solution)/shard_map/ppermute | solution.py:491
  75.5 9.0 %collective-permute-start.4 = (bf16[144,128]{1,0:T(8,128)(2,1)S(1)}, bf16[144,128]{1,0:T(8,128)(2,1)S(1)}, u32[]{:S(2)}, u32[]{:S(2)}) collective-permute-start(bf16[144,128]{1,0:T(8,128)(2,1)S(1)} %collective-permute-done.3), channel_id=1, source_target_pairs={{0,64},{32,224},{64,128},{96,32},{128,192},{160,96},{192,0},{224,1... | collective-permute-start | bytes 110600 | tf_op jit(solution)/shard_map/ppermute | solution.py:491
  79.5 13.6 %all-to-all-start.3 = ((bf16[16,120,128]{2,1,0:T(8,128)(2,1)}), bf16[16,120,128]{2,1,0:T(8,128)(2,1)S(1)}, u32[]{:S(2)}, u32[]{:S(2)}) async-start(bf16[16,120,128]{2,1,0:T(8,128)(2,1)} %shard_map.156), calls=%async_computation.3 | async-start | bytes 983040 | tf_op jit(solution)/shard_map/all_to_all | solution.py:502
  84.5 1.4 %collective-permute-start.6 = (f32[144,128]{1,0:T(8,128)S(1)}, f32[144,128]{1,0:T(8,128)S(1)}, u32[]{:S(2)}, u32[]{:S(2)}) collective-permute-start(f32[144,128]{1,0:T(8,128)S(1)} %add_add_fusion), channel_id=1, source_target_pairs={{0,16},{16,0},{1,17},{17,1},{2,18},{18,2},{3,19},{19,3},{4,20},{20... | collective-permute-start | bytes 221192 | tf_op jit(solution)/shard_map/ppermute | solution.py:400

commit v6 on v5

--- a/solution.py
+++ b/solution.py
@@ -109,18 +109,28 @@
     return 48 * (column % 4) + column // 4
 
 
-def pack_body(f_hbm, g_hbm, o_ref, f_ref, g_ref, flat_ref, sems):
-    copies = fetch((f_hbm, g_hbm), (f_ref, g_ref), sems)
-    copies[0].wait()
-    for j in range(6):
-        count = min(128, 8 * WPART - 128 * j)
+def pack_body(f_hbm, g_hbm, o_hbm, f_ref, g_ref, flat_ref, o_ref, sems, out_sems):
+    starts = [(128 * j, min(128, 8 * WPART - 128 * j)) for j in range(6)]
+    sources = [f_hbm.at[pl.ds(start, count)] for start, count in starts]
+    targets = [f_ref.at[pl.ds(start, count)] for start, count in starts]
+    copies = fetch(sources + [g_hbm], targets + [g_ref], sems)
+    sent = []
+
+    def send(rows, sem):
+        sent.append(pltpu.make_async_copy(o_ref.at[:, rows], o_hbm.at[:, rows], out_sems.at[sem]))
+        sent[-1].start()
+
+    for j, (start, count) in enumerate(starts):
         order = one_hot((128, count), row_of_latitude)
-        block = dot(order, f_ref[128 * j : 128 * j + count, :]).astype(BF16)
+        copies[j].wait()
+        block = dot(order, f_ref[start : start + count, :]).astype(BF16)
         for r in range(8):
             for h in range(2):
                 piece = block[16 * r : 16 * (r + 1), 128 * h : 128 * (h + 1)]
                 o_ref[2 * r + h, 16 * j : 16 * (j + 1), :] = piece
-    copies[1].wait()
+        if j % 2 == 1:
+            send(pl.ds(16 * (j - 1), 32), j // 2)
+    copies[6].wait()
     for v in range(VPART):
         flat_ref[4 * v : 4 * (v + 1), :] = g_ref[v].astype(F32)
     flat_ref[4 * VPART : 192, :] = jnp.zeros((192 - 4 * VPART, C), F32)
@@ -134,6 +144,9 @@
             odd = jnp.where(keep, swap64(top), bottom)
             o_ref[4 * o + 2 * i, WROWS:CHUNK_IN, :] = even.astype(BF16)
             o_ref[4 * o + 2 * i + 1, WROWS:CHUNK_IN, :] = odd.astype(BF16)
+    send(pl.ds(WROWS, VROWS), 3)
+    for copy in sent:
+        copy.wait()
 
 
 def flip(source, target, rows, columns):
@@ -414,8 +427,11 @@
             pltpu.VMEM((8 * WPART, C), BF16),
             pltpu.VMEM((VPART, 4, C), BF16),
             pltpu.VMEM((192, C), F32),
-            dma((2,)),
+            pltpu.VMEM((LANES, CHUNK_IN, 128), BF16),
+            dma((7,)),
+            dma((4,)),
         ],
+        out_place=HBM,
     )(
         in_hbm(jnp.swapaxes(fields[0], 0, 1).reshape(8 * WPART, C)), in_hbm(jnp.swapaxes(out_grad[0], 0, 1))
     )
@@ -500,10 +516,10 @@
     far = swap_bands(half)
     (sent,) = call(fields_body, [VMEM] * 3, [((LANES, CHUNK_IN, 128), BF16)], flops=300 << 20)(landed, tall, inv)
     landed = lax.all_to_all(sent, "azimuth", split_axis=0, concat_axis=0, tiled=True)
-    weight_grad = jnp.concatenate([jnp.where(low, half, far), jnp.where(low, far, half)], axis=1)
     field_grad, conv_out = call(
         unpack_body, [VMEM], [((8 * WPART, C), BF16), ((VPART, 4, C), BF16)], scratch=[pltpu.VMEM((192, C), F32)]
     )(landed)
+    weight_grad = jnp.concatenate([jnp.where(low, half, far), jnp.where(low, far, half)], axis=1)
     field_grad = jnp.swapaxes(field_grad.reshape(WPART, 8, C), 0, 1)
     return (jnp.swapaxes(conv_out, 0, 1)[None], field_grad[None], weight_grad.reshape(K, 16, C))
 

time: 95.9 us -> 96.5 us (level)
  no operation moved by 1% of the time
where the time goes in v6:
time: 96.5 us; the launch traced here: 94.8 us
  waiting for transfers between devices  39.2 us (41%)
  starting transfers between devices  33.2 us (34%)
  Pallas kernels  20.6 us (21%)
    all_to_all x3, waiting for transfers between devices, local(): lax.all_to_all(sent, 'azimuth', split_axis=0, concat_axis=0, tiled=True)  24.9 us
    all_to_all x3, starting transfers between devices, local(): lax.all_to_all(sent, 'azimuth', split_axis=0, concat_axis=0, tiled=True)  17.4 us
    ppermute x4, starting transfers between devices, send(): return lax.ppermute(value, 'ens', pairs)  10.5 us
    all_to_all x1, waiting for transfers between devices, local(): lax.all_to_all(sent, JOINT, split_axis=0, concat_axis=0, tiled=True)  6.8 us
    all_to_all x1, starting transfers between devices, local(): lax.all_to_all(sent, JOINT, split_axis=0, concat_axis=0, tiled=True)  4.99 us
    pallas_call x1, Pallas kernels, local(): call(middle_body, [SMEM, VMEM, VMEM, VMEM], [(chunk, BF16), (chunk, BF16)...  4.09 us
    ppermute x4, waiting for transfers between devices, send(): return lax.ppermute(value, 'ens', pairs)  3.99 us
    ppermute x3, waiting for transfers between devices, swap_bands(): return lax.ppermute(value, 'polar', [(0, 1), (1, 0)])  3.47 us
  transfers between devices with their start and end apart: 11, of which 8 were waited for; matrix products, arithmetic and copies ran while one was open for 1% of the time, Pallas kernels for 10%

profile of v6, /device:TPU:2, one launch (start us, length us, event | category | flops | bytes accessed | tf_op | source)
XLA Modules:
  0.0 94.8 jit_solution(3463311333625855927)
XLA Ops:
  0.6 2.9 %shard_map.148 = bf16[16,120,128]{2,1,0:T(8,128)(2,1)} custom-call(bf16[720,256]{1,0:T(8,128)(2,1)} %bitcast.26, bf16[45,4,256]{2,1,0:T(4,128)(2,1)} %bitcast.29), custom_call_target="tpu_custom_call" | custom-call | bytes 1048576 | tf_op jit(solution)/shard_map/pallas_call | solution.py:422
  3.5 7.5 %all-to-all-start = ((bf16[16,120,128]{2,1,0:T(8,128)(2,1)}), bf16[16,120,128]{2,1,0:T(8,128)(2,1)S(1)}, u32[]{:S(2)}, u32[]{:S(2)}) async-start(bf16[16,120,128]{2,1,0:T(8,128)(2,1)} %shard_map.148), calls=%async_computation | async-start | bytes 983040 | tf_op jit(solution)/shard_map/all_to_all | solution.py:438
  11.2 1.9 %shard_map.149 = (bf16[180,128]{1,0:T(8,128)(2,1)S(1)}, bf16[180,128]{1,0:T(8,128)(2,1)S(1)}) custom-call(s32[1,2]{1,0:T(1,128)S(1)} %add_bitcast_fusion.spot_ref.band_ref, s32[4,2]{1,0:T(4,128)S(1)} %copy.16.support_ref, bf16[45,4,720]{2,1,0:T(4,128)(2,1)} %bitcast.27), custom_call_target="tpu_custom_call" | custom-call | bytes 1048576 | tf_op jit(solution)/shard_map/pallas_call | solution.py:441
  13.1 2.6 %shard_map.150 = (bf16[2,384,768]{2,1,0:T(8,128)(2,1)S(1)}, bf16[2,512,384]{2,1,0:T(8,128)(2,1)S(1)}) custom-call(f32[2,8,384]{2,1,0:T(8,128)} %constant.30.clone.refs_0_, f32[2,8,384]{2,1,0:T(8,128)} %constant.31.clone.refs_1_, f32[2,96,384]{2,1,0:T(8,128)} %constant.32.clone.refs_2_, f32[2,96,384]{2,1,0:T(8,128)} %constant.33.clone.refs_3_, ...), custom_call_target="tpu_custom_call" | custom-call | bytes 5242880 | tf_op jit(solution)/shard_map/pallas_call | solution.py:451
  15.7 5.1 %all-to-all-done.r_ref = bf16[16,120,128]{2,1,0:T(8,128)(2,1)S(1)} async-done(((bf16[16,120,128]{2,1,0:T(8,128)(2,1)}), bf16[16,120,128]{2,1,0:T(8,128)(2,1)S(1)}, u32[]{:S(2)}, u32[]{:S(2)}) %all-to-all-start) | async-done | bytes 491552 | tf_op jit(solution)/shard_map/all_to_all | solution.py:438
  20.8 1.5 %shard_map.151 = bf16[32,40,128]{2,1,0:T(8,128)(2,1)} custom-call(bf16[16,120,128]{2,1,0:T(8,128)(2,1)S(1)} %all-to-all-done.r_ref, bf16[2,384,768]{2,1,0:T(8,128)(2,1)S(1)} %get-tuple-element.54.wt_ref, bf16[2,512,384]{2,1,0:T(8,128)(2,1)S(1)} %get-tuple-element.55.vt_ref), custom_call_target="tpu_custom_call" | custom-call | flops 314572800 | bytes 1048576 | tf_op jit(solution)/shard_map/pallas_call | solution.py:460
  22.3 5.0 %all-to-all-start.1 = ((bf16[32,40,128]{2,1,0:T(8,128)(2,1)}), bf16[32,40,128]{2,1,0:T(8,128)(2,1)S(1)}, u32[]{:S(2)}, u32[]{:S(2)}) async-start(bf16[32,40,128]{2,1,0:T(8,128)(2,1)} %shard_map.151), calls=%async_computation.1 | async-start | bytes 655360 | tf_op jit(solution)/shard_map/all_to_all | solution.py:461
  27.3 1.8 %shard_map.152 = (f32[144,384]{1,0:T(8,128)S(1)}, bf16[9,256,256]{2,1,0:T(8,128)(2,1)S(1)}) custom-call(s32[1,2]{1,0:T(1,128)S(1)} %add_bitcast_fusion.spot_ref.band_ref, bf16[180,128]{1,0:T(8,128)(2,1)S(1)} %get-tuple-element.58.mine_ref, bf16[180,128]{1,0:T(8,128)(2,1)S(1)} %collective-permute-done.got_ref, bf16[9,256,256]{2,1,0:T(8,128)(2,1)} %w_hbm.1), custom_call_target="tpu_custom_call" | custom-call | bytes 1048576 | tf_op jit(solution)/shard_map/pallas_call | solution.py:463
  29.1 6.8 %all-to-all-done.1 = bf16[32,40,128]{2,1,0:T(8,128)(2,1)S(1)} async-done(((bf16[32,40,128]{2,1,0:T(8,128)(2,1)}), bf16[32,40,128]{2,1,0:T(8,128)(2,1)S(1)}, u32[]{:S(2)}, u32[]{:S(2)}) %all-to-all-start.1) | async-done | bytes 327712 | tf_op jit(solution)/shard_map/all_to_all | solution.py:461
  35.9 4.1 %shard_map.153 = (bf16[16,184,128]{2,1,0:T(8,128)(2,1)S(1)}, bf16[16,184,128]{2,1,0:T(8,128)(2,1)S(1)}) custom-call(s32[1,2]{1,0:T(1,128)S(1)} %add_bitcast_fusion.spot_ref.band_ref, bf16[16,2,40,128]{3,2,1,0:T(8,128)(2,1)S(1)} %bitcast.25, f32[144,384]{1,0:T(8,128)S(1)} %get-tuple-element.60.p_ref, bf16[9,256,256]{2,1,0:T(8,128)(2,1)S(1)} %get-tuple-element.61.w_ref), custom_call_target="tpu_custom_call" | custom-call | flops 2147483648 | bytes 3145728 | tf_op jit(solution)/shard_map/pallas_call | solution.py:468
  40.1 2.2 %collective-permute-done.1.got_ref = bf16[16,184,128]{2,1,0:T(8,128)(2,1)S(1)} collective-permute-done((bf16[16,184,128]{2,1,0:T(8,128)(2,1)S(1)}, bf16[16,184,128]{2,1,0:T(8,128)(2,1)S(1)}, u32[]{:S(2)}, u32[]{:S(2)}) %collective-permute-start.1) | collective-permute-done | bytes 753696 | tf_op jit(solution)/shard_map/ppermute | solution.py:413
  42.3 1.6 %shard_map.154 = bf16[16,224,128]{2,1,0:T(8,128)(2,1)} custom-call(s32[1,2]{1,0:T(1,128)S(1)} %add_bitcast_fusion.spot_ref.band_ref, bf16[16,184,128]{2,1,0:T(8,128)(2,1)S(1)} %get-tuple-element.62.mine_ref, bf16[16,184,128]{2,1,0:T(8,128)(2,1)S(1)} %collective-permute-done.1.got_ref), custom_call_target="tpu_custom_call" | custom-call | bytes 2097152 | tf_op jit(solution)/shard_map/pallas_call | solution.py:481
  43.9 5.0 %all-to-all-start.2 = ((bf16[16,224,128]{2,1,0:T(8,128)(2,1)}), bf16[16,224,128]{2,1,0:T(8,128)(2,1)S(1)}, u32[]{:S(2)}, u32[]{:S(2)}) async-start(bf16[16,224,128]{2,1,0:T(8,128)(2,1)} %shard_map.154), calls=%async_computation.2 | async-start | bytes 1835008 | tf_op jit(solution)/shard_map/all_to_all | solution.py:489
  48.9 1.8 %shard_map.155 = (bf16[2,768,384]{2,1,0:T(8,128)(2,1)S(1)}, bf16[2,384,512]{2,1,0:T(8,128)(2,1)S(1)}) custom-call(f32[2,8,384]{2,1,0:T(8,128)} %constant.30.clone.refs_0_, f32[2,8,384]{2,1,0:T(8,128)} %constant.31.clone.refs_1_, f32[2,96,384]{2,1,0:T(8,128)} %constant.32.clone.refs_2_, f32[2,96,384]{2,1,0:T(8,128)} %constant.33.clone.refs_3_, ...), custom_call_target="tpu_custom_call" | custom-call | bytes 5242880 | tf_op jit(solution)/shard_map/pallas_call | solution.py:492
  50.7 13.3 %all-to-all-done.2.r_ref = bf16[16,224,128]{2,1,0:T(8,128)(2,1)S(1)} async-done(((bf16[16,224,128]{2,1,0:T(8,128)(2,1)}), bf16[16,224,128]{2,1,0:T(8,128)(2,1)S(1)}, u32[]{:S(2)}, u32[]{:S(2)}) %all-to-all-start.2) | async-done | bytes 917536 | tf_op jit(solution)/shard_map/all_to_all | solution.py:489
  64.1 2.0 %collective-permute-start.2 = (bf16[144,128]{1,0:T(8,128)(2,1)S(1)}, bf16[144,128]{1,0:T(8,128)(2,1)S(1)}, u32[]{:S(2)}, u32[]{:S(2)}) collective-permute-start(bf16[144,128]{1,0:T(8,128)(2,1)S(1)} %slice_reduce_fusion), channel_id=1, source_target_pairs={{0,32},{32,0},{64,96},{96,64},{128,160},{160,128},{192,224},{224,1... | collective-permute-start | bytes 110600 | tf_op jit(solution)/shard_map/ppermute | solution.py:507
  66.1 2.0 %collective-permute-done.2 = bf16[144,128]{1,0:T(8,128)(2,1)S(1)} collective-permute-done((bf16[144,128]{1,0:T(8,128)(2,1)S(1)}, bf16[144,128]{1,0:T(8,128)(2,1)S(1)}, u32[]{:S(2)}, u32[]{:S(2)}) %collective-permute-start.2) | collective-permute-done | bytes 36896 | tf_op jit(solution)/shard_map/ppermute | solution.py:507
  68.1 5.9 %collective-permute-start.3 = (bf16[144,128]{1,0:T(8,128)(2,1)S(1)}, bf16[144,128]{1,0:T(8,128)(2,1)S(1)}, u32[]{:S(2)}, u32[]{:S(2)}) collective-permute-start(bf16[144,128]{1,0:T(8,128)(2,1)S(1)} %add_convert_fusion), channel_id=1, source_target_pairs={{0,224},{32,64},{64,32},{96,128},{128,96},{160,192},{192,160},{224... | collective-permute-start | bytes 110600 | tf_op jit(solution)/shard_map/ppermute | solution.py:507
  74.1 1.9 %collective-permute-done.3 = bf16[144,128]{1,0:T(8,128)(2,1)S(1)} collective-permute-done((bf16[144,128]{1,0:T(8,128)(2,1)S(1)}, bf16[144,128]{1,0:T(8,128)(2,1)S(1)}, u32[]{:S(2)}, u32[]{:S(2)}) %collective-permute-start.3) | collective-permute-done | bytes 36896 | tf_op jit(solution)/shard_map/ppermute | solution.py:507
  76.0 2.6 %collective-permute-start.4 = (bf16[144,128]{1,0:T(8,128)(2,1)S(1)}, bf16[144,128]{1,0:T(8,128)(2,1)S(1)}, u32[]{:S(2)}, u32[]{:S(2)}) collective-permute-start(bf16[144,128]{1,0:T(8,128)(2,1)S(1)} %collective-permute-done.3), channel_id=1, source_target_pairs={{0,64},{32,224},{64,128},{96,32},{128,192},{160,96},{192,0},{224,1... | collective-permute-start | bytes 110600 | tf_op jit(solution)/shard_map/ppermute | solution.py:507
  78.6 1.5 %shard_map.156 = bf16[16,120,128]{2,1,0:T(8,128)(2,1)} custom-call(bf16[16,224,128]{2,1,0:T(8,128)(2,1)S(1)} %all-to-all-done.2.r_ref, bf16[2,768,384]{2,1,0:T(8,128)(2,1)S(1)} %get-tuple-element.75.w_ref, bf16[2,384,512]{2,1,0:T(8,128)(2,1)S(1)} %get-tuple-element.76.v_ref), custom_call_target="tpu_custom_call" | custom-call | flops 314572800 | bytes 1048576 | tf_op jit(solution)/shard_map/pallas_call | solution.py:517
  80.0 4.9 %all-to-all-start.3 = ((bf16[16,120,128]{2,1,0:T(8,128)(2,1)}), bf16[16,120,128]{2,1,0:T(8,128)(2,1)S(1)}, u32[]{:S(2)}, u32[]{:S(2)}) async-start(bf16[16,120,128]{2,1,0:T(8,128)(2,1)} %shard_map.156), calls=%async_computation.3 | async-start | bytes 983040 | tf_op jit(solution)/shard_map/all_to_all | solution.py:518
  85.1 1.2 %collective-permute-done.6 = f32[144,128]{1,0:T(8,128)S(1)} collective-permute-done((f32[144,128]{1,0:T(8,128)S(1)}, f32[144,128]{1,0:T(8,128)S(1)}, u32[]{:S(2)}, u32[]{:S(2)}) %collective-permute-start.6) | collective-permute-done | bytes 73760 | tf_op jit(solution)/shard_map/ppermute | solution.py:413
  87.1 6.6 %all-to-all-done.3.r_ref = bf16[16,120,128]{2,1,0:T(8,128)(2,1)S(1)} async-done(((bf16[16,120,128]{2,1,0:T(8,128)(2,1)}), bf16[16,120,128]{2,1,0:T(8,128)(2,1)S(1)}, u32[]{:S(2)}, u32[]{:S(2)}) %all-to-all-start.3) | async-done | bytes 491552 | tf_op jit(solution)/shard_map/all_to_all | solution.py:518
  (17 shorter events, 2.4 us)
Async XLA Ops:
  0.6 10.4 %copy-start = (s32[4,2]{0,1:T(2,128)S(1)}, s32[4,2]{0,1:T(2,128)}, u32[]{:S(2)}) copy-start(s32[4,2]{0,1:T(2,128)} %param.15) | copy-start | bytes 100
  3.5 17.3 %all-to-all-start = ((bf16[16,120,128]{2,1,0:T(8,128)(2,1)}), bf16[16,120,128]{2,1,0:T(8,128)(2,1)S(1)}, u32[]{:S(2)}, u32[]{:S(2)}) async-start(bf16[16,120,128]{2,1,0:T(8,128)(2,1)} %shard_map.148), calls=%async_computation | async-start | bytes 983040 | tf_op jit(solution)/shard_map/all_to_all | solution.py:438
  13.0 2.7 %collective-permute-start = (bf16[180,128]{1,0:T(8,128)(2,1)S(1)}, bf16[180,128]{1,0:T(8,128)(2,1)S(1)}, u32[]{:S(2)}, u32[]{:S(2)}) collective-permute-start(bf16[180,128]{1,0:T(8,128)(2,1)S(1)} %get-tuple-element.44), channel_id=1, source_target_pairs={{0,16},{16,0},{1,17},{17,1},{2,18},{18,2},{3,19},{19,3},{4,20},{20... | collective-permute-start | bytes 138248 | tf_op jit(solution)/shard_map/ppermute | solution.py:413
  22.3 13.6 %all-to-all-start.1 = ((bf16[32,40,128]{2,1,0:T(8,128)(2,1)}), bf16[32,40,128]{2,1,0:T(8,128)(2,1)S(1)}, u32[]{:S(2)}, u32[]{:S(2)}) async-start(bf16[32,40,128]{2,1,0:T(8,128)(2,1)} %shard_map.151), calls=%async_computation.1 | async-start | bytes 655360 | tf_op jit(solution)/shard_map/all_to_all | solution.py:461
  40.0 2.3 %collective-permute-start.1 = (bf16[16,184,128]{2,1,0:T(8,128)(2,1)S(1)}, bf16[16,184,128]{2,1,0:T(8,128)(2,1)S(1)}, u32[]{:S(2)}, u32[]{:S(2)}) collective-permute-start(bf16[16,184,128]{2,1,0:T(8,128)(2,1)S(1)} %get-tuple-element.63), channel_id=1, source_target_pairs={{0,16},{16,0},{1,17},{17,1},{2,18},{18,2},{3,19},{19,3},{4,20},{20... | collective-permute-start | bytes 2261000 | tf_op jit(solution)/shard_map/ppermute | solution.py:413
  43.9 20.1 %all-to-all-start.2 = ((bf16[16,224,128]{2,1,0:T(8,128)(2,1)}), bf16[16,224,128]{2,1,0:T(8,128)(2,1)S(1)}, u32[]{:S(2)}, u32[]{:S(2)}) async-start(bf16[16,224,128]{2,1,0:T(8,128)(2,1)} %shard_map.154), calls=%async_computation.2 | async-start | bytes 1835008 | tf_op jit(solution)/shard_map/all_to_all | solution.py:489
  64.1 4.0 %collective-permute-start.2 = (bf16[144,128]{1,0:T(8,128)(2,1)S(1)}, bf16[144,128]{1,0:T(8,128)(2,1)S(1)}, u32[]{:S(2)}, u32[]{:S(2)}) collective-permute-start(bf16[144,128]{1,0:T(8,128)(2,1)S(1)} %slice_reduce_fusion), channel_id=1, source_target_pairs={{0,32},{32,0},{64,96},{96,64},{128,160},{160,128},{192,224},{224,1... | collective-permute-start | bytes 110600 | tf_op jit(solution)/shard_map/ppermute | solution.py:507
  68.1 7.9 %collective-permute-start.3 = (bf16[144,128]{1,0:T(8,128)(2,1)S(1)}, bf16[144,128]{1,0:T(8,128)(2,1)S(1)}, u32[]{:S(2)}, u32[]{:S(2)}) collective-permute-start(bf16[144,128]{1,0:T(8,128)(2,1)S(1)} %add_convert_fusion), channel_id=1, source_target_pairs={{0,224},{32,64},{64,32},{96,128},{128,96},{160,192},{192,160},{224... | collective-permute-start | bytes 110600 | tf_op jit(solution)/shard_map/ppermute | solution.py:507
  76.0 9.0 %collective-permute-start.5 = (bf16[144,128]{1,0:T(8,128)(2,1)S(1)}, bf16[144,128]{1,0:T(8,128)(2,1)S(1)}, u32[]{:S(2)}, u32[]{:S(2)}) collective-permute-start(bf16[144,128]{1,0:T(8,128)(2,1)S(1)} %collective-permute-done.3), channel_id=1, source_target_pairs={{0,32},{32,0},{64,96},{96,64},{128,160},{160,128},{192,224},{224,1... | collective-permute-start | bytes 110600 | tf_op jit(solution)/shard_map/ppermute | solution.py:507
  76.0 9.0 %collective-permute-start.4 = (bf16[144,128]{1,0:T(8,128)(2,1)S(1)}, bf16[144,128]{1,0:T(8,128)(2,1)S(1)}, u32[]{:S(2)}, u32[]{:S(2)}) collective-permute-start(bf16[144,128]{1,0:T(8,128)(2,1)S(1)} %collective-permute-done.3), channel_id=1, source_target_pairs={{0,64},{32,224},{64,128},{96,32},{128,192},{160,96},{192,0},{224,1... | collective-permute-start | bytes 110600 | tf_op jit(solution)/shard_map/ppermute | solution.py:507
  80.0 13.6 %all-to-all-start.3 = ((bf16[16,120,128]{2,1,0:T(8,128)(2,1)}), bf16[16,120,128]{2,1,0:T(8,128)(2,1)S(1)}, u32[]{:S(2)}, u32[]{:S(2)}) async-start(bf16[16,120,128]{2,1,0:T(8,128)(2,1)} %shard_map.156), calls=%async_computation.3 | async-start | bytes 983040 | tf_op jit(solution)/shard_map/all_to_all | solution.py:518
  85.0 1.4 %collective-permute-start.6 = (f32[144,128]{1,0:T(8,128)S(1)}, f32[144,128]{1,0:T(8,128)S(1)}, u32[]{:S(2)}, u32[]{:S(2)}) collective-permute-start(f32[144,128]{1,0:T(8,128)S(1)} %add_add_fusion), channel_id=1, source_target_pairs={{0,16},{16,0},{1,17},{17,1},{2,18},{18,2},{3,19},{19,3},{4,20},{20... | collective-permute-start | bytes 221192 | tf_op jit(solution)/shard_map/ppermute | solution.py:413

commit v7 on v5

--- a/solution.py
+++ b/solution.py
@@ -60,12 +60,12 @@
 SMEM = pl.BlockSpec(memory_space=pltpu.SMEM)
 
 
-def call(body, places, outs, flops=0, scratch=(), nbytes=1 << 20, vmem=16, out_place=VMEM):
+def call(body, places, outs, flops=0, scratch=(), nbytes=1 << 20, vmem=16, out_places=None):
     return pl.pallas_call(
         body,
-        out_shape=[jax.ShapeDtypeStruct(s, d) for s, d in outs],
+        out_shape=[jax.ShapeDtypeStruct(*o) if isinstance(o, tuple) else o for o in outs],
         in_specs=places,
-        out_specs=[out_place] * len(outs),
+        out_specs=out_places or [VMEM] * len(outs),
         scratch_shapes=list(scratch),
         compiler_params=pltpu.CompilerParams(vmem_limit_bytes=vmem << 20),
         cost_estimate=pl.CostEstimate(flops=flops, bytes_accessed=nbytes, transcendentals=0),
@@ -158,11 +158,13 @@
 
 
 def table_body(*refs):
-    factors, (w_ref, v_ref) = refs[:8], refs[8:10]
-    held, sems = refs[10:18], refs[18]
+    factors, (w_ref, v_hbm) = refs[:8], refs[8:10]
+    held, (v_ref, sems) = refs[10:18], refs[18:]
     for copy in fetch(factors, held, sems):
         copy.wait()
     fill_tables(held[:4], held[4:], w_ref, v_ref)
+    (copy,) = fetch((v_ref,), (v_hbm,), sems)
+    copy.wait()
 
 
 def flipped_table_body(*refs):
@@ -328,29 +330,30 @@
             other_ref[a, rows, :] = jnp.where(low, second, first).astype(BF16)
 
 
-def merge_body(band_ref, mine_ref, got_ref, o_hbm, o_ref, sems):
+def merge_body(band_ref, mine_ref, got_ref, o_ref):
     low = band_ref[0, 0] == 0
-    copies = []
     for a in range(LANES):
         mine, got = mine_ref[a, 0:CHUNK_MID, :].astype(F32), got_ref[a, 0:CHUNK_MID, :].astype(F32)
         o_ref[a, 0:CHUNK_MID, :] = jnp.where(low, mine, got).astype(BF16)
         o_ref[a, CHUNK_MID : 2 * CHUNK_MID, :] = jnp.where(low, got, mine).astype(BF16)
         mine, got = mine_ref[a, CHUNK_MID:, :].astype(F32), got_ref[a, CHUNK_MID:, :].astype(F32)
         o_ref[a, 2 * CHUNK_MID :, :] = (mine + got).astype(BF16)
-        if a % 4 == 3:
-            part = slice(a - 3, a + 1)
-            copies.append(pltpu.make_async_copy(o_ref.at[part], o_hbm.at[part], sems.at[a // 4]))
-            copies[-1].start()
-    for copy in copies:
-        copy.wait()
-
-
-def fields_body(r_ref, w_ref, v_ref, o_ref):
+
+
+def fields_body(r_ref, w_ref, v_hbm, o_ref, v_ref, sems):
+    (copy,) = fetch((v_hbm,), (v_ref,), sems)
     fields, outs = [], []
     for e in range(BANDS):
         start = CHUNK_MID * e
         sg = r_ref[:, start + M16 : start + CHUNK_MID, :].reshape(LANES * 2 * M12, 128)
         fields.append(dot(w_ref[e], sg))
+    for side in range(2):
+        lanes = slice(HALF * side, HALF * (side + 1))
+        field = fields[0] + fields[1] if side == 0 else fields[0] - fields[1]
+        o_ref[lanes, 0:WROWS, :] = field.astype(BF16).reshape(HALF, WROWS, 128)
+    copy.wait()
+    for e in range(BANDS):
+        start = CHUNK_MID * e
         c = r_ref[:, start : start + M16, :].reshape(LANES * M16, 128).astype(F32)
         turned = swap64(c)
         keep = low_half(c.shape)
@@ -360,8 +363,6 @@
         outs.append(jnp.where(low_half((count, 128)), got[:count], got[count:]))
     for side in range(2):
         lanes = slice(HALF * side, HALF * (side + 1))
-        field = fields[0] + fields[1] if side == 0 else fields[0] - fields[1]
-        o_ref[lanes, 0:WROWS, :] = field.astype(BF16).reshape(HALF, WROWS, 128)
         out = outs[0] + outs[1] if side == 0 else outs[0] - outs[1]
         o_ref[lanes, WROWS:CHUNK_IN, :] = out.astype(BF16).reshape(HALF, VROWS, 128)
 
@@ -461,27 +462,19 @@
             pltpu.VMEM((384, 256), F32),
         ],
     )(spot, landed.reshape(HIN, 2, CHUNK_MID, 128), placed, staged)
+    factors, mine, other = lax.optimization_barrier((factors, mine, other))
     got = swap_bands(other)
-    (sent,) = call(
-        merge_body,
-        [SMEM, VMEM, VMEM],
-        [((LANES, CHUNK_OUT, 128), BF16)],
-        nbytes=2 << 20,
-        scratch=[pltpu.VMEM((LANES, CHUNK_OUT, 128), BF16), dma((4,))],
-        out_place=HBM,
-    )(spot, mine, got)
-    landed = lax.all_to_all(sent, "azimuth", split_axis=0, concat_axis=0, tiled=True)
-
-    factors, sent = lax.optimization_barrier((factors, sent))
     tall, inv = call(
         table_body,
         [HBM] * 8,
-        [((2, 768, 384), BF16), ((2, 384, 512), BF16)],
+        [((2, 768, 384), BF16), pltpu.HBM((2, 384, 512), BF16)],
         nbytes=5 << 20,
-        scratch=held + [dma((8,))],
+        scratch=held + [pltpu.VMEM((2, 384, 512), BF16), dma((8,))],
+        out_places=[VMEM, HBM],
     )(*[in_hbm(a) for a in factors])
-
-    landed, tall, inv = lax.optimization_barrier((landed, tall, inv))
+    got, tall, inv = lax.optimization_barrier((got, tall, inv))
+    (sent,) = call(merge_body, [SMEM, VMEM, VMEM], [((LANES, CHUNK_OUT, 128), BF16)], nbytes=2 << 20)(spot, mine, got)
+    landed = lax.all_to_all(sent, "azimuth", split_axis=0, concat_axis=0, tiled=True)
 
     members = lax.axis_size("ens")
 
@@ -498,12 +491,18 @@
     behind = send(beside, 1, -1)
     half = (pair.astype(F32) + across.astype(F32)) + (beside.astype(F32) + behind.astype(F32))
     far = swap_bands(half)
-    (sent,) = call(fields_body, [VMEM] * 3, [((LANES, CHUNK_IN, 128), BF16)], flops=300 << 20)(landed, tall, inv)
+    (sent,) = call(
+        fields_body,
+        [VMEM, VMEM, HBM],
+        [((LANES, CHUNK_IN, 128), BF16)],
+        flops=300 << 20,
+        scratch=[pltpu.VMEM((2, 384, 512), BF16), dma((1,))],
+    )(landed, tall, in_hbm(inv))
     landed = lax.all_to_all(sent, "azimuth", split_axis=0, concat_axis=0, tiled=True)
-    weight_grad = jnp.concatenate([jnp.where(low, half, far), jnp.where(low, far, half)], axis=1)
     field_grad, conv_out = call(
         unpack_body, [VMEM], [((8 * WPART, C), BF16), ((VPART, 4, C), BF16)], scratch=[pltpu.VMEM((192, C), F32)]
     )(landed)
+    weight_grad = jnp.concatenate([jnp.where(low, half, far), jnp.where(low, far, half)], axis=1)
     field_grad = jnp.swapaxes(field_grad.reshape(WPART, 8, C), 0, 1)
     return (jnp.swapaxes(conv_out, 0, 1)[None], field_grad[None], weight_grad.reshape(K, 16, C))
 

time: 95.9 us -> 95.8 us (level)
  blocking collectives: 0 us -> 19.4 us
  waiting for transfers between devices: 39.2 us -> 23.7 us
  starting transfers between devices: 33.2 us -> 28.1 us
  Pallas kernels: 20.1 us -> 21.1 us
    all_to_all x0 -> x1, blocking collectives: none -> 19.4 us  [local(): lax.all_to_all(sent, 'azimuth', split_axis=0, concat_axis=0, tiled=True)]
    all_to_all x3 -> x2, waiting for transfers between devices: 24.9 us -> 11.7 us  [local(): lax.all_to_all(sent, 'azimuth', split_axis=0, concat_axis=0, tiled=True)]
    all_to_all x3 -> x2, starting transfers between devices: 17.4 us -> 12.3 us  [local(): lax.all_to_all(sent, 'azimuth', split_axis=0, concat_axis=0, tiled=True)]
    ppermute x3, waiting for transfers between devices: 3.47 us -> 1.25 us  [swap_bands(): return lax.ppermute(value, 'polar', [(0, 1), (1, 0)])]
    pallas_call x2, Pallas kernels: 3.28 us -> 5.11 us  [the longest x1 2.73 us: local(): call(fields_body, [VMEM, VMEM, HBM], [((LANES, CHUNK_IN, 128), BF16)], fl...]
  transfers between devices with their start and end apart: 11 -> 10, of which waited for: 8 -> 6; matrix products, arithmetic and copies ran while one was open for 1% -> 1% of each run, Pallas kernels for 10% -> 12%
where the time goes in v7:
time: 95.8 us; the launch traced here: 94.1 us
  starting transfers between devices  28.1 us (29%)
  waiting for transfers between devices  23.7 us (25%)
  Pallas kernels  21.1 us (22%)
  blocking collectives  19.4 us (20%)
    all_to_all x1, blocking collectives, local(): lax.all_to_all(sent, 'azimuth', split_axis=0, concat_axis=0, tiled=True)  19.4 us
    all_to_all x2, starting transfers between devices, local(): lax.all_to_all(sent, 'azimuth', split_axis=0, concat_axis=0, tiled=True)  12.3 us
    all_to_all x2, waiting for transfers between devices, local(): lax.all_to_all(sent, 'azimuth', split_axis=0, concat_axis=0, tiled=True)  11.7 us
    ppermute x4, starting transfers between devices, send(): return lax.ppermute(value, 'ens', pairs)  10.5 us
    all_to_all x1, waiting for transfers between devices, local(): lax.all_to_all(sent, JOINT, split_axis=0, concat_axis=0, tiled=True)  6.8 us
    all_to_all x1, starting transfers between devices, local(): lax.all_to_all(sent, JOINT, split_axis=0, concat_axis=0, tiled=True)  4.99 us
    pallas_call x1, Pallas kernels, local(): call(middle_body, [SMEM, VMEM, VMEM, VMEM], [(chunk, BF16), (chunk, BF16)...  4.09 us
    ppermute x4, waiting for transfers between devices, send(): return lax.ppermute(value, 'ens', pairs)  4 us
  transfers between devices with their start and end apart: 10, of which 6 were waited for; matrix products, arithmetic and copies ran while one was open for 1% of the time, Pallas kernels for 12%

profile of v7, /device:TPU:2, one launch (start us, length us, event | category | flops | bytes accessed | tf_op | source)
XLA Modules:
  0.0 94.1 jit_solution(1689052806997951293)
XLA Ops:
  0.6 2.3 %shard_map.148 = bf16[16,120,128]{2,1,0:T(8,128)(2,1)} custom-call(bf16[720,256]{1,0:T(8,128)(2,1)} %bitcast.26, bf16[45,4,256]{2,1,0:T(4,128)(2,1)} %bitcast.29), custom_call_target="tpu_custom_call" | custom-call | bytes 1048576 | tf_op jit(solution)/shard_map/pallas_call | solution.py:410
  3.0 7.5 %all-to-all-start = ((bf16[16,120,128]{2,1,0:T(8,128)(2,1)}), bf16[16,120,128]{2,1,0:T(8,128)(2,1)S(1)}, u32[]{:S(2)}, u32[]{:S(2)}) async-start(bf16[16,120,128]{2,1,0:T(8,128)(2,1)} %shard_map.148), calls=%async_computation | async-start | bytes 983040 | tf_op jit(solution)/shard_map/all_to_all | solution.py:423
  10.6 1.9 %shard_map.149 = (bf16[180,128]{1,0:T(8,128)(2,1)S(1)}, bf16[180,128]{1,0:T(8,128)(2,1)S(1)}) custom-call(s32[1,2]{1,0:T(1,128)S(1)} %add_bitcast_fusion.spot_ref.band_ref, s32[4,2]{1,0:T(4,128)S(1)} %copy.16.support_ref, bf16[45,4,720]{2,1,0:T(4,128)(2,1)} %bitcast.27), custom_call_target="tpu_custom_call" | custom-call | bytes 1048576 | tf_op jit(solution)/shard_map/pallas_call | solution.py:426
  12.6 2.6 %shard_map.150 = (bf16[2,384,768]{2,1,0:T(8,128)(2,1)S(1)}, bf16[2,512,384]{2,1,0:T(8,128)(2,1)S(1)}) custom-call(f32[2,8,384]{2,1,0:T(8,128)} %constant.30.clone.refs_0_, f32[2,8,384]{2,1,0:T(8,128)} %constant.31.clone.refs_1_, f32[2,96,384]{2,1,0:T(8,128)} %constant.32.clone.refs_2_, f32[2,96,384]{2,1,0:T(8,128)} %constant.33.clone.refs_3_, ...), custom_call_target="tpu_custom_call" | custom-call | bytes 5242880 | tf_op jit(solution)/shard_map/pallas_call | solution.py:436
  15.2 5.1 %all-to-all-done.r_ref = bf16[16,120,128]{2,1,0:T(8,128)(2,1)S(1)} async-done(((bf16[16,120,128]{2,1,0:T(8,128)(2,1)}), bf16[16,120,128]{2,1,0:T(8,128)(2,1)S(1)}, u32[]{:S(2)}, u32[]{:S(2)}) %all-to-all-start) | async-done | bytes 491552 | tf_op jit(solution)/shard_map/all_to_all | solution.py:423
  20.3 1.5 %shard_map.151 = bf16[32,40,128]{2,1,0:T(8,128)(2,1)} custom-call(bf16[16,120,128]{2,1,0:T(8,128)(2,1)S(1)} %all-to-all-done.r_ref, bf16[2,384,768]{2,1,0:T(8,128)(2,1)S(1)} %get-tuple-element.56.wt_ref, bf16[2,512,384]{2,1,0:T(8,128)(2,1)S(1)} %get-tuple-element.57.vt_ref), custom_call_target="tpu_custom_call" | custom-call | flops 314572800 | bytes 1048576 | tf_op jit(solution)/shard_map/pallas_call | solution.py:445
  21.7 5.0 %all-to-all-start.1 = ((bf16[32,40,128]{2,1,0:T(8,128)(2,1)}), bf16[32,40,128]{2,1,0:T(8,128)(2,1)S(1)}, u32[]{:S(2)}, u32[]{:S(2)}) async-start(bf16[32,40,128]{2,1,0:T(8,128)(2,1)} %shard_map.151), calls=%async_computation.1 | async-start | bytes 655360 | tf_op jit(solution)/shard_map/all_to_all | solution.py:446
  26.7 1.8 %shard_map.152 = (f32[144,384]{1,0:T(8,128)S(1)}, bf16[9,256,256]{2,1,0:T(8,128)(2,1)S(1)}) custom-call(s32[1,2]{1,0:T(1,128)S(1)} %add_bitcast_fusion.spot_ref.band_ref, bf16[180,128]{1,0:T(8,128)(2,1)S(1)} %get-tuple-element.60.mine_ref, bf16[180,128]{1,0:T(8,128)(2,1)S(1)} %collective-permute-done.got_ref, bf16[9,256,256]{2,1,0:T(8,128)(2,1)} %w_hbm.1), custom_call_target="tpu_custom_call" | custom-call | bytes 1048576 | tf_op jit(solution)/shard_map/pallas_call | solution.py:448
  28.6 6.8 %all-to-all-done.1 = bf16[32,40,128]{2,1,0:T(8,128)(2,1)S(1)} async-done(((bf16[32,40,128]{2,1,0:T(8,128)(2,1)}), bf16[32,40,128]{2,1,0:T(8,128)(2,1)S(1)}, u32[]{:S(2)}, u32[]{:S(2)}) %all-to-all-start.1) | async-done | bytes 327712 | tf_op jit(solution)/shard_map/all_to_all | solution.py:446
  35.4 4.1 %shard_map.153 = (bf16[16,184,128]{2,1,0:T(8,128)(2,1)S(1)}, bf16[16,184,128]{2,1,0:T(8,128)(2,1)S(1)}) custom-call(s32[1,2]{1,0:T(1,128)S(1)} %add_bitcast_fusion.spot_ref.band_ref, bf16[16,2,40,128]{3,2,1,0:T(8,128)(2,1)S(1)} %bitcast.25, f32[144,384]{1,0:T(8,128)S(1)} %get-tuple-element.62.p_ref, bf16[9,256,256]{2,1,0:T(8,128)(2,1)S(1)} %get-tuple-element.63.w_ref), custom_call_target="tpu_custom_call" | custom-call | flops 2147483648 | bytes 3145728 | tf_op jit(solution)/shard_map/pallas_call | solution.py:453
  39.6 2.4 %shard_map.154 = (bf16[2,768,384]{2,1,0:T(8,128)(2,1)S(1)}, bf16[2,384,512]{2,1,0:T(8,128)(2,1)}) custom-call(f32[2,8,384]{2,1,0:T(8,128)} %constant.30.clone.refs_0_, f32[2,8,384]{2,1,0:T(8,128)} %constant.31.clone.refs_1_, f32[2,96,384]{2,1,0:T(8,128)} %constant.32.clone.refs_2_, f32[2,96,384]{2,1,0:T(8,128)} %constant.33.clone.refs_3_, ...), custom_call_target="tpu_custom_call" | custom-call | bytes 5242880 | tf_op jit(solution)/shard_map/pallas_call | solution.py:467
  42.0 0.8 shard_map.155
  42.7 19.4 %all_to_all.20.r_ref = bf16[16,224,128]{2,1,0:T(8,128)(2,1)S(1)} all-to-all(bf16[16,224,128]{2,1,0:T(8,128)(2,1)S(1)} %shard_map.155), channel_id=1, replica_groups=mesh['ens'=8,'polar'=2,'azimuth'=16] {'azimuth'}, dimensions={0} | all-to-all | bytes 1835008 | tf_op jit(solution)/shard_map/all_to_all | solution.py:477
  62.2 2.0 %collective-permute-start.2 = (bf16[144,128]{1,0:T(8,128)(2,1)S(1)}, bf16[144,128]{1,0:T(8,128)(2,1)S(1)}, u32[]{:S(2)}, u32[]{:S(2)}) collective-permute-start(bf16[144,128]{1,0:T(8,128)(2,1)S(1)} %slice_reduce_fusion), channel_id=1, source_target_pairs={{0,32},{32,0},{64,96},{96,64},{128,160},{160,128},{192,224},{224,1... | collective-permute-start | bytes 110600 | tf_op jit(solution)/shard_map/ppermute | solution.py:484
  64.2 2.1 %collective-permute-done.2 = bf16[144,128]{1,0:T(8,128)(2,1)S(1)} collective-permute-done((bf16[144,128]{1,0:T(8,128)(2,1)S(1)}, bf16[144,128]{1,0:T(8,128)(2,1)S(1)}, u32[]{:S(2)}, u32[]{:S(2)}) %collective-permute-start.2) | collective-permute-done | bytes 36896 | tf_op jit(solution)/shard_map/ppermute | solution.py:484
  66.3 5.9 %collective-permute-start.3 = (bf16[144,128]{1,0:T(8,128)(2,1)S(1)}, bf16[144,128]{1,0:T(8,128)(2,1)S(1)}, u32[]{:S(2)}, u32[]{:S(2)}) collective-permute-start(bf16[144,128]{1,0:T(8,128)(2,1)S(1)} %add_convert_fusion), channel_id=1, source_target_pairs={{0,224},{32,64},{64,32},{96,128},{128,96},{160,192},{192,160},{224... | collective-permute-start | bytes 110600 | tf_op jit(solution)/shard_map/ppermute | solution.py:484
  72.2 1.9 %collective-permute-done.3 = bf16[144,128]{1,0:T(8,128)(2,1)S(1)} collective-permute-done((bf16[144,128]{1,0:T(8,128)(2,1)S(1)}, bf16[144,128]{1,0:T(8,128)(2,1)S(1)}, u32[]{:S(2)}, u32[]{:S(2)}) %collective-permute-start.3) | collective-permute-done | bytes 36896 | tf_op jit(solution)/shard_map/ppermute | solution.py:484
  74.2 2.6 %collective-permute-start.4 = (bf16[144,128]{1,0:T(8,128)(2,1)S(1)}, bf16[144,128]{1,0:T(8,128)(2,1)S(1)}, u32[]{:S(2)}, u32[]{:S(2)}) collective-permute-start(bf16[144,128]{1,0:T(8,128)(2,1)S(1)} %collective-permute-done.3), channel_id=1, source_target_pairs={{0,64},{32,224},{64,128},{96,32},{128,192},{160,96},{192,0},{224,1... | collective-permute-start | bytes 110600 | tf_op jit(solution)/shard_map/ppermute | solution.py:484
  76.7 2.7 %shard_map.156 = bf16[16,120,128]{2,1,0:T(8,128)(2,1)} custom-call(bf16[16,224,128]{2,1,0:T(8,128)(2,1)S(1)} %all_to_all.20.r_ref, bf16[2,768,384]{2,1,0:T(8,128)(2,1)S(1)} %get-tuple-element.79.w_ref, bf16[2,384,512]{2,1,0:T(8,128)(2,1)} %get-tuple-element.80.v_hbm), custom_call_target="tpu_custom_call" | custom-call | flops 314572800 | bytes 1048576 | tf_op jit(solution)/shard_map/pallas_call | solution.py:494
  79.5 4.8 %all-to-all-start.3 = ((bf16[16,120,128]{2,1,0:T(8,128)(2,1)}), bf16[16,120,128]{2,1,0:T(8,128)(2,1)S(1)}, u32[]{:S(2)}, u32[]{:S(2)}) async-start(bf16[16,120,128]{2,1,0:T(8,128)(2,1)} %shard_map.156), calls=%async_computation.3 | async-start | bytes 983040 | tf_op jit(solution)/shard_map/all_to_all | solution.py:501
  84.4 1.2 %collective-permute-done.6 = f32[144,128]{1,0:T(8,128)S(1)} collective-permute-done((f32[144,128]{1,0:T(8,128)S(1)}, f32[144,128]{1,0:T(8,128)S(1)}, u32[]{:S(2)}, u32[]{:S(2)}) %collective-permute-start.6) | collective-permute-done | bytes 73760 | tf_op jit(solution)/shard_map/ppermute | solution.py:401
  85.7 0.7 pad_maximum_fusion
  86.4 6.6 %all-to-all-done.3.r_ref = bf16[16,120,128]{2,1,0:T(8,128)(2,1)S(1)} async-done(((bf16[16,120,128]{2,1,0:T(8,128)(2,1)}), bf16[16,120,128]{2,1,0:T(8,128)(2,1)S(1)}, u32[]{:S(2)}, u32[]{:S(2)}) %all-to-all-start.3) | async-done | bytes 491552 | tf_op jit(solution)/shard_map/all_to_all | solution.py:501
  93.0 1.1 %shard_map.157 = (bf16[720,256]{1,0:T(8,128)(2,1)}, bf16[45,4,256]{2,1,0:T(4,128)(2,1)}) custom-call(bf16[16,120,128]{2,1,0:T(8,128)(2,1)S(1)} %all-to-all-done.3.r_ref), custom_call_target="tpu_custom_call" | custom-call | bytes 1048576 | tf_op jit(solution)/shard_map/pallas_call | solution.py:502
  (16 shorter events, 0.6 us)
Async XLA Ops:
  0.6 9.8 %copy-start = (s32[4,2]{0,1:T(2,128)S(1)}, s32[4,2]{0,1:T(2,128)}, u32[]{:S(2)}) copy-start(s32[4,2]{0,1:T(2,128)} %param.15) | copy-start | bytes 100
  3.0 17.3 %all-to-all-start = ((bf16[16,120,128]{2,1,0:T(8,128)(2,1)}), bf16[16,120,128]{2,1,0:T(8,128)(2,1)S(1)}, u32[]{:S(2)}, u32[]{:S(2)}) async-start(bf16[16,120,128]{2,1,0:T(8,128)(2,1)} %shard_map.148), calls=%async_computation | async-start | bytes 983040 | tf_op jit(solution)/shard_map/all_to_all | solution.py:423
  12.5 2.7 %collective-permute-start = (bf16[180,128]{1,0:T(8,128)(2,1)S(1)}, bf16[180,128]{1,0:T(8,128)(2,1)S(1)}, u32[]{:S(2)}, u32[]{:S(2)}) collective-permute-start(bf16[180,128]{1,0:T(8,128)(2,1)S(1)} %get-tuple-element.54), channel_id=1, source_target_pairs={{0,16},{16,0},{1,17},{17,1},{2,18},{18,2},{3,19},{19,3},{4,20},{20... | collective-permute-start | bytes 138248 | tf_op jit(solution)/shard_map/ppermute | solution.py:401
  21.7 13.6 %all-to-all-start.1 = ((bf16[32,40,128]{2,1,0:T(8,128)(2,1)}), bf16[32,40,128]{2,1,0:T(8,128)(2,1)S(1)}, u32[]{:S(2)}, u32[]{:S(2)}) async-start(bf16[32,40,128]{2,1,0:T(8,128)(2,1)} %shard_map.151), calls=%async_computation.1 | async-start | bytes 655360 | tf_op jit(solution)/shard_map/all_to_all | solution.py:446
  39.5 2.5 %collective-permute-start.1 = (bf16[16,184,128]{2,1,0:T(8,128)(2,1)S(1)}, bf16[16,184,128]{2,1,0:T(8,128)(2,1)S(1)}, u32[]{:S(2)}, u32[]{:S(2)}) collective-permute-start(bf16[16,184,128]{2,1,0:T(8,128)(2,1)S(1)} %get-tuple-element.67), channel_id=1, source_target_pairs={{0,16},{16,0},{1,17},{17,1},{2,18},{18,2},{3,19},{19,3},{4,20},{20... | collective-permute-start | bytes 2261000 | tf_op jit(solution)/shard_map/ppermute | solution.py:401
  62.2 4.0 %collective-permute-start.2 = (bf16[144,128]{1,0:T(8,128)(2,1)S(1)}, bf16[144,128]{1,0:T(8,128)(2,1)S(1)}, u32[]{:S(2)}, u32[]{:S(2)}) collective-permute-start(bf16[144,128]{1,0:T(8,128)(2,1)S(1)} %slice_reduce_fusion), channel_id=1, source_target_pairs={{0,32},{32,0},{64,96},{96,64},{128,160},{160,128},{192,224},{224,1... | collective-permute-start | bytes 110600 | tf_op jit(solution)/shard_map/ppermute | solution.py:484
  66.3 7.9 %collective-permute-start.3 = (bf16[144,128]{1,0:T(8,128)(2,1)S(1)}, bf16[144,128]{1,0:T(8,128)(2,1)S(1)}, u32[]{:S(2)}, u32[]{:S(2)}) collective-permute-start(bf16[144,128]{1,0:T(8,128)(2,1)S(1)} %add_convert_fusion), channel_id=1, source_target_pairs={{0,224},{32,64},{64,32},{96,128},{128,96},{160,192},{192,160},{224... | collective-permute-start | bytes 110600 | tf_op jit(solution)/shard_map/ppermute | solution.py:484
  74.2 10.1 %collective-permute-start.5 = (bf16[144,128]{1,0:T(8,128)(2,1)S(1)}, bf16[144,128]{1,0:T(8,128)(2,1)S(1)}, u32[]{:S(2)}, u32[]{:S(2)}) collective-permute-start(bf16[144,128]{1,0:T(8,128)(2,1)S(1)} %collective-permute-done.3), channel_id=1, source_target_pairs={{0,32},{32,0},{64,96},{96,64},{128,160},{160,128},{192,224},{224,1... | collective-permute-start | bytes 110600 | tf_op jit(solution)/shard_map/ppermute | solution.py:484
  74.2 10.1 %collective-permute-start.4 = (bf16[144,128]{1,0:T(8,128)(2,1)S(1)}, bf16[144,128]{1,0:T(8,128)(2,1)S(1)}, u32[]{:S(2)}, u32[]{:S(2)}) collective-permute-start(bf16[144,128]{1,0:T(8,128)(2,1)S(1)} %collective-permute-done.3), channel_id=1, source_target_pairs={{0,64},{32,224},{64,128},{96,32},{128,192},{160,96},{192,0},{224,1... | collective-permute-start | bytes 110600 | tf_op jit(solution)/shard_map/ppermute | solution.py:484
  79.5 13.5 %all-to-all-start.3 = ((bf16[16,120,128]{2,1,0:T(8,128)(2,1)}), bf16[16,120,128]{2,1,0:T(8,128)(2,1)S(1)}, u32[]{:S(2)}, u32[]{:S(2)}) async-start(bf16[16,120,128]{2,1,0:T(8,128)(2,1)} %shard_map.156), calls=%async_computation.3 | async-start | bytes 983040 | tf_op jit(solution)/shard_map/all_to_all | solution.py:501
  84.3 1.4 %collective-permute-start.6 = (f32[144,128]{1,0:T(8,128)S(1)}, f32[144,128]{1,0:T(8,128)S(1)}, u32[]{:S(2)}, u32[]{:S(2)}) collective-permute-start(f32[144,128]{1,0:T(8,128)S(1)} %add_add_fusion), channel_id=1, source_target_pairs={{0,16},{16,0},{1,17},{17,1},{2,18},{18,2},{3,19},{19,3},{4,20},{20... | collective-permute-start | bytes 221192 | tf_op jit(solution)/shard_map/ppermute | solution.py:401

commit v8 on v7

--- a/solution.py
+++ b/solution.py
@@ -143,12 +143,17 @@
             target[128 * j : 128 * (j + 1), 128 * i : 128 * (i + 1)] = piece.T.astype(BF16)
 
 
-def fill_tables(w, v, w_ref, v_ref):
+def fill_wide(w, w_ref):
     for e in range(BANDS):
         for b in range(HALF):
             one, two = w[0][e, b : b + 1, :], w[1][e, b : b + 1, :]
             block = one * w[2][e] + two * w[3][e]
             w_ref[e, WROWS * b : WROWS * (b + 1), :] = block.astype(BF16)
+
+
+def fill_narrow(v, v_ref):
+    for e in range(BANDS):
+        for b in range(HALF):
             one, two = v[0][e, b : b + 1, :], v[1][e, b : b + 1, :]
             for part in range(2):
                 rows = slice(VROWS * part, VROWS * (part + 1))
@@ -159,12 +164,16 @@
 
 def table_body(*refs):
     factors, (w_ref, v_hbm) = refs[:8], refs[8:10]
-    held, (v_ref, sems) = refs[10:18], refs[18:]
-    for copy in fetch(factors, held, sems):
+    held, (v_ref, sems, out_sem) = refs[10:18], refs[18:]
+    copies = fetch(factors[4:] + factors[:4], held[4:] + held[:4], sems)
+    for copy in copies[:4]:
         copy.wait()
-    fill_tables(held[:4], held[4:], w_ref, v_ref)
-    (copy,) = fetch((v_ref,), (v_hbm,), sems)
-    copy.wait()
+    fill_narrow(held[4:], v_ref)
+    (out,) = fetch((v_ref,), (v_hbm,), out_sem)
+    for copy in copies[4:]:
+        copy.wait()
+    fill_wide(held[:4], w_ref)
+    out.wait()
 
 
 def flipped_table_body(*refs):
@@ -172,7 +181,8 @@
     held, (w_ref, v_ref, sems) = refs[10:18], refs[18:]
     for copy in fetch(factors, held, sems):
         copy.wait()
-    fill_tables(held[:4], held[4:], w_ref, v_ref)
+    fill_wide(held[:4], w_ref)
+    fill_narrow(held[4:], v_ref)
     for e in range(BANDS):
         flip(w_ref.at[e], wt_ref.at[e], HALF * WROWS, 2 * LANES * M12)
         flip(v_ref.at[e], vt_ref.at[e], 2 * HALF * VROWS, 2 * LANES * M16)
@@ -341,7 +351,7 @@
 
 
 def fields_body(r_ref, w_ref, v_hbm, o_ref, v_ref, sems):
-    (copy,) = fetch((v_hbm,), (v_ref,), sems)
+    copies = fetch((v_hbm.at[0], v_hbm.at[1]), (v_ref.at[0], v_ref.at[1]), sems)
     fields, outs = [], []
     for e in range(BANDS):
         start = CHUNK_MID * e
@@ -351,8 +361,8 @@
         lanes = slice(HALF * side, HALF * (side + 1))
         field = fields[0] + fields[1] if side == 0 else fields[0] - fields[1]
         o_ref[lanes, 0:WROWS, :] = field.astype(BF16).reshape(HALF, WROWS, 128)
-    copy.wait()
     for e in range(BANDS):
+        copies[e].wait()
         start = CHUNK_MID * e
         c = r_ref[:, start : start + M16, :].reshape(LANES * M16, 128).astype(F32)
         turned = swap64(c)
@@ -469,7 +479,7 @@
         [HBM] * 8,
         [((2, 768, 384), BF16), pltpu.HBM((2, 384, 512), BF16)],
         nbytes=5 << 20,
-        scratch=held + [pltpu.VMEM((2, 384, 512), BF16), dma((8,))],
+        scratch=held + [pltpu.VMEM((2, 384, 512), BF16), dma((8,)), dma((1,))],
         out_places=[VMEM, HBM],
     )(*[in_hbm(a) for a in factors])
     got, tall, inv = lax.optimization_barrier((got, tall, inv))
@@ -487,8 +497,8 @@
     got = send(half, 1, -1)
     pair = (half.astype(F32) + got.astype(F32)).astype(BF16)
     beside = send(pair, -1, 1)
+    behind = send(pair, -2, 2)
     across = send(beside, 2, -2)
-    behind = send(beside, 1, -1)
     half = (pair.astype(F32) + across.astype(F32)) + (beside.astype(F32) + behind.astype(F32))
     far = swap_bands(half)
     (sent,) = call(
@@ -496,7 +506,7 @@
         [VMEM, VMEM, HBM],
         [((LANES, CHUNK_IN, 128), BF16)],
         flops=300 << 20,
-        scratch=[pltpu.VMEM((2, 384, 512), BF16), dma((1,))],
+        scratch=[pltpu.VMEM((2, 384, 512), BF16), dma((2,))],
     )(landed, tall, in_hbm(inv))
     landed = lax.all_to_all(sent, "azimuth", split_axis=0, concat_axis=0, tiled=True)
     field_grad, conv_out = call(

time: 95.8 us -> 95.9 us (level)
  the two profiles are of different devices: /device:TPU:2 before, /device:TPU:32 now
where the time goes in v8:
time: 95.9 us; the launch traced here: 95.3 us
  waiting for transfers between devices  27.4 us (29%)
  starting transfers between devices  25.6 us (27%)
  Pallas kernels  21.2 us (22%)
  blocking collectives  19.3 us (20%)
    all_to_all x1, blocking collectives, local(): lax.all_to_all(sent, 'azimuth', split_axis=0, concat_axis=0, tiled=True)  19.3 us
    all_to_all x2, waiting for transfers between devices, local(): lax.all_to_all(sent, 'azimuth', split_axis=0, concat_axis=0, tiled=True)  14.3 us
    ppermute x4, starting transfers between devices, send(): return lax.ppermute(value, 'ens', pairs)  10.9 us
    all_to_all x2, starting transfers between devices, local(): lax.all_to_all(sent, 'azimuth', split_axis=0, concat_axis=0, tiled=True)  10.6 us
    all_to_all x1, waiting for transfers between devices, local(): lax.all_to_all(sent, JOINT, split_axis=0, concat_axis=0, tiled=True)  8.01 us
    pallas_call x1, Pallas kernels, local(): call(middle_body, [SMEM, VMEM, VMEM, VMEM], [(chunk, BF16), (chunk, BF16)...  4.09 us
    all_to_all x1, starting transfers between devices, local(): lax.all_to_all(sent, JOINT, split_axis=0, concat_axis=0, tiled=True)  3.88 us
    ppermute x4, waiting for transfers between devices, send(): return lax.ppermute(value, 'ens', pairs)  3.85 us
  transfers between devices with their start and end apart: 10, of which 5 were waited for; matrix products, arithmetic and copies ran while one was open for 1% of the time, Pallas kernels for 12%

profile of v8, /device:TPU:32, one launch (start us, length us, event | category | flops | bytes accessed | tf_op | source)
XLA Modules:
  0.0 95.3 jit_solution(4164105914809959182)
XLA Ops:
  0.6 2.3 %shard_map.148 = bf16[16,120,128]{2,1,0:T(8,128)(2,1)} custom-call(bf16[720,256]{1,0:T(8,128)(2,1)} %bitcast.26, bf16[45,4,256]{2,1,0:T(4,128)(2,1)} %bitcast.29), custom_call_target="tpu_custom_call" | custom-call | bytes 1048576 | tf_op jit(solution)/shard_map/pallas_call | solution.py:420
  3.0 7.0 %all-to-all-start = ((bf16[16,120,128]{2,1,0:T(8,128)(2,1)}), bf16[16,120,128]{2,1,0:T(8,128)(2,1)S(1)}, u32[]{:S(2)}, u32[]{:S(2)}) async-start(bf16[16,120,128]{2,1,0:T(8,128)(2,1)} %shard_map.148), calls=%async_computation | async-start | bytes 983040 | tf_op jit(solution)/shard_map/all_to_all | solution.py:433
  10.2 1.9 %shard_map.149 = (bf16[180,128]{1,0:T(8,128)(2,1)S(1)}, bf16[180,128]{1,0:T(8,128)(2,1)S(1)}) custom-call(s32[1,2]{1,0:T(1,128)S(1)} %add_bitcast_fusion.spot_ref.band_ref, s32[4,2]{1,0:T(4,128)S(1)} %copy.16.support_ref, bf16[45,4,720]{2,1,0:T(4,128)(2,1)} %bitcast.27), custom_call_target="tpu_custom_call" | custom-call | bytes 1048576 | tf_op jit(solution)/shard_map/pallas_call | solution.py:436
  12.2 2.6 %shard_map.150 = (bf16[2,384,768]{2,1,0:T(8,128)(2,1)S(1)}, bf16[2,512,384]{2,1,0:T(8,128)(2,1)S(1)}) custom-call(f32[2,8,384]{2,1,0:T(8,128)} %constant.30.clone.refs_0_, f32[2,8,384]{2,1,0:T(8,128)} %constant.31.clone.refs_1_, f32[2,96,384]{2,1,0:T(8,128)} %constant.32.clone.refs_2_, f32[2,96,384]{2,1,0:T(8,128)} %constant.33.clone.refs_3_, ...), custom_call_target="tpu_custom_call" | custom-call | bytes 5242880 | tf_op jit(solution)/shard_map/pallas_call | solution.py:446
  14.8 6.4 %all-to-all-done.r_ref = bf16[16,120,128]{2,1,0:T(8,128)(2,1)S(1)} async-done(((bf16[16,120,128]{2,1,0:T(8,128)(2,1)}), bf16[16,120,128]{2,1,0:T(8,128)(2,1)S(1)}, u32[]{:S(2)}, u32[]{:S(2)}) %all-to-all-start) | async-done | bytes 491552 | tf_op jit(solution)/shard_map/all_to_all | solution.py:433
  21.2 1.5 %shard_map.151 = bf16[32,40,128]{2,1,0:T(8,128)(2,1)} custom-call(bf16[16,120,128]{2,1,0:T(8,128)(2,1)S(1)} %all-to-all-done.r_ref, bf16[2,384,768]{2,1,0:T(8,128)(2,1)S(1)} %get-tuple-element.56.wt_ref, bf16[2,512,384]{2,1,0:T(8,128)(2,1)S(1)} %get-tuple-element.57.vt_ref), custom_call_target="tpu_custom_call" | custom-call | flops 314572800 | bytes 1048576 | tf_op jit(solution)/shard_map/pallas_call | solution.py:455
  22.7 3.9 %all-to-all-start.1 = ((bf16[32,40,128]{2,1,0:T(8,128)(2,1)}), bf16[32,40,128]{2,1,0:T(8,128)(2,1)S(1)}, u32[]{:S(2)}, u32[]{:S(2)}) async-start(bf16[32,40,128]{2,1,0:T(8,128)(2,1)} %shard_map.151), calls=%async_computation.1 | async-start | bytes 655360 | tf_op jit(solution)/shard_map/all_to_all | solution.py:456
  26.6 1.8 %shard_map.152 = (f32[144,384]{1,0:T(8,128)S(1)}, bf16[9,256,256]{2,1,0:T(8,128)(2,1)S(1)}) custom-call(s32[1,2]{1,0:T(1,128)S(1)} %add_bitcast_fusion.spot_ref.band_ref, bf16[180,128]{1,0:T(8,128)(2,1)S(1)} %get-tuple-element.60.mine_ref, bf16[180,128]{1,0:T(8,128)(2,1)S(1)} %collective-permute-done.got_ref, bf16[9,256,256]{2,1,0:T(8,128)(2,1)} %w_hbm.1), custom_call_target="tpu_custom_call" | custom-call | bytes 1048576 | tf_op jit(solution)/shard_map/pallas_call | solution.py:458
  28.4 8.0 %all-to-all-done.1 = bf16[32,40,128]{2,1,0:T(8,128)(2,1)S(1)} async-done(((bf16[32,40,128]{2,1,0:T(8,128)(2,1)}), bf16[32,40,128]{2,1,0:T(8,128)(2,1)S(1)}, u32[]{:S(2)}, u32[]{:S(2)}) %all-to-all-start.1) | async-done | bytes 327712 | tf_op jit(solution)/shard_map/all_to_all | solution.py:456
  36.4 4.1 %shard_map.153 = (bf16[16,184,128]{2,1,0:T(8,128)(2,1)S(1)}, bf16[16,184,128]{2,1,0:T(8,128)(2,1)S(1)}) custom-call(s32[1,2]{1,0:T(1,128)S(1)} %add_bitcast_fusion.spot_ref.band_ref, bf16[16,2,40,128]{3,2,1,0:T(8,128)(2,1)S(1)} %bitcast.25, f32[144,384]{1,0:T(8,128)S(1)} %get-tuple-element.62.p_ref, bf16[9,256,256]{2,1,0:T(8,128)(2,1)S(1)} %get-tuple-element.63.w_ref), custom_call_target="tpu_custom_call" | custom-call | flops 2147483648 | bytes 3145728 | tf_op jit(solution)/shard_map/pallas_call | solution.py:463
  40.6 2.2 %shard_map.154 = (bf16[2,768,384]{2,1,0:T(8,128)(2,1)S(1)}, bf16[2,384,512]{2,1,0:T(8,128)(2,1)}) custom-call(f32[2,8,384]{2,1,0:T(8,128)} %constant.30.clone.refs_0_, f32[2,8,384]{2,1,0:T(8,128)} %constant.31.clone.refs_1_, f32[2,96,384]{2,1,0:T(8,128)} %constant.32.clone.refs_2_, f32[2,96,384]{2,1,0:T(8,128)} %constant.33.clone.refs_3_, ...), custom_call_target="tpu_custom_call" | custom-call | bytes 5242880 | tf_op jit(solution)/shard_map/pallas_call | solution.py:477
  42.8 0.8 shard_map.155
  43.6 19.3 %all_to_all.20.r_ref = bf16[16,224,128]{2,1,0:T(8,128)(2,1)S(1)} all-to-all(bf16[16,224,128]{2,1,0:T(8,128)(2,1)S(1)} %shard_map.155), channel_id=1, replica_groups=mesh['ens'=8,'polar'=2,'azimuth'=16] {'azimuth'}, dimensions={0} | all-to-all | bytes 1835008 | tf_op jit(solution)/shard_map/all_to_all | solution.py:487
  63.0 0.2 collective-permute-start.2
  63.2 3.8 %collective-permute-done.2 = bf16[144,128]{1,0:T(8,128)(2,1)S(1)} collective-permute-done((bf16[144,128]{1,0:T(8,128)(2,1)S(1)}, bf16[144,128]{1,0:T(8,128)(2,1)S(1)}, u32[]{:S(2)}, u32[]{:S(2)}) %collective-permute-start.2) | collective-permute-done | bytes 36896 | tf_op jit(solution)/shard_map/ppermute | solution.py:494
  67.0 2.0 %collective-permute-start.3 = (bf16[144,128]{1,0:T(8,128)(2,1)S(1)}, bf16[144,128]{1,0:T(8,128)(2,1)S(1)}, u32[]{:S(2)}, u32[]{:S(2)}) collective-permute-start(bf16[144,128]{1,0:T(8,128)(2,1)S(1)} %add_convert_fusion), channel_id=1, source_target_pairs={{0,224},{32,64},{64,32},{96,128},{128,96},{160,192},{192,160},{224... | collective-permute-start | bytes 110600 | tf_op jit(solution)/shard_map/ppermute | solution.py:494
  69.0 4.5 %collective-permute-start.5 = (bf16[144,128]{1,0:T(8,128)(2,1)S(1)}, bf16[144,128]{1,0:T(8,128)(2,1)S(1)}, u32[]{:S(2)}, u32[]{:S(2)}) collective-permute-start(bf16[144,128]{1,0:T(8,128)(2,1)S(1)} %add_convert_fusion), channel_id=1, source_target_pairs={{0,192},{32,96},{64,0},{96,160},{128,64},{160,224},{192,128},{224,... | collective-permute-start | bytes 110600 | tf_op jit(solution)/shard_map/ppermute | solution.py:494
  73.5 4.2 %collective-permute-start.4 = (bf16[144,128]{1,0:T(8,128)(2,1)S(1)}, bf16[144,128]{1,0:T(8,128)(2,1)S(1)}, u32[]{:S(2)}, u32[]{:S(2)}) collective-permute-start(bf16[144,128]{1,0:T(8,128)(2,1)S(1)} %collective-permute-done.3), channel_id=1, source_target_pairs={{0,64},{32,224},{64,128},{96,32},{128,192},{160,96},{192,0},{224,1... | collective-permute-start | bytes 110600 | tf_op jit(solution)/shard_map/ppermute | solution.py:494
  77.7 3.0 %shard_map.156 = bf16[16,120,128]{2,1,0:T(8,128)(2,1)} custom-call(bf16[16,224,128]{2,1,0:T(8,128)(2,1)S(1)} %all_to_all.20.r_ref, bf16[2,768,384]{2,1,0:T(8,128)(2,1)S(1)} %get-tuple-element.79.w_ref, bf16[2,384,512]{2,1,0:T(8,128)(2,1)} %get-tuple-element.80.v_hbm), custom_call_target="tpu_custom_call" | custom-call | flops 314572800 | bytes 1048576 | tf_op jit(solution)/shard_map/pallas_call | solution.py:504
  80.7 3.6 %all-to-all-start.3 = ((bf16[16,120,128]{2,1,0:T(8,128)(2,1)}), bf16[16,120,128]{2,1,0:T(8,128)(2,1)S(1)}, u32[]{:S(2)}, u32[]{:S(2)}) async-start(bf16[16,120,128]{2,1,0:T(8,128)(2,1)} %shard_map.156), calls=%async_computation.3 | async-start | bytes 983040 | tf_op jit(solution)/shard_map/all_to_all | solution.py:511
  84.4 1.2 %collective-permute-done.6 = f32[144,128]{1,0:T(8,128)S(1)} collective-permute-done((f32[144,128]{1,0:T(8,128)S(1)}, f32[144,128]{1,0:T(8,128)S(1)}, u32[]{:S(2)}, u32[]{:S(2)}) %collective-permute-start.6) | collective-permute-done | bytes 73760 | tf_op jit(solution)/shard_map/ppermute | solution.py:411
  85.7 0.7 pad_maximum_fusion
  86.4 7.8 %all-to-all-done.3.r_ref = bf16[16,120,128]{2,1,0:T(8,128)(2,1)S(1)} async-done(((bf16[16,120,128]{2,1,0:T(8,128)(2,1)}), bf16[16,120,128]{2,1,0:T(8,128)(2,1)S(1)}, u32[]{:S(2)}, u32[]{:S(2)}) %all-to-all-start.3) | async-done | bytes 491552 | tf_op jit(solution)/shard_map/all_to_all | solution.py:511
  94.2 1.1 %shard_map.157 = (bf16[720,256]{1,0:T(8,128)(2,1)}, bf16[45,4,256]{2,1,0:T(4,128)(2,1)}) custom-call(bf16[16,120,128]{2,1,0:T(8,128)(2,1)S(1)} %all-to-all-done.3.r_ref), custom_call_target="tpu_custom_call" | custom-call | bytes 1048576 | tf_op jit(solution)/shard_map/pallas_call | solution.py:512
  (16 shorter events, 0.6 us)
Async XLA Ops:
  0.6 9.4 %copy-start = (s32[4,2]{0,1:T(2,128)S(1)}, s32[4,2]{0,1:T(2,128)}, u32[]{:S(2)}) copy-start(s32[4,2]{0,1:T(2,128)} %param.15) | copy-start | bytes 100
  3.0 18.2 %all-to-all-start = ((bf16[16,120,128]{2,1,0:T(8,128)(2,1)}), bf16[16,120,128]{2,1,0:T(8,128)(2,1)S(1)}, u32[]{:S(2)}, u32[]{:S(2)}) async-start(bf16[16,120,128]{2,1,0:T(8,128)(2,1)} %shard_map.148), calls=%async_computation | async-start | bytes 983040 | tf_op jit(solution)/shard_map/all_to_all | solution.py:433
  12.1 2.7 %collective-permute-start = (bf16[180,128]{1,0:T(8,128)(2,1)S(1)}, bf16[180,128]{1,0:T(8,128)(2,1)S(1)}, u32[]{:S(2)}, u32[]{:S(2)}) collective-permute-start(bf16[180,128]{1,0:T(8,128)(2,1)S(1)} %get-tuple-element.54), channel_id=1, source_target_pairs={{0,16},{16,0},{1,17},{17,1},{2,18},{18,2},{3,19},{19,3},{4,20},{20... | collective-permute-start | bytes 138248 | tf_op jit(solution)/shard_map/ppermute | solution.py:411
  22.7 13.7 %all-to-all-start.1 = ((bf16[32,40,128]{2,1,0:T(8,128)(2,1)}), bf16[32,40,128]{2,1,0:T(8,128)(2,1)S(1)}, u32[]{:S(2)}, u32[]{:S(2)}) async-start(bf16[32,40,128]{2,1,0:T(8,128)(2,1)} %shard_map.151), calls=%async_computation.1 | async-start | bytes 655360 | tf_op jit(solution)/shard_map/all_to_all | solution.py:456
  40.5 2.3 %collective-permute-start.1 = (bf16[16,184,128]{2,1,0:T(8,128)(2,1)S(1)}, bf16[16,184,128]{2,1,0:T(8,128)(2,1)S(1)}, u32[]{:S(2)}, u32[]{:S(2)}) collective-permute-start(bf16[16,184,128]{2,1,0:T(8,128)(2,1)S(1)} %get-tuple-element.67), channel_id=1, source_target_pairs={{0,16},{16,0},{1,17},{17,1},{2,18},{18,2},{3,19},{19,3},{4,20},{20... | collective-permute-start | bytes 2261000 | tf_op jit(solution)/shard_map/ppermute | solution.py:411
  63.0 4.0 %collective-permute-start.2 = (bf16[144,128]{1,0:T(8,128)(2,1)S(1)}, bf16[144,128]{1,0:T(8,128)(2,1)S(1)}, u32[]{:S(2)}, u32[]{:S(2)}) collective-permute-start(bf16[144,128]{1,0:T(8,128)(2,1)S(1)} %slice_reduce_fusion), channel_id=1, source_target_pairs={{0,32},{32,0},{64,96},{96,64},{128,160},{160,128},{192,224},{224,1... | collective-permute-start | bytes 110600 | tf_op jit(solution)/shard_map/ppermute | solution.py:494
  67.0 6.5 %collective-permute-start.3 = (bf16[144,128]{1,0:T(8,128)(2,1)S(1)}, bf16[144,128]{1,0:T(8,128)(2,1)S(1)}, u32[]{:S(2)}, u32[]{:S(2)}) collective-permute-start(bf16[144,128]{1,0:T(8,128)(2,1)S(1)} %add_convert_fusion), channel_id=1, source_target_pairs={{0,224},{32,64},{64,32},{96,128},{128,96},{160,192},{192,160},{224... | collective-permute-start | bytes 110600 | tf_op jit(solution)/shard_map/ppermute | solution.py:494
  69.0 15.2 %collective-permute-start.5 = (bf16[144,128]{1,0:T(8,128)(2,1)S(1)}, bf16[144,128]{1,0:T(8,128)(2,1)S(1)}, u32[]{:S(2)}, u32[]{:S(2)}) collective-permute-start(bf16[144,128]{1,0:T(8,128)(2,1)S(1)} %add_convert_fusion), channel_id=1, source_target_pairs={{0,192},{32,96},{64,0},{96,160},{128,64},{160,224},{192,128},{224,... | collective-permute-start | bytes 110600 | tf_op jit(solution)/shard_map/ppermute | solution.py:494
  73.5 10.8 %collective-permute-start.4 = (bf16[144,128]{1,0:T(8,128)(2,1)S(1)}, bf16[144,128]{1,0:T(8,128)(2,1)S(1)}, u32[]{:S(2)}, u32[]{:S(2)}) collective-permute-start(bf16[144,128]{1,0:T(8,128)(2,1)S(1)} %collective-permute-done.3), channel_id=1, source_target_pairs={{0,64},{32,224},{64,128},{96,32},{128,192},{160,96},{192,0},{224,1... | collective-permute-start | bytes 110600 | tf_op jit(solution)/shard_map/ppermute | solution.py:494
  80.7 13.5 %all-to-all-start.3 = ((bf16[16,120,128]{2,1,0:T(8,128)(2,1)}), bf16[16,120,128]{2,1,0:T(8,128)(2,1)S(1)}, u32[]{:S(2)}, u32[]{:S(2)}) async-start(bf16[16,120,128]{2,1,0:T(8,128)(2,1)} %shard_map.156), calls=%async_computation.3 | async-start | bytes 983040 | tf_op jit(solution)/shard_map/all_to_all | solution.py:511
  84.3 1.4 %collective-permute-start.6 = (f32[144,128]{1,0:T(8,128)S(1)}, f32[144,128]{1,0:T(8,128)S(1)}, u32[]{:S(2)}, u32[]{:S(2)}) collective-permute-start(f32[144,128]{1,0:T(8,128)S(1)} %add_add_fusion), channel_id=1, source_target_pairs={{0,16},{16,0},{1,17},{17,1},{2,18},{18,2},{3,19},{19,3},{4,20},{20... | collective-permute-start | bytes 221192 | tf_op jit(solution)/shard_map/ppermute | solution.py:411

commit v9 on v8

--- a/solution.py
+++ b/solution.py
@@ -110,17 +110,8 @@
 
 
 def pack_body(f_hbm, g_hbm, o_ref, f_ref, g_ref, flat_ref, sems):
-    copies = fetch((f_hbm, g_hbm), (f_ref, g_ref), sems)
+    copies = fetch((g_hbm, f_hbm), (g_ref, f_ref), sems)
     copies[0].wait()
-    for j in range(6):
-        count = min(128, 8 * WPART - 128 * j)
-        order = one_hot((128, count), row_of_latitude)
-        block = dot(order, f_ref[128 * j : 128 * j + count, :]).astype(BF16)
-        for r in range(8):
-            for h in range(2):
-                piece = block[16 * r : 16 * (r + 1), 128 * h : 128 * (h + 1)]
-                o_ref[2 * r + h, 16 * j : 16 * (j + 1), :] = piece
-    copies[1].wait()
     for v in range(VPART):
         flat_ref[4 * v : 4 * (v + 1), :] = g_ref[v].astype(F32)
     flat_ref[4 * VPART : 192, :] = jnp.zeros((192 - 4 * VPART, C), F32)
@@ -134,6 +125,15 @@
             odd = jnp.where(keep, swap64(top), bottom)
             o_ref[4 * o + 2 * i, WROWS:CHUNK_IN, :] = even.astype(BF16)
             o_ref[4 * o + 2 * i + 1, WROWS:CHUNK_IN, :] = odd.astype(BF16)
+    copies[1].wait()
+    for j in range(6):
+        count = min(128, 8 * WPART - 128 * j)
+        order = one_hot((128, count), row_of_latitude)
+        block = dot(order, f_ref[128 * j : 128 * j + count, :]).astype(BF16)
+        for r in range(8):
+            for h in range(2):
+                piece = block[16 * r : 16 * (r + 1), 128 * h : 128 * (h + 1)]
+                o_ref[2 * r + h, 16 * j : 16 * (j + 1), :] = piece
 
 
 def flip(source, target, rows, columns):
@@ -351,7 +351,7 @@
 
 
 def fields_body(r_ref, w_ref, v_hbm, o_ref, v_ref, sems):
-    copies = fetch((v_hbm.at[0], v_hbm.at[1]), (v_ref.at[0], v_ref.at[1]), sems)
+    (copy,) = fetch((v_hbm,), (v_ref,), sems)
     fields, outs = [], []
     for e in range(BANDS):
         start = CHUNK_MID * e
@@ -361,8 +361,8 @@
         lanes = slice(HALF * side, HALF * (side + 1))
         field = fields[0] + fields[1] if side == 0 else fields[0] - fields[1]
         o_ref[lanes, 0:WROWS, :] = field.astype(BF16).reshape(HALF, WROWS, 128)
+    copy.wait()
     for e in range(BANDS):
-        copies[e].wait()
         start = CHUNK_MID * e
         c = r_ref[:, start : start + M16, :].reshape(LANES * M16, 128).astype(F32)
         turned = swap64(c)
@@ -407,13 +407,19 @@
         c_ref[v] = rows[4 * v : 4 * (v + 1), :].astype(BF16)
 
 
+def place_body(band_ref, half_ref, far_ref, o_ref):
+    low = band_ref[0, 0] == 0
+    half, far = half_ref[...], far_ref[...]
+    o_ref[:, 0:128] = jnp.where(low, half, far)
+    o_ref[:, 128:256] = jnp.where(low, far, half)
+
+
 def swap_bands(value):
     return lax.ppermute(value, "polar", [(0, 1), (1, 0)])
 
 
 def local(fields, basis_spectra, support, weights, out_grad):
     band = lax.axis_index("polar").astype(jnp.int32)
-    low = band == 0
     spot = jnp.stack([band, lax.axis_index("azimuth").astype(jnp.int32)]).reshape(1, 2)
     wide, narrow = factor_tables()
     dma = pltpu.SemaphoreType.DMA
@@ -497,8 +503,8 @@
     got = send(half, 1, -1)
     pair = (half.astype(F32) + got.astype(F32)).astype(BF16)
     beside = send(pair, -1, 1)
-    behind = send(pair, -2, 2)
     across = send(beside, 2, -2)
+    behind = send(beside, 1, -1)
     half = (pair.astype(F32) + across.astype(F32)) + (beside.astype(F32) + behind.astype(F32))
     far = swap_bands(half)
     (sent,) = call(
@@ -506,13 +512,13 @@
         [VMEM, VMEM, HBM],
         [((LANES, CHUNK_IN, 128), BF16)],
         flops=300 << 20,
-        scratch=[pltpu.VMEM((2, 384, 512), BF16), dma((2,))],
+        scratch=[pltpu.VMEM((2, 384, 512), BF16), dma((1,))],
     )(landed, tall, in_hbm(inv))
     landed = lax.all_to_all(sent, "azimuth", split_axis=0, concat_axis=0, tiled=True)
     field_grad, conv_out = call(
         unpack_body, [VMEM], [((8 * WPART, C), BF16), ((VPART, 4, C), BF16)], scratch=[pltpu.VMEM((192, C), F32)]
     )(landed)
-    weight_grad = jnp.concatenate([jnp.where(low, half, far), jnp.where(low, far, half)], axis=1)
+    (weight_grad,) = call(place_body, [SMEM, VMEM, VMEM], [((K * 16, C), F32)])(spot, half, far)
     field_grad = jnp.swapaxes(field_grad.reshape(WPART, 8, C), 0, 1)
     return (jnp.swapaxes(conv_out, 0, 1)[None], field_grad[None], weight_grad.reshape(K, 16, C))
 

time: 95.9 us -> 90.7 us (0.946)
  the two profiles are of different devices: /device:TPU:32 before, /device:TPU:2 now
where the time goes in v9:
time: 90.7 us; the launch traced here: 89.3 us
  starting transfers between devices  27.1 us (30%)
  Pallas kernels  22.1 us (24%)
  waiting for transfers between devices  19.6 us (22%)
  blocking collectives  19.4 us (21%)
    all_to_all x1, blocking collectives, local(): lax.all_to_all(sent, 'azimuth', split_axis=0, concat_axis=0, tiled=True)  19.4 us
    all_to_all x2, starting transfers between devices, local(): lax.all_to_all(sent, 'azimuth', split_axis=0, concat_axis=0, tiled=True)  12.3 us
    ppermute x4, starting transfers between devices, send(): return lax.ppermute(value, 'ens', pairs)  9.51 us
    all_to_all x1, waiting for transfers between devices, local(): lax.all_to_all(sent, JOINT, split_axis=0, concat_axis=0, tiled=True)  6.8 us
    ppermute x4, waiting for transfers between devices, send(): return lax.ppermute(value, 'ens', pairs)  6.49 us
    all_to_all x2, waiting for transfers between devices, local(): lax.all_to_all(sent, 'azimuth', split_axis=0, concat_axis=0, tiled=True)  5.08 us
    all_to_all x1, starting transfers between devices, local(): lax.all_to_all(sent, JOINT, split_axis=0, concat_axis=0, tiled=True)  4.99 us
    pallas_call x1, Pallas kernels, local(): call(middle_body, [SMEM, VMEM, VMEM, VMEM], [(chunk, BF16), (chunk, BF16)...  4.09 us
  transfers between devices with their start and end apart: 10, of which 6 were waited for; matrix products, arithmetic and copies ran while one was open for 0% of the time, Pallas kernels for 14%

profile of v9, /device:TPU:2, one launch (start us, length us, event | category | flops | bytes accessed | tf_op | source)
XLA Modules:
  0.0 89.3 jit_solution(15856386569527239519)
XLA Ops:
  0.6 2.3 %shard_map.148 = bf16[16,120,128]{2,1,0:T(8,128)(2,1)} custom-call(bf16[720,256]{1,0:T(8,128)(2,1)} %bitcast.26, bf16[45,4,256]{2,1,0:T(4,128)(2,1)} %bitcast.29), custom_call_target="tpu_custom_call" | custom-call | bytes 1048576 | tf_op jit(solution)/shard_map/pallas_call | solution.py:426
  2.9 7.5 %all-to-all-start = ((bf16[16,120,128]{2,1,0:T(8,128)(2,1)}), bf16[16,120,128]{2,1,0:T(8,128)(2,1)S(1)}, u32[]{:S(2)}, u32[]{:S(2)}) async-start(bf16[16,120,128]{2,1,0:T(8,128)(2,1)} %shard_map.148), calls=%async_computation | async-start | bytes 983040 | tf_op jit(solution)/shard_map/all_to_all | solution.py:439
  10.6 1.9 %shard_map.149 = (bf16[180,128]{1,0:T(8,128)(2,1)S(1)}, bf16[180,128]{1,0:T(8,128)(2,1)S(1)}) custom-call(s32[1,2]{1,0:T(1,128)S(1)} %add_bitcast_fusion.spot_ref.band_ref, s32[4,2]{1,0:T(4,128)S(1)} %copy.16.support_ref, bf16[45,4,720]{2,1,0:T(4,128)(2,1)} %bitcast.27), custom_call_target="tpu_custom_call" | custom-call | bytes 1048576 | tf_op jit(solution)/shard_map/pallas_call | solution.py:442
  12.5 2.6 %shard_map.150 = (bf16[2,384,768]{2,1,0:T(8,128)(2,1)S(1)}, bf16[2,512,384]{2,1,0:T(8,128)(2,1)S(1)}) custom-call(f32[2,8,384]{2,1,0:T(8,128)} %constant.28.clone.refs_0_, f32[2,8,384]{2,1,0:T(8,128)} %constant.29.clone.refs_1_, f32[2,96,384]{2,1,0:T(8,128)} %constant.30.clone.refs_2_, f32[2,96,384]{2,1,0:T(8,128)} %constant.31.clone.refs_3_, ...), custom_call_target="tpu_custom_call" | custom-call | bytes 5242880 | tf_op jit(solution)/shard_map/pallas_call | solution.py:452
  15.1 5.1 %all-to-all-done.r_ref = bf16[16,120,128]{2,1,0:T(8,128)(2,1)S(1)} async-done(((bf16[16,120,128]{2,1,0:T(8,128)(2,1)}), bf16[16,120,128]{2,1,0:T(8,128)(2,1)S(1)}, u32[]{:S(2)}, u32[]{:S(2)}) %all-to-all-start) | async-done | bytes 491552 | tf_op jit(solution)/shard_map/all_to_all | solution.py:439
  20.2 1.5 %shard_map.151 = bf16[32,40,128]{2,1,0:T(8,128)(2,1)} custom-call(bf16[16,120,128]{2,1,0:T(8,128)(2,1)S(1)} %all-to-all-done.r_ref, bf16[2,384,768]{2,1,0:T(8,128)(2,1)S(1)} %get-tuple-element.56.wt_ref, bf16[2,512,384]{2,1,0:T(8,128)(2,1)S(1)} %get-tuple-element.57.vt_ref), custom_call_target="tpu_custom_call" | custom-call | flops 314572800 | bytes 1048576 | tf_op jit(solution)/shard_map/pallas_call | solution.py:461
  21.7 5.0 %all-to-all-start.1 = ((bf16[32,40,128]{2,1,0:T(8,128)(2,1)}), bf16[32,40,128]{2,1,0:T(8,128)(2,1)S(1)}, u32[]{:S(2)}, u32[]{:S(2)}) async-start(bf16[32,40,128]{2,1,0:T(8,128)(2,1)} %shard_map.151), calls=%async_computation.1 | async-start | bytes 655360 | tf_op jit(solution)/shard_map/all_to_all | solution.py:462
  26.7 1.8 %shard_map.152 = (f32[144,384]{1,0:T(8,128)S(1)}, bf16[9,256,256]{2,1,0:T(8,128)(2,1)S(1)}) custom-call(s32[1,2]{1,0:T(1,128)S(1)} %add_bitcast_fusion.spot_ref.band_ref, bf16[180,128]{1,0:T(8,128)(2,1)S(1)} %get-tuple-element.60.mine_ref, bf16[180,128]{1,0:T(8,128)(2,1)S(1)} %collective-permute-done.got_ref, bf16[9,256,256]{2,1,0:T(8,128)(2,1)} %w_hbm.1), custom_call_target="tpu_custom_call" | custom-call | bytes 1048576 | tf_op jit(solution)/shard_map/pallas_call | solution.py:464
  28.5 6.8 %all-to-all-done.1 = bf16[32,40,128]{2,1,0:T(8,128)(2,1)S(1)} async-done(((bf16[32,40,128]{2,1,0:T(8,128)(2,1)}), bf16[32,40,128]{2,1,0:T(8,128)(2,1)S(1)}, u32[]{:S(2)}, u32[]{:S(2)}) %all-to-all-start.1) | async-done | bytes 327712 | tf_op jit(solution)/shard_map/all_to_all | solution.py:462
  35.3 4.1 %shard_map.153 = (bf16[16,184,128]{2,1,0:T(8,128)(2,1)S(1)}, bf16[16,184,128]{2,1,0:T(8,128)(2,1)S(1)}) custom-call(s32[1,2]{1,0:T(1,128)S(1)} %add_bitcast_fusion.spot_ref.band_ref, bf16[16,2,40,128]{3,2,1,0:T(8,128)(2,1)S(1)} %bitcast.25, f32[144,384]{1,0:T(8,128)S(1)} %get-tuple-element.62.p_ref, bf16[9,256,256]{2,1,0:T(8,128)(2,1)S(1)} %get-tuple-element.63.w_ref), custom_call_target="tpu_custom_call" | custom-call | flops 2147483648 | bytes 3145728 | tf_op jit(solution)/shard_map/pallas_call | solution.py:469
  39.5 2.2 %shard_map.154 = (bf16[2,768,384]{2,1,0:T(8,128)(2,1)S(1)}, bf16[2,384,512]{2,1,0:T(8,128)(2,1)}) custom-call(f32[2,8,384]{2,1,0:T(8,128)} %constant.28.clone.refs_0_, f32[2,8,384]{2,1,0:T(8,128)} %constant.29.clone.refs_1_, f32[2,96,384]{2,1,0:T(8,128)} %constant.30.clone.refs_2_, f32[2,96,384]{2,1,0:T(8,128)} %constant.31.clone.refs_3_, ...), custom_call_target="tpu_custom_call" | custom-call | bytes 5242880 | tf_op jit(solution)/shard_map/pallas_call | solution.py:483
  41.7 0.8 shard_map.155
  42.5 19.4 %all_to_all.20.r_ref = bf16[16,224,128]{2,1,0:T(8,128)(2,1)S(1)} all-to-all(bf16[16,224,128]{2,1,0:T(8,128)(2,1)S(1)} %shard_map.155), channel_id=1, replica_groups=mesh['ens'=8,'polar'=2,'azimuth'=16] {'azimuth'}, dimensions={0} | all-to-all | bytes 1835008 | tf_op jit(solution)/shard_map/all_to_all | solution.py:493
  62.0 2.0 %collective-permute-start.2 = (bf16[144,128]{1,0:T(8,128)(2,1)S(1)}, bf16[144,128]{1,0:T(8,128)(2,1)S(1)}, u32[]{:S(2)}, u32[]{:S(2)}) collective-permute-start(bf16[144,128]{1,0:T(8,128)(2,1)S(1)} %slice_reduce_fusion), channel_id=1, source_target_pairs={{0,32},{32,0},{64,96},{96,64},{128,160},{160,128},{192,224},{224,1... | collective-permute-start | bytes 110600 | tf_op jit(solution)/shard_map/ppermute | solution.py:500
  64.0 2.7 %shard_map.156 = bf16[16,120,128]{2,1,0:T(8,128)(2,1)} custom-call(bf16[16,224,128]{2,1,0:T(8,128)(2,1)S(1)} %all_to_all.20.r_ref, bf16[2,768,384]{2,1,0:T(8,128)(2,1)S(1)} %get-tuple-element.79.w_ref, bf16[2,384,512]{2,1,0:T(8,128)(2,1)} %get-tuple-element.80.v_hbm), custom_call_target="tpu_custom_call" | custom-call | flops 314572800 | bytes 1048576 | tf_op jit(solution)/shard_map/pallas_call | solution.py:510
  66.7 4.8 %all-to-all-start.3 = ((bf16[16,120,128]{2,1,0:T(8,128)(2,1)}), bf16[16,120,128]{2,1,0:T(8,128)(2,1)S(1)}, u32[]{:S(2)}, u32[]{:S(2)}) async-start(bf16[16,120,128]{2,1,0:T(8,128)(2,1)} %shard_map.156), calls=%async_computation.3 | async-start | bytes 983040 | tf_op jit(solution)/shard_map/all_to_all | solution.py:517
  71.6 5.0 %collective-permute-start.3 = (bf16[144,128]{1,0:T(8,128)(2,1)S(1)}, bf16[144,128]{1,0:T(8,128)(2,1)S(1)}, u32[]{:S(2)}, u32[]{:S(2)}) collective-permute-start(bf16[144,128]{1,0:T(8,128)(2,1)S(1)} %add_convert_fusion), channel_id=1, source_target_pairs={{0,224},{32,64},{64,32},{96,128},{128,96},{160,192},{192,160},{224... | collective-permute-start | bytes 110600 | tf_op jit(solution)/shard_map/ppermute | solution.py:500
  76.6 1.9 %collective-permute-done.3 = bf16[144,128]{1,0:T(8,128)(2,1)S(1)} collective-permute-done((bf16[144,128]{1,0:T(8,128)(2,1)S(1)}, bf16[144,128]{1,0:T(8,128)(2,1)S(1)}, u32[]{:S(2)}, u32[]{:S(2)}) %collective-permute-start.3) | collective-permute-done | bytes 36896 | tf_op jit(solution)/shard_map/ppermute | solution.py:500
  78.6 2.5 %collective-permute-start.4 = (bf16[144,128]{1,0:T(8,128)(2,1)S(1)}, bf16[144,128]{1,0:T(8,128)(2,1)S(1)}, u32[]{:S(2)}, u32[]{:S(2)}) collective-permute-start(bf16[144,128]{1,0:T(8,128)(2,1)S(1)} %collective-permute-done.3), channel_id=1, source_target_pairs={{0,64},{32,224},{64,128},{96,32},{128,192},{160,96},{192,0},{224,1... | collective-permute-start | bytes 110600 | tf_op jit(solution)/shard_map/ppermute | solution.py:500
  81.0 1.5 %collective-permute-done.5 = bf16[144,128]{1,0:T(8,128)(2,1)S(1)} collective-permute-done((bf16[144,128]{1,0:T(8,128)(2,1)S(1)}, bf16[144,128]{1,0:T(8,128)(2,1)S(1)}, u32[]{:S(2)}, u32[]{:S(2)}) %collective-permute-start.5) | collective-permute-done | bytes 36896 | tf_op jit(solution)/shard_map/ppermute | solution.py:500
  82.5 3.1 %collective-permute-done.4 = bf16[144,128]{1,0:T(8,128)(2,1)S(1)} collective-permute-done((bf16[144,128]{1,0:T(8,128)(2,1)S(1)}, bf16[144,128]{1,0:T(8,128)(2,1)S(1)}, u32[]{:S(2)}, u32[]{:S(2)}) %collective-permute-start.4) | collective-permute-done | bytes 36896 | tf_op jit(solution)/shard_map/ppermute | solution.py:500
  85.7 1.3 %collective-permute-done.6.far_ref = f32[144,128]{1,0:T(8,128)S(1)} collective-permute-done((f32[144,128]{1,0:T(8,128)S(1)}, f32[144,128]{1,0:T(8,128)S(1)}, u32[]{:S(2)}, u32[]{:S(2)}) %collective-permute-start.6) | collective-permute-done | bytes 73760 | tf_op jit(solution)/shard_map/ppermute | solution.py:418
  87.0 1.2 %shard_map.158 = f32[144,256]{1,0:T(8,128)} custom-call(s32[1,2]{1,0:T(1,128)S(1)} %add_bitcast_fusion.spot_ref.band_ref, f32[144,128]{1,0:T(8,128)S(1)} %add_add_fusion.half_ref, f32[144,128]{1,0:T(8,128)S(1)} %collective-permute-done.6.far_ref), custom_call_target="tpu_custom_call" | custom-call | bytes 1048576 | tf_op jit(solution)/shard_map/pallas_call | solution.py:521
  88.2 1.1 %shard_map.157 = (bf16[720,256]{1,0:T(8,128)(2,1)}, bf16[45,4,256]{2,1,0:T(4,128)(2,1)}) custom-call(bf16[16,120,128]{2,1,0:T(8,128)(2,1)S(1)} %all-to-all-done.3.r_ref), custom_call_target="tpu_custom_call" | custom-call | bytes 1048576 | tf_op jit(solution)/shard_map/pallas_call | solution.py:518
  (15 shorter events, 0.6 us)
Async XLA Ops:
  0.6 9.8 %copy-start = (s32[4,2]{0,1:T(2,128)S(1)}, s32[4,2]{0,1:T(2,128)}, u32[]{:S(2)}) copy-start(s32[4,2]{0,1:T(2,128)} %param.15) | copy-start | bytes 100
  2.9 17.3 %all-to-all-start = ((bf16[16,120,128]{2,1,0:T(8,128)(2,1)}), bf16[16,120,128]{2,1,0:T(8,128)(2,1)S(1)}, u32[]{:S(2)}, u32[]{:S(2)}) async-start(bf16[16,120,128]{2,1,0:T(8,128)(2,1)} %shard_map.148), calls=%async_computation | async-start | bytes 983040 | tf_op jit(solution)/shard_map/all_to_all | solution.py:439
  12.4 2.7 %collective-permute-start = (bf16[180,128]{1,0:T(8,128)(2,1)S(1)}, bf16[180,128]{1,0:T(8,128)(2,1)S(1)}, u32[]{:S(2)}, u32[]{:S(2)}) collective-permute-start(bf16[180,128]{1,0:T(8,128)(2,1)S(1)} %get-tuple-element.54), channel_id=1, source_target_pairs={{0,16},{16,0},{1,17},{17,1},{2,18},{18,2},{3,19},{19,3},{4,20},{20... | collective-permute-start | bytes 138248 | tf_op jit(solution)/shard_map/ppermute | solution.py:418
  21.7 13.6 %all-to-all-start.1 = ((bf16[32,40,128]{2,1,0:T(8,128)(2,1)}), bf16[32,40,128]{2,1,0:T(8,128)(2,1)S(1)}, u32[]{:S(2)}, u32[]{:S(2)}) async-start(bf16[32,40,128]{2,1,0:T(8,128)(2,1)} %shard_map.151), calls=%async_computation.1 | async-start | bytes 655360 | tf_op jit(solution)/shard_map/all_to_all | solution.py:462
  39.4 2.3 %collective-permute-start.1 = (bf16[16,184,128]{2,1,0:T(8,128)(2,1)S(1)}, bf16[16,184,128]{2,1,0:T(8,128)(2,1)S(1)}, u32[]{:S(2)}, u32[]{:S(2)}) collective-permute-start(bf16[16,184,128]{2,1,0:T(8,128)(2,1)S(1)} %get-tuple-element.67), channel_id=1, source_target_pairs={{0,16},{16,0},{1,17},{17,1},{2,18},{18,2},{3,19},{19,3},{4,20},{20... | collective-permute-start | bytes 2261000 | tf_op jit(solution)/shard_map/ppermute | solution.py:418
  62.0 9.6 %collective-permute-start.2 = (bf16[144,128]{1,0:T(8,128)(2,1)S(1)}, bf16[144,128]{1,0:T(8,128)(2,1)S(1)}, u32[]{:S(2)}, u32[]{:S(2)}) collective-permute-start(bf16[144,128]{1,0:T(8,128)(2,1)S(1)} %slice_reduce_fusion), channel_id=1, source_target_pairs={{0,32},{32,0},{64,96},{96,64},{128,160},{160,128},{192,224},{224,1... | collective-permute-start | bytes 110600 | tf_op jit(solution)/shard_map/ppermute | solution.py:500
  66.7 21.4 %all-to-all-start.3 = ((bf16[16,120,128]{2,1,0:T(8,128)(2,1)}), bf16[16,120,128]{2,1,0:T(8,128)(2,1)S(1)}, u32[]{:S(2)}, u32[]{:S(2)}) async-start(bf16[16,120,128]{2,1,0:T(8,128)(2,1)} %shard_map.156), calls=%async_computation.3 | async-start | bytes 983040 | tf_op jit(solution)/shard_map/all_to_all | solution.py:517
  71.6 7.0 %collective-permute-start.3 = (bf16[144,128]{1,0:T(8,128)(2,1)S(1)}, bf16[144,128]{1,0:T(8,128)(2,1)S(1)}, u32[]{:S(2)}, u32[]{:S(2)}) collective-permute-start(bf16[144,128]{1,0:T(8,128)(2,1)S(1)} %add_convert_fusion), channel_id=1, source_target_pairs={{0,224},{32,64},{64,32},{96,128},{128,96},{160,192},{192,160},{224... | collective-permute-start | bytes 110600 | tf_op jit(solution)/shard_map/ppermute | solution.py:500
  78.6 4.0 %collective-permute-start.5 = (bf16[144,128]{1,0:T(8,128)(2,1)S(1)}, bf16[144,128]{1,0:T(8,128)(2,1)S(1)}, u32[]{:S(2)}, u32[]{:S(2)}) collective-permute-start(bf16[144,128]{1,0:T(8,128)(2,1)S(1)} %collective-permute-done.3), channel_id=1, source_target_pairs={{0,32},{32,0},{64,96},{96,64},{128,160},{160,128},{192,224},{224,1... | collective-permute-start | bytes 110600 | tf_op jit(solution)/shard_map/ppermute | solution.py:500
  78.6 7.0 %collective-permute-start.4 = (bf16[144,128]{1,0:T(8,128)(2,1)S(1)}, bf16[144,128]{1,0:T(8,128)(2,1)S(1)}, u32[]{:S(2)}, u32[]{:S(2)}) collective-permute-start(bf16[144,128]{1,0:T(8,128)(2,1)S(1)} %collective-permute-done.3), channel_id=1, source_target_pairs={{0,64},{32,224},{64,128},{96,32},{128,192},{160,96},{192,0},{224,1... | collective-permute-start | bytes 110600 | tf_op jit(solution)/shard_map/ppermute | solution.py:500
  85.6 1.4 %collective-permute-start.6 = (f32[144,128]{1,0:T(8,128)S(1)}, f32[144,128]{1,0:T(8,128)S(1)}, u32[]{:S(2)}, u32[]{:S(2)}) collective-permute-start(f32[144,128]{1,0:T(8,128)S(1)} %add_add_fusion.half_ref), channel_id=1, source_target_pairs={{0,16},{16,0},{1,17},{17,1},{2,18},{18,2},{3,19},{19,3},{4,20},{20... | collective-permute-start | bytes 221192 | tf_op jit(solution)/shard_map/ppermute | solution.py:418

commit v10 on v9

--- a/solution.py
+++ b/solution.py
@@ -280,7 +280,11 @@
             gs_ref[32 * o : 32 * o + 16, cols] = jnp.where(keep, first, swap64(second)).astype(BF16)
             gs_ref[32 * o + 16 : 32 * o + 32, cols] = jnp.where(keep, swap64(first), second).astype(BF16)
     used = M12 * 16
-    gs = dot(one_hot((used, 256), row_of_share), gs_ref[...]).astype(BF16)
+    low = band_ref[0, 0] == 0
+    ordered = dot(one_hot((used, 256), row_of_share), gs_ref[...])
+    gs = ordered.astype(BF16)
+    left, right = ordered[:, :128], ordered[:, 128:]
+    turned = jnp.concatenate([jnp.where(low, left, right), jnp.where(low, right, left)], axis=1).astype(BF16)
     width = HIN * 2 * M12
     x = jnp.concatenate(
         [r_ref[:, h, M16:CHUNK_MID, :].reshape(width, 128) for h in range(2)], axis=1
@@ -291,18 +295,16 @@
         == lax.broadcasted_iota(jnp.int32, (width, used), 1) // 16
     )
     spread = one_hot((16, used), lambda column: column % 16)
-    low = band_ref[0, 0] == 0
-
     for k in range(K):
         placed = p_ref[16 * k : 16 * (k + 1), :]
         blocks = [jnp.where(lane_mode == m, placed, 0.0).astype(BF16) for m in range(M12)]
         mixed = dot(jnp.concatenate(blocks, axis=0), x).astype(BF16)
         out_now = dot(mixed, w_ref[k])
-        grad = lax.dot_general(mixed, gs, (((0,), (0,)), ((), ())), preferred_element_type=F32)
+        grad = lax.dot_general(mixed, turned, (((0,), (0,)), ((), ())), preferred_element_type=F32)
         where_to = (slice(None), slice(CHUNK_MID + 16 * k, CHUNK_MID + 16 * (k + 1)), slice(None))
         shape = (LANES, 16, 128)
-        mine_ref[where_to] = jnp.where(low, grad[:, :128], grad[:, 128:]).astype(BF16).reshape(shape)
-        other_ref[where_to] = jnp.where(low, grad[:, 128:], grad[:, :128]).astype(BF16).reshape(shape)
+        mine_ref[where_to] = grad[:, :128].astype(BF16).reshape(shape)
+        other_ref[where_to] = grad[:, 128:].astype(BF16).reshape(shape)
         back = lax.dot_general(gs, w_ref[k], (((1,), (1,)), ((), ())), preferred_element_type=F32)
         grown = lax.dot_general(
             placed.astype(BF16), spread, (((0,), (0,)), ((), ())), preferred_element_type=F32
@@ -407,19 +409,13 @@
         c_ref[v] = rows[4 * v : 4 * (v + 1), :].astype(BF16)
 
 
-def place_body(band_ref, half_ref, far_ref, o_ref):
-    low = band_ref[0, 0] == 0
-    half, far = half_ref[...], far_ref[...]
-    o_ref[:, 0:128] = jnp.where(low, half, far)
-    o_ref[:, 128:256] = jnp.where(low, far, half)
-
-
 def swap_bands(value):
     return lax.ppermute(value, "polar", [(0, 1), (1, 0)])
 
 
 def local(fields, basis_spectra, support, weights, out_grad):
     band = lax.axis_index("polar").astype(jnp.int32)
+    low = band == 0
     spot = jnp.stack([band, lax.axis_index("azimuth").astype(jnp.int32)]).reshape(1, 2)
     wide, narrow = factor_tables()
     dma = pltpu.SemaphoreType.DMA
@@ -518,7 +514,7 @@
     field_grad, conv_out = call(
         unpack_body, [VMEM], [((8 * WPART, C), BF16), ((VPART, 4, C), BF16)], scratch=[pltpu.VMEM((192, C), F32)]
     )(landed)
-    (weight_grad,) = call(place_body, [SMEM, VMEM, VMEM], [((K * 16, C), F32)])(spot, half, far)
+    weight_grad = jnp.concatenate([jnp.where(low, half, far), jnp.where(low, far, half)], axis=1)
     field_grad = jnp.swapaxes(field_grad.reshape(WPART, 8, C), 0, 1)
     return (jnp.swapaxes(conv_out, 0, 1)[None], field_grad[None], weight_grad.reshape(K, 16, C))
 

time: 90.7 us -> 95.6 us (1.054)
  waiting for transfers between devices: 19.6 us -> 23.7 us
  Pallas kernels: 22.1 us -> 20.9 us
  starting transfers between devices: 27.1 us -> 28.1 us
    all_to_all x2, waiting for transfers between devices: 5.08 us -> 11.7 us  [local(): lax.all_to_all(sent, 'azimuth', split_axis=0, concat_axis=0, tiled=True)]
    ppermute x4, waiting for transfers between devices: 6.49 us -> 3.99 us  [send(): return lax.ppermute(value, 'ens', pairs)]
    pallas_call x1 -> x0, Pallas kernels: 1.22 us -> none  [local(): call(place_body, [SMEM, VMEM, VMEM], [((K * 16, C), F32)])(spot, half, far)]
    ppermute x4, starting transfers between devices: 9.51 us -> 10.5 us  [send(): return lax.ppermute(value, 'ens', pairs)]
  transfers between devices with their start and end apart: 10 -> 10, of which waited for: 6 -> 6; matrix products, arithmetic and copies ran while one was open for 0% -> 1% of each run, Pallas kernels for 14% -> 12%
where the time goes in v10:
time: 95.6 us; the launch traced here: 93.8 us
  starting transfers between devices  28.1 us (29%)
  waiting for transfers between devices  23.7 us (25%)
  Pallas kernels  20.9 us (22%)
  blocking collectives  19.4 us (20%)
    all_to_all x1, blocking collectives, local(): lax.all_to_all(sent, 'azimuth', split_axis=0, concat_axis=0, tiled=True)  19.4 us
    all_to_all x2, starting transfers between devices, local(): lax.all_to_all(sent, 'azimuth', split_axis=0, concat_axis=0, tiled=True)  12.3 us
    all_to_all x2, waiting for transfers between devices, local(): lax.all_to_all(sent, 'azimuth', split_axis=0, concat_axis=0, tiled=True)  11.7 us
    ppermute x4, starting transfers between devices, send(): return lax.ppermute(value, 'ens', pairs)  10.5 us
    all_to_all x1, waiting for transfers between devices, local(): lax.all_to_all(sent, JOINT, split_axis=0, concat_axis=0, tiled=True)  6.8 us
    all_to_all x1, starting transfers between devices, local(): lax.all_to_all(sent, JOINT, split_axis=0, concat_axis=0, tiled=True)  4.99 us
    pallas_call x1, Pallas kernels, local(): call(middle_body, [SMEM, VMEM, VMEM, VMEM], [(chunk, BF16), (chunk, BF16)...  4.08 us
    ppermute x4, waiting for transfers between devices, send(): return lax.ppermute(value, 'ens', pairs)  3.99 us
  transfers between devices with their start and end apart: 10, of which 6 were waited for; matrix products, arithmetic and copies ran while one was open for 1% of the time, Pallas kernels for 12%

profile of v10, /device:TPU:2, one launch (start us, length us, event | category | flops | bytes accessed | tf_op | source)
XLA Modules:
  0.0 93.8 jit_solution(11609692903487904514)
XLA Ops:
  0.6 2.3 %shard_map.148 = bf16[16,120,128]{2,1,0:T(8,128)(2,1)} custom-call(bf16[720,256]{1,0:T(8,128)(2,1)} %bitcast.26, bf16[45,4,256]{2,1,0:T(4,128)(2,1)} %bitcast.29), custom_call_target="tpu_custom_call" | custom-call | bytes 1048576 | tf_op jit(solution)/shard_map/pallas_call | solution.py:422
  2.9 7.5 %all-to-all-start = ((bf16[16,120,128]{2,1,0:T(8,128)(2,1)}), bf16[16,120,128]{2,1,0:T(8,128)(2,1)S(1)}, u32[]{:S(2)}, u32[]{:S(2)}) async-start(bf16[16,120,128]{2,1,0:T(8,128)(2,1)} %shard_map.148), calls=%async_computation | async-start | bytes 983040 | tf_op jit(solution)/shard_map/all_to_all | solution.py:435
  10.6 1.9 %shard_map.149 = (bf16[180,128]{1,0:T(8,128)(2,1)S(1)}, bf16[180,128]{1,0:T(8,128)(2,1)S(1)}) custom-call(s32[1,2]{1,0:T(1,128)S(1)} %add_bitcast_fusion.spot_ref.band_ref, s32[4,2]{1,0:T(4,128)S(1)} %copy.16.support_ref, bf16[45,4,720]{2,1,0:T(4,128)(2,1)} %bitcast.27), custom_call_target="tpu_custom_call" | custom-call | bytes 1048576 | tf_op jit(solution)/shard_map/pallas_call | solution.py:438
  12.5 2.6 %shard_map.150 = (bf16[2,384,768]{2,1,0:T(8,128)(2,1)S(1)}, bf16[2,512,384]{2,1,0:T(8,128)(2,1)S(1)}) custom-call(f32[2,8,384]{2,1,0:T(8,128)} %constant.30.clone.refs_0_, f32[2,8,384]{2,1,0:T(8,128)} %constant.31.clone.refs_1_, f32[2,96,384]{2,1,0:T(8,128)} %constant.32.clone.refs_2_, f32[2,96,384]{2,1,0:T(8,128)} %constant.33.clone.refs_3_, ...), custom_call_target="tpu_custom_call" | custom-call | bytes 5242880 | tf_op jit(solution)/shard_map/pallas_call | solution.py:448
  15.2 5.1 %all-to-all-done.r_ref = bf16[16,120,128]{2,1,0:T(8,128)(2,1)S(1)} async-done(((bf16[16,120,128]{2,1,0:T(8,128)(2,1)}), bf16[16,120,128]{2,1,0:T(8,128)(2,1)S(1)}, u32[]{:S(2)}, u32[]{:S(2)}) %all-to-all-start) | async-done | bytes 491552 | tf_op jit(solution)/shard_map/all_to_all | solution.py:435
  20.2 1.5 %shard_map.151 = bf16[32,40,128]{2,1,0:T(8,128)(2,1)} custom-call(bf16[16,120,128]{2,1,0:T(8,128)(2,1)S(1)} %all-to-all-done.r_ref, bf16[2,384,768]{2,1,0:T(8,128)(2,1)S(1)} %get-tuple-element.56.wt_ref, bf16[2,512,384]{2,1,0:T(8,128)(2,1)S(1)} %get-tuple-element.57.vt_ref), custom_call_target="tpu_custom_call" | custom-call | flops 314572800 | bytes 1048576 | tf_op jit(solution)/shard_map/pallas_call | solution.py:457
  21.7 5.0 %all-to-all-start.1 = ((bf16[32,40,128]{2,1,0:T(8,128)(2,1)}), bf16[32,40,128]{2,1,0:T(8,128)(2,1)S(1)}, u32[]{:S(2)}, u32[]{:S(2)}) async-start(bf16[32,40,128]{2,1,0:T(8,128)(2,1)} %shard_map.151), calls=%async_computation.1 | async-start | bytes 655360 | tf_op jit(solution)/shard_map/all_to_all | solution.py:458
  26.7 1.8 %shard_map.152 = (f32[144,384]{1,0:T(8,128)S(1)}, bf16[9,256,256]{2,1,0:T(8,128)(2,1)S(1)}) custom-call(s32[1,2]{1,0:T(1,128)S(1)} %add_bitcast_fusion.spot_ref.band_ref, bf16[180,128]{1,0:T(8,128)(2,1)S(1)} %get-tuple-element.60.mine_ref, bf16[180,128]{1,0:T(8,128)(2,1)S(1)} %collective-permute-done.got_ref, bf16[9,256,256]{2,1,0:T(8,128)(2,1)} %w_hbm.1), custom_call_target="tpu_custom_call" | custom-call | bytes 1048576 | tf_op jit(solution)/shard_map/pallas_call | solution.py:460
  28.5 6.8 %all-to-all-done.1 = bf16[32,40,128]{2,1,0:T(8,128)(2,1)S(1)} async-done(((bf16[32,40,128]{2,1,0:T(8,128)(2,1)}), bf16[32,40,128]{2,1,0:T(8,128)(2,1)S(1)}, u32[]{:S(2)}, u32[]{:S(2)}) %all-to-all-start.1) | async-done | bytes 327712 | tf_op jit(solution)/shard_map/all_to_all | solution.py:458
  35.3 4.1 %shard_map.153 = (bf16[16,184,128]{2,1,0:T(8,128)(2,1)S(1)}, bf16[16,184,128]{2,1,0:T(8,128)(2,1)S(1)}) custom-call(s32[1,2]{1,0:T(1,128)S(1)} %add_bitcast_fusion.spot_ref.band_ref, bf16[16,2,40,128]{3,2,1,0:T(8,128)(2,1)S(1)} %bitcast.25, f32[144,384]{1,0:T(8,128)S(1)} %get-tuple-element.62.p_ref, bf16[9,256,256]{2,1,0:T(8,128)(2,1)S(1)} %get-tuple-element.63.w_ref), custom_call_target="tpu_custom_call" | custom-call | flops 2147483648 | bytes 3145728 | tf_op jit(solution)/shard_map/pallas_call | solution.py:465
  39.5 2.2 %shard_map.154 = (bf16[2,768,384]{2,1,0:T(8,128)(2,1)S(1)}, bf16[2,384,512]{2,1,0:T(8,128)(2,1)}) custom-call(f32[2,8,384]{2,1,0:T(8,128)} %constant.30.clone.refs_0_, f32[2,8,384]{2,1,0:T(8,128)} %constant.31.clone.refs_1_, f32[2,96,384]{2,1,0:T(8,128)} %constant.32.clone.refs_2_, f32[2,96,384]{2,1,0:T(8,128)} %constant.33.clone.refs_3_, ...), custom_call_target="tpu_custom_call" | custom-call | bytes 5242880 | tf_op jit(solution)/shard_map/pallas_call | solution.py:479
  41.7 0.8 shard_map.155
  42.5 19.4 %all_to_all.20.r_ref = bf16[16,224,128]{2,1,0:T(8,128)(2,1)S(1)} all-to-all(bf16[16,224,128]{2,1,0:T(8,128)(2,1)S(1)} %shard_map.155), channel_id=1, replica_groups=mesh['ens'=8,'polar'=2,'azimuth'=16] {'azimuth'}, dimensions={0} | all-to-all | bytes 1835008 | tf_op jit(solution)/shard_map/all_to_all | solution.py:489
  62.0 2.0 %collective-permute-start.2 = (bf16[144,128]{1,0:T(8,128)(2,1)S(1)}, bf16[144,128]{1,0:T(8,128)(2,1)S(1)}, u32[]{:S(2)}, u32[]{:S(2)}) collective-permute-start(bf16[144,128]{1,0:T(8,128)(2,1)S(1)} %slice_reduce_fusion), channel_id=1, source_target_pairs={{0,32},{32,0},{64,96},{96,64},{128,160},{160,128},{192,224},{224,1... | collective-permute-start | bytes 110600 | tf_op jit(solution)/shard_map/ppermute | solution.py:496
  64.0 2.0 %collective-permute-done.2 = bf16[144,128]{1,0:T(8,128)(2,1)S(1)} collective-permute-done((bf16[144,128]{1,0:T(8,128)(2,1)S(1)}, bf16[144,128]{1,0:T(8,128)(2,1)S(1)}, u32[]{:S(2)}, u32[]{:S(2)}) %collective-permute-start.2) | collective-permute-done | bytes 36896 | tf_op jit(solution)/shard_map/ppermute | solution.py:496
  66.1 5.9 %collective-permute-start.3 = (bf16[144,128]{1,0:T(8,128)(2,1)S(1)}, bf16[144,128]{1,0:T(8,128)(2,1)S(1)}, u32[]{:S(2)}, u32[]{:S(2)}) collective-permute-start(bf16[144,128]{1,0:T(8,128)(2,1)S(1)} %add_convert_fusion), channel_id=1, source_target_pairs={{0,224},{32,64},{64,32},{96,128},{128,96},{160,192},{192,160},{224... | collective-permute-start | bytes 110600 | tf_op jit(solution)/shard_map/ppermute | solution.py:496
  72.0 1.9 %collective-permute-done.3 = bf16[144,128]{1,0:T(8,128)(2,1)S(1)} collective-permute-done((bf16[144,128]{1,0:T(8,128)(2,1)S(1)}, bf16[144,128]{1,0:T(8,128)(2,1)S(1)}, u32[]{:S(2)}, u32[]{:S(2)}) %collective-permute-start.3) | collective-permute-done | bytes 36896 | tf_op jit(solution)/shard_map/ppermute | solution.py:496
  73.9 2.6 %collective-permute-start.4 = (bf16[144,128]{1,0:T(8,128)(2,1)S(1)}, bf16[144,128]{1,0:T(8,128)(2,1)S(1)}, u32[]{:S(2)}, u32[]{:S(2)}) collective-permute-start(bf16[144,128]{1,0:T(8,128)(2,1)S(1)} %collective-permute-done.3), channel_id=1, source_target_pairs={{0,64},{32,224},{64,128},{96,32},{128,192},{160,96},{192,0},{224,1... | collective-permute-start | bytes 110600 | tf_op jit(solution)/shard_map/ppermute | solution.py:496
  76.5 2.7 %shard_map.156 = bf16[16,120,128]{2,1,0:T(8,128)(2,1)} custom-call(bf16[16,224,128]{2,1,0:T(8,128)(2,1)S(1)} %all_to_all.20.r_ref, bf16[2,768,384]{2,1,0:T(8,128)(2,1)S(1)} %get-tuple-element.79.w_ref, bf16[2,384,512]{2,1,0:T(8,128)(2,1)} %get-tuple-element.80.v_hbm), custom_call_target="tpu_custom_call" | custom-call | flops 314572800 | bytes 1048576 | tf_op jit(solution)/shard_map/pallas_call | solution.py:506
  79.2 4.8 %all-to-all-start.3 = ((bf16[16,120,128]{2,1,0:T(8,128)(2,1)}), bf16[16,120,128]{2,1,0:T(8,128)(2,1)S(1)}, u32[]{:S(2)}, u32[]{:S(2)}) async-start(bf16[16,120,128]{2,1,0:T(8,128)(2,1)} %shard_map.156), calls=%async_computation.3 | async-start | bytes 983040 | tf_op jit(solution)/shard_map/all_to_all | solution.py:513
  84.2 1.2 %collective-permute-done.6 = f32[144,128]{1,0:T(8,128)S(1)} collective-permute-done((f32[144,128]{1,0:T(8,128)S(1)}, f32[144,128]{1,0:T(8,128)S(1)}, u32[]{:S(2)}, u32[]{:S(2)}) %collective-permute-start.6) | collective-permute-done | bytes 73760 | tf_op jit(solution)/shard_map/ppermute | solution.py:413
  85.5 0.7 pad_maximum_fusion
  86.2 6.6 %all-to-all-done.3.r_ref = bf16[16,120,128]{2,1,0:T(8,128)(2,1)S(1)} async-done(((bf16[16,120,128]{2,1,0:T(8,128)(2,1)}), bf16[16,120,128]{2,1,0:T(8,128)(2,1)S(1)}, u32[]{:S(2)}, u32[]{:S(2)}) %all-to-all-start.3) | async-done | bytes 491552 | tf_op jit(solution)/shard_map/all_to_all | solution.py:513
  92.8 1.1 %shard_map.157 = (bf16[720,256]{1,0:T(8,128)(2,1)}, bf16[45,4,256]{2,1,0:T(4,128)(2,1)}) custom-call(bf16[16,120,128]{2,1,0:T(8,128)(2,1)S(1)} %all-to-all-done.3.r_ref), custom_call_target="tpu_custom_call" | custom-call | bytes 1048576 | tf_op jit(solution)/shard_map/pallas_call | solution.py:514
  (16 shorter events, 0.6 us)
Async XLA Ops:
  0.6 9.8 %copy-start = (s32[4,2]{0,1:T(2,128)S(1)}, s32[4,2]{0,1:T(2,128)}, u32[]{:S(2)}) copy-start(s32[4,2]{0,1:T(2,128)} %param.15) | copy-start | bytes 100
  2.9 17.3 %all-to-all-start = ((bf16[16,120,128]{2,1,0:T(8,128)(2,1)}), bf16[16,120,128]{2,1,0:T(8,128)(2,1)S(1)}, u32[]{:S(2)}, u32[]{:S(2)}) async-start(bf16[16,120,128]{2,1,0:T(8,128)(2,1)} %shard_map.148), calls=%async_computation | async-start | bytes 983040 | tf_op jit(solution)/shard_map/all_to_all | solution.py:435
  12.4 2.7 %collective-permute-start = (bf16[180,128]{1,0:T(8,128)(2,1)S(1)}, bf16[180,128]{1,0:T(8,128)(2,1)S(1)}, u32[]{:S(2)}, u32[]{:S(2)}) collective-permute-start(bf16[180,128]{1,0:T(8,128)(2,1)S(1)} %get-tuple-element.54), channel_id=1, source_target_pairs={{0,16},{16,0},{1,17},{17,1},{2,18},{18,2},{3,19},{19,3},{4,20},{20... | collective-permute-start | bytes 138248 | tf_op jit(solution)/shard_map/ppermute | solution.py:413
  21.7 13.6 %all-to-all-start.1 = ((bf16[32,40,128]{2,1,0:T(8,128)(2,1)}), bf16[32,40,128]{2,1,0:T(8,128)(2,1)S(1)}, u32[]{:S(2)}, u32[]{:S(2)}) async-start(bf16[32,40,128]{2,1,0:T(8,128)(2,1)} %shard_map.151), calls=%async_computation.1 | async-start | bytes 655360 | tf_op jit(solution)/shard_map/all_to_all | solution.py:458
  39.4 2.3 %collective-permute-start.1 = (bf16[16,184,128]{2,1,0:T(8,128)(2,1)S(1)}, bf16[16,184,128]{2,1,0:T(8,128)(2,1)S(1)}, u32[]{:S(2)}, u32[]{:S(2)}) collective-permute-start(bf16[16,184,128]{2,1,0:T(8,128)(2,1)S(1)} %get-tuple-element.67), channel_id=1, source_target_pairs={{0,16},{16,0},{1,17},{17,1},{2,18},{18,2},{3,19},{19,3},{4,20},{20... | collective-permute-start | bytes 2261000 | tf_op jit(solution)/shard_map/ppermute | solution.py:413
  62.0 4.0 %collective-permute-start.2 = (bf16[144,128]{1,0:T(8,128)(2,1)S(1)}, bf16[144,128]{1,0:T(8,128)(2,1)S(1)}, u32[]{:S(2)}, u32[]{:S(2)}) collective-permute-start(bf16[144,128]{1,0:T(8,128)(2,1)S(1)} %slice_reduce_fusion), channel_id=1, source_target_pairs={{0,32},{32,0},{64,96},{96,64},{128,160},{160,128},{192,224},{224,1... | collective-permute-start | bytes 110600 | tf_op jit(solution)/shard_map/ppermute | solution.py:496
  66.1 7.9 %collective-permute-start.3 = (bf16[144,128]{1,0:T(8,128)(2,1)S(1)}, bf16[144,128]{1,0:T(8,128)(2,1)S(1)}, u32[]{:S(2)}, u32[]{:S(2)}) collective-permute-start(bf16[144,128]{1,0:T(8,128)(2,1)S(1)} %add_convert_fusion), channel_id=1, source_target_pairs={{0,224},{32,64},{64,32},{96,128},{128,96},{160,192},{192,160},{224... | collective-permute-start | bytes 110600 | tf_op jit(solution)/shard_map/ppermute | solution.py:496
  73.9 10.1 %collective-permute-start.5 = (bf16[144,128]{1,0:T(8,128)(2,1)S(1)}, bf16[144,128]{1,0:T(8,128)(2,1)S(1)}, u32[]{:S(2)}, u32[]{:S(2)}) collective-permute-start(bf16[144,128]{1,0:T(8,128)(2,1)S(1)} %collective-permute-done.3), channel_id=1, source_target_pairs={{0,32},{32,0},{64,96},{96,64},{128,160},{160,128},{192,224},{224,1... | collective-permute-start | bytes 110600 | tf_op jit(solution)/shard_map/ppermute | solution.py:496
  73.9 10.1 %collective-permute-start.4 = (bf16[144,128]{1,0:T(8,128)(2,1)S(1)}, bf16[144,128]{1,0:T(8,128)(2,1)S(1)}, u32[]{:S(2)}, u32[]{:S(2)}) collective-permute-start(bf16[144,128]{1,0:T(8,128)(2,1)S(1)} %collective-permute-done.3), channel_id=1, source_target_pairs={{0,64},{32,224},{64,128},{96,32},{128,192},{160,96},{192,0},{224,1... | collective-permute-start | bytes 110600 | tf_op jit(solution)/shard_map/ppermute | solution.py:496
  79.2 13.5 %all-to-all-start.3 = ((bf16[16,120,128]{2,1,0:T(8,128)(2,1)}), bf16[16,120,128]{2,1,0:T(8,128)(2,1)S(1)}, u32[]{:S(2)}, u32[]{:S(2)}) async-start(bf16[16,120,128]{2,1,0:T(8,128)(2,1)} %shard_map.156), calls=%async_computation.3 | async-start | bytes 983040 | tf_op jit(solution)/shard_map/all_to_all | solution.py:513
  84.1 1.4 %collective-permute-start.6 = (f32[144,128]{1,0:T(8,128)S(1)}, f32[144,128]{1,0:T(8,128)S(1)}, u32[]{:S(2)}, u32[]{:S(2)}) collective-permute-start(f32[144,128]{1,0:T(8,128)S(1)} %add_add_fusion), channel_id=1, source_target_pairs={{0,16},{16,0},{1,17},{17,1},{2,18},{18,2},{3,19},{19,3},{4,20},{20... | collective-permute-start | bytes 221192 | tf_op jit(solution)/shard_map/ppermute | solution.py:413

commit v11 on v10

--- a/solution.py
+++ b/solution.py
@@ -270,7 +270,7 @@
     return 16 * (column % 16) + column // 16
 
 
-def middle_body(band_ref, r_ref, p_ref, w_ref, mine_ref, other_ref, gs_ref, out_ref, sg_ref):
+def middle_body(band_ref, r_ref, p_ref, w_ref, mine_ref, other_ref, gs_ref, sg_ref, mixed_ref, back_ref, at_ref):
     keep = low_half((M16, 128))
     for o in range(HOUT):
         for i in range(2):
@@ -290,36 +290,37 @@
         [r_ref[:, h, M16:CHUNK_MID, :].reshape(width, 128) for h in range(2)], axis=1
     )
     lane_mode = lax.broadcasted_iota(jnp.int32, (16, width), 1) % M12
-    diagonal = (
-        lax.broadcasted_iota(jnp.int32, (width, used), 0) % M12
-        == lax.broadcasted_iota(jnp.int32, (width, used), 1) // 16
-    )
-    spread = one_hot((16, used), lambda column: column % 16)
+    for k in range(0, K, 2):
+        pair = min(2, K - k)
+        row = lax.broadcasted_iota(jnp.int32, (16 * pair, used * pair), 0)
+        column = lax.broadcasted_iota(jnp.int32, (16 * pair, used * pair), 1)
+        spread = jnp.where(row == 16 * (column // used) + column % 16, 1.0, 0.0).astype(BF16)
+        row = lax.broadcasted_iota(jnp.int32, (width, used * pair), 0) % M12
+        column = (lax.broadcasted_iota(jnp.int32, (width, used * pair), 1) // 16) % M12
+        grown = lax.dot_general(
+            p_ref[16 * k : 16 * (k + pair), :].astype(BF16),
+            spread,
+            (((0,), (0,)), ((), ())),
+            preferred_element_type=F32,
+        )
+        at_ref[:, used * k : used * (k + pair)] = jnp.where(row == column, grown, 0.0).astype(BF16)
     for k in range(K):
         placed = p_ref[16 * k : 16 * (k + 1), :]
         blocks = [jnp.where(lane_mode == m, placed, 0.0).astype(BF16) for m in range(M12)]
         mixed = dot(jnp.concatenate(blocks, axis=0), x).astype(BF16)
-        out_now = dot(mixed, w_ref[k])
+        mixed_ref[:, C * k : C * (k + 1)] = mixed
         grad = lax.dot_general(mixed, turned, (((0,), (0,)), ((), ())), preferred_element_type=F32)
         where_to = (slice(None), slice(CHUNK_MID + 16 * k, CHUNK_MID + 16 * (k + 1)), slice(None))
         shape = (LANES, 16, 128)
         mine_ref[where_to] = grad[:, :128].astype(BF16).reshape(shape)
         other_ref[where_to] = grad[:, 128:].astype(BF16).reshape(shape)
         back = lax.dot_general(gs, w_ref[k], (((1,), (1,)), ((), ())), preferred_element_type=F32)
-        grown = lax.dot_general(
-            placed.astype(BF16), spread, (((0,), (0,)), ((), ())), preferred_element_type=F32
-        )
-        sg_now = dot(jnp.where(diagonal, grown, 0.0).astype(BF16), back.astype(BF16))
-        if k == 0:
-            out_ref[...] = out_now
-            sg_ref[...] = sg_now
-        else:
-            out_ref[...] += out_now
-            sg_ref[...] += sg_now
-
+        back_ref[used * k : used * (k + 1), :] = back.astype(BF16)
+    out = dot(mixed_ref[...], w_ref[...].reshape(K * C, C)).astype(BF16)
+    sg_ref[...] = dot(at_ref[...], back_ref[...])
     ordered = lax.dot_general(
         one_hot((used, 256), row_of_share),
-        out_ref[...].astype(BF16),
+        out,
         (((0,), (0,)), ((), ())),
         preferred_element_type=F32,
     )
@@ -470,8 +471,10 @@
         nbytes=3 << 20,
         scratch=[
             pltpu.VMEM((256, 256), BF16),
-            pltpu.VMEM((192, 256), F32),
             pltpu.VMEM((384, 256), F32),
+            pltpu.VMEM((192, K * C), BF16),
+            pltpu.VMEM((K * 192, 256), BF16),
+            pltpu.VMEM((384, K * 192), BF16),
         ],
     )(spot, landed.reshape(HIN, 2, CHUNK_MID, 128), placed, staged)
     factors, mine, other = lax.optimization_barrier((factors, mine, other))

time: 95.6 us -> 95.7 us (level)
  no operation moved by 1% of the time
where the time goes in v11:
time: 95.7 us; the launch traced here: 94 us
  starting transfers between devices  28.1 us (29%)
  waiting for transfers between devices  23.7 us (25%)
  Pallas kernels  21.1 us (22%)
  blocking collectives  19.4 us (20%)
    all_to_all x1, blocking collectives, local(): lax.all_to_all(sent, 'azimuth', split_axis=0, concat_axis=0, tiled=True)  19.4 us
    all_to_all x2, starting transfers between devices, local(): lax.all_to_all(sent, 'azimuth', split_axis=0, concat_axis=0, tiled=True)  12.3 us
    all_to_all x2, waiting for transfers between devices, local(): lax.all_to_all(sent, 'azimuth', split_axis=0, concat_axis=0, tiled=True)  11.7 us
    ppermute x4, starting transfers between devices, send(): return lax.ppermute(value, 'ens', pairs)  10.5 us
    all_to_all x1, waiting for transfers between devices, local(): lax.all_to_all(sent, JOINT, split_axis=0, concat_axis=0, tiled=True)  6.8 us
    all_to_all x1, starting transfers between devices, local(): lax.all_to_all(sent, JOINT, split_axis=0, concat_axis=0, tiled=True)  4.99 us
    pallas_call x1, Pallas kernels, local(): call(middle_body, [SMEM, VMEM, VMEM, VMEM], [(chunk, BF16), (chunk, BF16)...  4.26 us
    ppermute x4, waiting for transfers between devices, send(): return lax.ppermute(value, 'ens', pairs)  3.99 us
  transfers between devices with their start and end apart: 10, of which 6 were waited for; matrix products, arithmetic and copies ran while one was open for 1% of the time, Pallas kernels for 12%

profile of v11, /device:TPU:2, one launch (start us, length us, event | category | flops | bytes accessed | tf_op | source)
XLA Modules:
  0.0 94.0 jit_solution(4613068903924433453)
XLA Ops:
  0.6 2.3 %shard_map.148 = bf16[16,120,128]{2,1,0:T(8,128)(2,1)} custom-call(bf16[720,256]{1,0:T(8,128)(2,1)} %bitcast.26, bf16[45,4,256]{2,1,0:T(4,128)(2,1)} %bitcast.29), custom_call_target="tpu_custom_call" | custom-call | bytes 1048576 | tf_op jit(solution)/shard_map/pallas_call | solution.py:423
  2.9 7.5 %all-to-all-start = ((bf16[16,120,128]{2,1,0:T(8,128)(2,1)}), bf16[16,120,128]{2,1,0:T(8,128)(2,1)S(1)}, u32[]{:S(2)}, u32[]{:S(2)}) async-start(bf16[16,120,128]{2,1,0:T(8,128)(2,1)} %shard_map.148), calls=%async_computation | async-start | bytes 983040 | tf_op jit(solution)/shard_map/all_to_all | solution.py:436
  10.6 1.9 %shard_map.149 = (bf16[180,128]{1,0:T(8,128)(2,1)S(1)}, bf16[180,128]{1,0:T(8,128)(2,1)S(1)}) custom-call(s32[1,2]{1,0:T(1,128)S(1)} %add_bitcast_fusion.spot_ref.band_ref, s32[4,2]{1,0:T(4,128)S(1)} %copy.16.support_ref, bf16[45,4,720]{2,1,0:T(4,128)(2,1)} %bitcast.27), custom_call_target="tpu_custom_call" | custom-call | bytes 1048576 | tf_op jit(solution)/shard_map/pallas_call | solution.py:439
  12.5 2.6 %shard_map.150 = (bf16[2,384,768]{2,1,0:T(8,128)(2,1)S(1)}, bf16[2,512,384]{2,1,0:T(8,128)(2,1)S(1)}) custom-call(f32[2,8,384]{2,1,0:T(8,128)} %constant.30.clone.refs_0_, f32[2,8,384]{2,1,0:T(8,128)} %constant.31.clone.refs_1_, f32[2,96,384]{2,1,0:T(8,128)} %constant.32.clone.refs_2_, f32[2,96,384]{2,1,0:T(8,128)} %constant.33.clone.refs_3_, ...), custom_call_target="tpu_custom_call" | custom-call | bytes 5242880 | tf_op jit(solution)/shard_map/pallas_call | solution.py:449
  15.2 5.1 %all-to-all-done.r_ref = bf16[16,120,128]{2,1,0:T(8,128)(2,1)S(1)} async-done(((bf16[16,120,128]{2,1,0:T(8,128)(2,1)}), bf16[16,120,128]{2,1,0:T(8,128)(2,1)S(1)}, u32[]{:S(2)}, u32[]{:S(2)}) %all-to-all-start) | async-done | bytes 491552 | tf_op jit(solution)/shard_map/all_to_all | solution.py:436
  20.2 1.5 %shard_map.151 = bf16[32,40,128]{2,1,0:T(8,128)(2,1)} custom-call(bf16[16,120,128]{2,1,0:T(8,128)(2,1)S(1)} %all-to-all-done.r_ref, bf16[2,384,768]{2,1,0:T(8,128)(2,1)S(1)} %get-tuple-element.56.wt_ref, bf16[2,512,384]{2,1,0:T(8,128)(2,1)S(1)} %get-tuple-element.57.vt_ref), custom_call_target="tpu_custom_call" | custom-call | flops 314572800 | bytes 1048576 | tf_op jit(solution)/shard_map/pallas_call | solution.py:458
  21.7 5.0 %all-to-all-start.1 = ((bf16[32,40,128]{2,1,0:T(8,128)(2,1)}), bf16[32,40,128]{2,1,0:T(8,128)(2,1)S(1)}, u32[]{:S(2)}, u32[]{:S(2)}) async-start(bf16[32,40,128]{2,1,0:T(8,128)(2,1)} %shard_map.151), calls=%async_computation.1 | async-start | bytes 655360 | tf_op jit(solution)/shard_map/all_to_all | solution.py:459
  26.7 1.8 %shard_map.152 = (f32[144,384]{1,0:T(8,128)S(1)}, bf16[9,256,256]{2,1,0:T(8,128)(2,1)S(1)}) custom-call(s32[1,2]{1,0:T(1,128)S(1)} %add_bitcast_fusion.spot_ref.band_ref, bf16[180,128]{1,0:T(8,128)(2,1)S(1)} %get-tuple-element.60.mine_ref, bf16[180,128]{1,0:T(8,128)(2,1)S(1)} %collective-permute-done.got_ref, bf16[9,256,256]{2,1,0:T(8,128)(2,1)} %w_hbm.1), custom_call_target="tpu_custom_call" | custom-call | bytes 1048576 | tf_op jit(solution)/shard_map/pallas_call | solution.py:461
  28.5 6.8 %all-to-all-done.1 = bf16[32,40,128]{2,1,0:T(8,128)(2,1)S(1)} async-done(((bf16[32,40,128]{2,1,0:T(8,128)(2,1)}), bf16[32,40,128]{2,1,0:T(8,128)(2,1)S(1)}, u32[]{:S(2)}, u32[]{:S(2)}) %all-to-all-start.1) | async-done | bytes 327712 | tf_op jit(solution)/shard_map/all_to_all | solution.py:459
  35.3 4.3 %shard_map.153 = (bf16[16,184,128]{2,1,0:T(8,128)(2,1)S(1)}, bf16[16,184,128]{2,1,0:T(8,128)(2,1)S(1)}) custom-call(s32[1,2]{1,0:T(1,128)S(1)} %add_bitcast_fusion.spot_ref.band_ref, bf16[16,2,40,128]{3,2,1,0:T(8,128)(2,1)S(1)} %bitcast.25, f32[144,384]{1,0:T(8,128)S(1)} %get-tuple-element.62.p_ref, bf16[9,256,256]{2,1,0:T(8,128)(2,1)S(1)} %get-tuple-element.63.w_ref), custom_call_target="tpu_custom_call" | custom-call | flops 2147483648 | bytes 3145728 | tf_op jit(solution)/shard_map/pallas_call | solution.py:466
  39.7 2.2 %shard_map.154 = (bf16[2,768,384]{2,1,0:T(8,128)(2,1)S(1)}, bf16[2,384,512]{2,1,0:T(8,128)(2,1)}) custom-call(f32[2,8,384]{2,1,0:T(8,128)} %constant.30.clone.refs_0_, f32[2,8,384]{2,1,0:T(8,128)} %constant.31.clone.refs_1_, f32[2,96,384]{2,1,0:T(8,128)} %constant.32.clone.refs_2_, f32[2,96,384]{2,1,0:T(8,128)} %constant.33.clone.refs_3_, ...), custom_call_target="tpu_custom_call" | custom-call | bytes 5242880 | tf_op jit(solution)/shard_map/pallas_call | solution.py:482
  41.9 0.8 shard_map.155
  42.7 19.4 %all_to_all.20.r_ref = bf16[16,224,128]{2,1,0:T(8,128)(2,1)S(1)} all-to-all(bf16[16,224,128]{2,1,0:T(8,128)(2,1)S(1)} %shard_map.155), channel_id=1, replica_groups=mesh['ens'=8,'polar'=2,'azimuth'=16] {'azimuth'}, dimensions={0} | all-to-all | bytes 1835008 | tf_op jit(solution)/shard_map/all_to_all | solution.py:492
  62.2 2.0 %collective-permute-start.2 = (bf16[144,128]{1,0:T(8,128)(2,1)S(1)}, bf16[144,128]{1,0:T(8,128)(2,1)S(1)}, u32[]{:S(2)}, u32[]{:S(2)}) collective-permute-start(bf16[144,128]{1,0:T(8,128)(2,1)S(1)} %slice_reduce_fusion), channel_id=1, source_target_pairs={{0,32},{32,0},{64,96},{96,64},{128,160},{160,128},{192,224},{224,1... | collective-permute-start | bytes 110600 | tf_op jit(solution)/shard_map/ppermute | solution.py:499
  64.2 2.0 %collective-permute-done.2 = bf16[144,128]{1,0:T(8,128)(2,1)S(1)} collective-permute-done((bf16[144,128]{1,0:T(8,128)(2,1)S(1)}, bf16[144,128]{1,0:T(8,128)(2,1)S(1)}, u32[]{:S(2)}, u32[]{:S(2)}) %collective-permute-start.2) | collective-permute-done | bytes 36896 | tf_op jit(solution)/shard_map/ppermute | solution.py:499
  66.2 5.9 %collective-permute-start.3 = (bf16[144,128]{1,0:T(8,128)(2,1)S(1)}, bf16[144,128]{1,0:T(8,128)(2,1)S(1)}, u32[]{:S(2)}, u32[]{:S(2)}) collective-permute-start(bf16[144,128]{1,0:T(8,128)(2,1)S(1)} %add_convert_fusion), channel_id=1, source_target_pairs={{0,224},{32,64},{64,32},{96,128},{128,96},{160,192},{192,160},{224... | collective-permute-start | bytes 110600 | tf_op jit(solution)/shard_map/ppermute | solution.py:499
  72.2 1.9 %collective-permute-done.3 = bf16[144,128]{1,0:T(8,128)(2,1)S(1)} collective-permute-done((bf16[144,128]{1,0:T(8,128)(2,1)S(1)}, bf16[144,128]{1,0:T(8,128)(2,1)S(1)}, u32[]{:S(2)}, u32[]{:S(2)}) %collective-permute-start.3) | collective-permute-done | bytes 36896 | tf_op jit(solution)/shard_map/ppermute | solution.py:499
  74.1 2.6 %collective-permute-start.4 = (bf16[144,128]{1,0:T(8,128)(2,1)S(1)}, bf16[144,128]{1,0:T(8,128)(2,1)S(1)}, u32[]{:S(2)}, u32[]{:S(2)}) collective-permute-start(bf16[144,128]{1,0:T(8,128)(2,1)S(1)} %collective-permute-done.3), channel_id=1, source_target_pairs={{0,64},{32,224},{64,128},{96,32},{128,192},{160,96},{192,0},{224,1... | collective-permute-start | bytes 110600 | tf_op jit(solution)/shard_map/ppermute | solution.py:499
  76.7 2.7 %shard_map.156 = bf16[16,120,128]{2,1,0:T(8,128)(2,1)} custom-call(bf16[16,224,128]{2,1,0:T(8,128)(2,1)S(1)} %all_to_all.20.r_ref, bf16[2,768,384]{2,1,0:T(8,128)(2,1)S(1)} %get-tuple-element.79.w_ref, bf16[2,384,512]{2,1,0:T(8,128)(2,1)} %get-tuple-element.80.v_hbm), custom_call_target="tpu_custom_call" | custom-call | flops 314572800 | bytes 1048576 | tf_op jit(solution)/shard_map/pallas_call | solution.py:509
  79.4 4.8 %all-to-all-start.3 = ((bf16[16,120,128]{2,1,0:T(8,128)(2,1)}), bf16[16,120,128]{2,1,0:T(8,128)(2,1)S(1)}, u32[]{:S(2)}, u32[]{:S(2)}) async-start(bf16[16,120,128]{2,1,0:T(8,128)(2,1)} %shard_map.156), calls=%async_computation.3 | async-start | bytes 983040 | tf_op jit(solution)/shard_map/all_to_all | solution.py:516
  84.4 1.2 %collective-permute-done.6 = f32[144,128]{1,0:T(8,128)S(1)} collective-permute-done((f32[144,128]{1,0:T(8,128)S(1)}, f32[144,128]{1,0:T(8,128)S(1)}, u32[]{:S(2)}, u32[]{:S(2)}) %collective-permute-start.6) | collective-permute-done | bytes 73760 | tf_op jit(solution)/shard_map/ppermute | solution.py:414
  85.7 0.7 pad_maximum_fusion
  86.3 6.6 %all-to-all-done.3.r_ref = bf16[16,120,128]{2,1,0:T(8,128)(2,1)S(1)} async-done(((bf16[16,120,128]{2,1,0:T(8,128)(2,1)}), bf16[16,120,128]{2,1,0:T(8,128)(2,1)S(1)}, u32[]{:S(2)}, u32[]{:S(2)}) %all-to-all-start.3) | async-done | bytes 491552 | tf_op jit(solution)/shard_map/all_to_all | solution.py:516
  92.9 1.1 %shard_map.157 = (bf16[720,256]{1,0:T(8,128)(2,1)}, bf16[45,4,256]{2,1,0:T(4,128)(2,1)}) custom-call(bf16[16,120,128]{2,1,0:T(8,128)(2,1)S(1)} %all-to-all-done.3.r_ref), custom_call_target="tpu_custom_call" | custom-call | bytes 1048576 | tf_op jit(solution)/shard_map/pallas_call | solution.py:517
  (16 shorter events, 0.6 us)
Async XLA Ops:
  0.6 9.8 %copy-start = (s32[4,2]{0,1:T(2,128)S(1)}, s32[4,2]{0,1:T(2,128)}, u32[]{:S(2)}) copy-start(s32[4,2]{0,1:T(2,128)} %param.15) | copy-start | bytes 100
  2.9 17.3 %all-to-all-start = ((bf16[16,120,128]{2,1,0:T(8,128)(2,1)}), bf16[16,120,128]{2,1,0:T(8,128)(2,1)S(1)}, u32[]{:S(2)}, u32[]{:S(2)}) async-start(bf16[16,120,128]{2,1,0:T(8,128)(2,1)} %shard_map.148), calls=%async_computation | async-start | bytes 983040 | tf_op jit(solution)/shard_map/all_to_all | solution.py:436
  12.4 2.7 %collective-permute-start = (bf16[180,128]{1,0:T(8,128)(2,1)S(1)}, bf16[180,128]{1,0:T(8,128)(2,1)S(1)}, u32[]{:S(2)}, u32[]{:S(2)}) collective-permute-start(bf16[180,128]{1,0:T(8,128)(2,1)S(1)} %get-tuple-element.54), channel_id=1, source_target_pairs={{0,16},{16,0},{1,17},{17,1},{2,18},{18,2},{3,19},{19,3},{4,20},{20... | collective-permute-start | bytes 138248 | tf_op jit(solution)/shard_map/ppermute | solution.py:414
  21.7 13.6 %all-to-all-start.1 = ((bf16[32,40,128]{2,1,0:T(8,128)(2,1)}), bf16[32,40,128]{2,1,0:T(8,128)(2,1)S(1)}, u32[]{:S(2)}, u32[]{:S(2)}) async-start(bf16[32,40,128]{2,1,0:T(8,128)(2,1)} %shard_map.151), calls=%async_computation.1 | async-start | bytes 655360 | tf_op jit(solution)/shard_map/all_to_all | solution.py:459
  39.6 2.3 %collective-permute-start.1 = (bf16[16,184,128]{2,1,0:T(8,128)(2,1)S(1)}, bf16[16,184,128]{2,1,0:T(8,128)(2,1)S(1)}, u32[]{:S(2)}, u32[]{:S(2)}) collective-permute-start(bf16[16,184,128]{2,1,0:T(8,128)(2,1)S(1)} %get-tuple-element.67), channel_id=1, source_target_pairs={{0,16},{16,0},{1,17},{17,1},{2,18},{18,2},{3,19},{19,3},{4,20},{20... | collective-permute-start | bytes 2261000 | tf_op jit(solution)/shard_map/ppermute | solution.py:414
  62.2 4.0 %collective-permute-start.2 = (bf16[144,128]{1,0:T(8,128)(2,1)S(1)}, bf16[144,128]{1,0:T(8,128)(2,1)S(1)}, u32[]{:S(2)}, u32[]{:S(2)}) collective-permute-start(bf16[144,128]{1,0:T(8,128)(2,1)S(1)} %slice_reduce_fusion), channel_id=1, source_target_pairs={{0,32},{32,0},{64,96},{96,64},{128,160},{160,128},{192,224},{224,1... | collective-permute-start | bytes 110600 | tf_op jit(solution)/shard_map/ppermute | solution.py:499
  66.2 7.9 %collective-permute-start.3 = (bf16[144,128]{1,0:T(8,128)(2,1)S(1)}, bf16[144,128]{1,0:T(8,128)(2,1)S(1)}, u32[]{:S(2)}, u32[]{:S(2)}) collective-permute-start(bf16[144,128]{1,0:T(8,128)(2,1)S(1)} %add_convert_fusion), channel_id=1, source_target_pairs={{0,224},{32,64},{64,32},{96,128},{128,96},{160,192},{192,160},{224... | collective-permute-start | bytes 110600 | tf_op jit(solution)/shard_map/ppermute | solution.py:499
  74.1 10.1 %collective-permute-start.5 = (bf16[144,128]{1,0:T(8,128)(2,1)S(1)}, bf16[144,128]{1,0:T(8,128)(2,1)S(1)}, u32[]{:S(2)}, u32[]{:S(2)}) collective-permute-start(bf16[144,128]{1,0:T(8,128)(2,1)S(1)} %collective-permute-done.3), channel_id=1, source_target_pairs={{0,32},{32,0},{64,96},{96,64},{128,160},{160,128},{192,224},{224,1... | collective-permute-start | bytes 110600 | tf_op jit(solution)/shard_map/ppermute | solution.py:499
  74.1 10.1 %collective-permute-start.4 = (bf16[144,128]{1,0:T(8,128)(2,1)S(1)}, bf16[144,128]{1,0:T(8,128)(2,1)S(1)}, u32[]{:S(2)}, u32[]{:S(2)}) collective-permute-start(bf16[144,128]{1,0:T(8,128)(2,1)S(1)} %collective-permute-done.3), channel_id=1, source_target_pairs={{0,64},{32,224},{64,128},{96,32},{128,192},{160,96},{192,0},{224,1... | collective-permute-start | bytes 110600 | tf_op jit(solution)/shard_map/ppermute | solution.py:499
  79.4 13.5 %all-to-all-start.3 = ((bf16[16,120,128]{2,1,0:T(8,128)(2,1)}), bf16[16,120,128]{2,1,0:T(8,128)(2,1)S(1)}, u32[]{:S(2)}, u32[]{:S(2)}) async-start(bf16[16,120,128]{2,1,0:T(8,128)(2,1)} %shard_map.156), calls=%async_computation.3 | async-start | bytes 983040 | tf_op jit(solution)/shard_map/all_to_all | solution.py:516
  84.3 1.4 %collective-permute-start.6 = (f32[144,128]{1,0:T(8,128)S(1)}, f32[144,128]{1,0:T(8,128)S(1)}, u32[]{:S(2)}, u32[]{:S(2)}) collective-permute-start(f32[144,128]{1,0:T(8,128)S(1)} %add_add_fusion), channel_id=1, source_target_pairs={{0,16},{16,0},{1,17},{17,1},{2,18},{18,2},{3,19},{19,3},{4,20},{20... | collective-permute-start | bytes 221192 | tf_op jit(solution)/shard_map/ppermute | solution.py:414
